TPU v7x, 256 devices: a whole 4x4x8 slice. The times are simulated.
256 devices in a mesh: row: 4 (over x_lo, core), col: 16 (over z, x_hi), layer: 4 (over y).
Axes of the slice: x: 4 (x_hi: 2, x_lo: 2; x = x_hi * 2 + x_lo), y: 4, z: 8, core: 2. Of those that a mesh axis runs over, the one named last changes fastest.
Arguments:
- values: bfloat16 [8192, 8192], P('row', 'col'), may hold values from 0.0099487305 to 1
- tile_mask: int32 [64, 64], P('row', 'col'), may hold values from 0 to 1, as said below
Outputs:
- clustered: float32 [8192, 8192], P('row', ('col', 'layer'))
Inputs may be any that keep to these rules, and one draw needn't show every extreme that they name: `tile_mask`: every diagonal tile is nonzero. The blocks of (64 / 4) x 4 tiles that one device holds each have at most 32 nonzero tiles and at least 4; the block in the first grid row and first grid column has exactly 32.
All inputs are finite; a program needn't handle non-finite values.
Results may differ from a plain program's by a relative error of at most 0.0065.
Values may be sent and summed in bfloat16 or wider, within the bound.
No kernel may reach another device: no remote copies, remote signals or barrier semaphores. Data moves between devices by JAX's collectives and lax.ppermute only.
A program may use at most 128 MiB of HBM per device.

v0:
```python
import functools

import jax
import jax.numpy as jnp
from jax import lax
from jax.experimental import pallas as pl
from jax.experimental.pallas import tpu as pltpu
from jax.sharding import PartitionSpec as P


T = 128
HEAD = 16
SCALE = 16.0
VMEM = pl.BlockSpec(memory_space=pltpu.VMEM)
ANY = pl.BlockSpec(memory_space=pl.ANY)


def share_kernel(halves, per, depth_tiles, mask_hbm, values_hbm, part_ref, mask_ref, table_ref, sem):
    tiles_r, tiles_c = mask_ref.shape
    layer, col = lax.axis_index("layer"), lax.axis_index("col")
    z = lax.div(col, 2)
    section = ((lax.div(z, 4) ^ (z & 1)) * 2) + (col & 1)
    dead = tiles_r * tiles_c
    count = halves * per
    size = HEAD + per * T
    copy = pltpu.make_async_copy(mask_hbm, mask_ref, sem)
    copy.start()
    copy.wait()
    for s in range(count):
        table_ref[s] = dead
    n = -layer * count
    for i in range(tiles_r):
        for c in range(tiles_c):
            live = mask_ref[i, c] != 0
            spot = jnp.where(live & (n >= 0) & (n < count), n, count)
            table_ref[spot] = i * tiles_c + c
            n = n + live.astype(jnp.int32)
    starts = [(s // per) * size + HEAD + (s % per) * T for s in range(count)]

    def fetch(s):
        t = table_ref[s]
        i, c = lax.div(t, tiles_c), lax.rem(t, tiles_c)
        return pltpu.make_async_copy(
            values_hbm.at[pl.ds(pl.multiple_of(i * T, T), T), pl.ds(pl.multiple_of(c * T, T), T)],
            part_ref.at[starts[s]:starts[s] + T, :],
            sem,
        )

    for s in range(count):
        @pl.when(table_ref[s] < dead)
        def _():
            fetch(s).start()

        @pl.when(table_ref[s] >= dead)
        def _():
            part_ref[starts[s]:starts[s] + T, :] = jnp.zeros((T, T), jnp.bfloat16)

    row = lax.broadcasted_iota(jnp.int32, (HEAD, T), 0)
    for h in range(halves):
        head = jnp.full((HEAD, T), tiles_r * depth_tiles, jnp.int32)
        for j in range(per):
            t = table_ref[h * per + j]
            at = lax.div(t, tiles_c) * depth_tiles + section * tiles_c + lax.rem(t, tiles_c)
            head = jnp.where((row == j) & (t < dead), at, head)
        part_ref[h * size:h * size + HEAD, :] = head.astype(jnp.float32).astype(jnp.bfloat16)
    for s in range(count):
        @pl.when(table_ref[s] < dead)
        def _():
            fetch(s).wait()


def share(mask, values, per, halves, depth_tiles):
    return pl.pallas_call(
        functools.partial(share_kernel, halves, per, depth_tiles),
        out_shape=jax.ShapeDtypeStruct((halves * (HEAD + per * T), T), jnp.bfloat16),
        in_specs=[ANY, ANY],
        out_specs=VMEM,
        scratch_shapes=[
            pltpu.SMEM(mask.shape, jnp.int32),
            pltpu.SMEM((halves * per + 1,), jnp.int32),
            pltpu.SemaphoreType.DMA,
        ],
        cost_estimate=pl.CostEstimate(flops=2**20, bytes_accessed=2 * 2**20, transcendentals=0),
        name="share",
    )(mask, values)


def mask_kernel(mask_hbm, values_ref, out_ref, sums_ref, mask_ref, sem):
    tiles_r, tiles_c = mask_ref.shape
    copy = pltpu.make_async_copy(mask_hbm, mask_ref, sem)
    copy.start()
    copy.wait()
    x_lo = lax.div(lax.axis_index("row"), 2)
    sums = [jnp.zeros((8, T), jnp.float32)] * tiles_c
    for i in range(tiles_r):
        half = (i // (tiles_r // 2)) ^ x_lo
        at = i % (tiles_r // 2) * T
        for c in range(tiles_c):
            tile = values_ref[i * T:(i + 1) * T, c * T:(c + 1) * T]
            tile = jnp.where(mask_ref[i, c] != 0, tile, jnp.zeros_like(tile))
            out_ref[half, at:at + T, c * T:(c + 1) * T] = tile
            sums[c] = sums[c] + jnp.sum(tile.astype(jnp.float32).reshape(T // 8, 8, T), axis=0)
    for c in range(tiles_c):
        sums_ref[c:c + 1, :] = jnp.sum(sums[c], axis=0, keepdims=True)


def mask_block(mask, values):
    height, width = values.shape
    return pl.pallas_call(
        mask_kernel,
        out_shape=(
            jax.ShapeDtypeStruct((2, height // 2, width), jnp.bfloat16),
            jax.ShapeDtypeStruct((mask.shape[1], T), jnp.float32),
        ),
        in_specs=[ANY, VMEM],
        out_specs=(VMEM, VMEM),
        scratch_shapes=[pltpu.SMEM(mask.shape, jnp.int32), pltpu.SemaphoreType.DMA],
        cost_estimate=pl.CostEstimate(flops=2**20, bytes_accessed=4 * 2**20, transcendentals=0),
        name="mask_block",
    )(mask, values)


def scale_kernel(halves, per, raw_ref, *refs):
    mass_refs, part_ref = refs[:-1], refs[-1]
    size = HEAD + per * T
    sums = mass_refs[0][...]
    for ref in mass_refs[1:]:
        sums = sums + ref[...]
    tiles_c = sums.shape[0]
    for h in range(halves):
        head = raw_ref[h * size:h * size + HEAD, :]
        part_ref[h * size:h * size + HEAD, :] = head
        which = lax.rem(head.astype(jnp.float32).astype(jnp.int32), tiles_c)
        for j in range(per):
            mine = which[j:j + 1, :]
            mass = sums[0:1, :]
            for c in range(1, tiles_c):
                mass = jnp.where(mine == c, sums[c:c + 1, :], mass)
            at = slice(h * size + HEAD + j * T, h * size + HEAD + (j + 1) * T)
            part_ref[at, :] = (raw_ref[at, :].astype(jnp.float32) / mass).astype(jnp.bfloat16)


def scale(raw, masses, per, halves):
    return pl.pallas_call(
        functools.partial(scale_kernel, halves, per),
        out_shape=jax.ShapeDtypeStruct(raw.shape, raw.dtype),
        in_specs=[VMEM] * (1 + len(masses)),
        out_specs=VMEM,
        cost_estimate=pl.CostEstimate(flops=2**20, bytes_accessed=2**20, transcendentals=0),
        name="scale",
    )(raw, *masses)


def product_kernel(n_parts, counts, per, *refs):
    part_refs = refs[:n_parts]
    right_refs = refs[n_parts:2 + n_parts]
    out_ref = refs[2 + n_parts]
    left, spots, table, sem = refs[3 + n_parts:]
    layer = lax.axis_index("layer")
    rows, depth = left.shape
    rows = rows - T
    n_layer = out_ref.shape[0]
    kt = depth // T
    size = HEAD + per * T

    lane = lax.broadcasted_iota(jnp.int32, (8, T), 1)
    found = jnp.zeros((8, T), jnp.int32)
    q = 0
    for ref, count in zip(part_refs, counts, strict=True):
        for h in range(count):
            head = ref[h * size:h * size + HEAD, :].astype(jnp.float32).astype(jnp.int32)
            found = jnp.where(lane == q, head[:8, :], found)
            q += 1
    spots[...] = found

    def zero_left(i, _):
        left[pl.ds(pl.multiple_of(i * 64, 64), 64), :] = jnp.zeros((64, depth), jnp.bfloat16)
        return 0

    lax.fori_loop(0, rows // 64, zero_left, 0)
    copy = pltpu.make_async_copy(spots, table, sem)
    copy.start()
    copy.wait()
    q = 0
    for ref, count in zip(part_refs, counts, strict=True):
        for h in range(count):
            for j in range(per):
                t = table[j, q]
                i, k = lax.div(t, kt), lax.rem(t, kt)
                left[pl.ds(pl.multiple_of(i * T, T), T), pl.ds(pl.multiple_of(k * T, T), T)] = (
                    ref[h * size + HEAD + j * T:h * size + HEAD + (j + 1) * T, :]
                )
            q += 1
    block = 256
    mid = depth // 2

    def multiply(m, _):
        at = pl.ds(pl.multiple_of(m * block, block), block)
        out = jnp.dot(left[at, :mid], right_refs[0][...], preferred_element_type=jnp.float32)
        out = out + jnp.dot(left[at, mid:], right_refs[1][...], preferred_element_type=jnp.float32)
        for j in range(n_layer):
            out_ref[lax.rem(j + n_layer - layer, n_layer), at, :] = SCALE * out[:, j * T:(j + 1) * T]
        return 0

    lax.fori_loop(0, rows // block, multiply, 0)


def product(parts, counts, per, rights, rows, depth, n_layer):
    n_parts = len(parts)
    width = rights[0].shape[1]
    return pl.pallas_call(
        functools.partial(product_kernel, n_parts, counts, per),
        out_shape=jax.ShapeDtypeStruct((n_layer, rows, width // n_layer), jnp.float32),
        in_specs=[VMEM] * (n_parts + 2),
        out_specs=VMEM,
        scratch_shapes=[
            pltpu.VMEM((rows + T, depth), jnp.bfloat16),
            pltpu.VMEM((8, T), jnp.int32),
            pltpu.SMEM((8, T), jnp.int32),
            pltpu.SemaphoreType.DMA,
        ],
        cost_estimate=pl.CostEstimate(flops=2 * rows * depth * width, bytes_accessed=8 * 2**20, transcendentals=0),
        compiler_params=pltpu.CompilerParams(vmem_limit_bytes=48 * 2**20),
        name="product",
    )(*parts, *rights)


def coords(sizes):
    n_row, n_col, n_layer = sizes
    for r in range(n_row):
        for c in range(n_col):
            for y in range(n_layer):
                yield r, c, y


def flat(r, c, y, sizes):
    return (r * sizes[1] + c) * sizes[2] + y


def named(array, axes, perm):
    return lax.ppermute(array, axes, perm)


def shards(sizes, values, tile_mask):
    n_row, n_col, n_layer = sizes
    axes = ("row", "col", "layer")
    height, _ = values.shape
    slots = tile_mask.size // 2
    halves = 2
    per = slots // n_layer // halves
    half = HEAD + per * T
    n_z = n_col // 2
    depth = height * n_row // n_layer
    f16, f32 = jnp.float16, jnp.float32

    raw = share(tile_mask, values, per, halves, depth // T)

    spread = {}
    for r, c, y in coords(sizes):
        zz, hi = c // 2, c % 2
        y_to = zz % n_layer
        move = {0: 2 - 4 * hi, 1: 1, 2: 0, 3: -1}[(y - y_to) % n_layer]
        spread[r, c, y] = flat(r // 2 * 2 + hi, (zz + move) % n_z * 2 + r % 2, y_to, sizes)
    raw = named(raw, axes, [(flat(*at, sizes), to) for at, to in spread.items()])
    masked, sums = mask_block(tile_mask, values)
    masses = [
        named(sums, axes, [(flat(r, c, y, sizes), spread[r ^ k, c, y]) for r, c, y in coords(sizes)])
        for k in range(n_row)
    ]
    part = scale(raw, masses, per, halves)

    def ring(step):
        return [(c, (c // 2 + step) % n_z * 2 + c % 2) for c in range(n_col)]

    chains = {(k, d): part[k * half:(k + 1) * half] for k in range(halves) for d in (1, -1)}
    mine = [chains[k, 1] for k in range(halves)]
    for step in range(1, n_z // 2 + 1):
        for (k, d) in list(chains):
            if step == n_z // 2 and (k == 0) != (d == 1):
                continue
            chains[k, d] = named(chains[k, d], "col", ring(d))
            mine.append(chains[k, d])
    swap = [(r, r ^ 1) for r in range(n_row)]
    parts = mine + [named(p, "row", swap) for p in mine]

    n_x = n_row // 2 * 2
    rights = []
    for m in range(2):
        perm = []
        for r, c, y in coords(sizes):
            lo, core, zz, hi = r // 2, r % 2, c // 2, c % 2
            y_to = core * 2 + (m ^ lo)
            x_to = (hi * 2 + lo + 2 - (y - y_to)) % n_x
            lo_to, hi_to = x_to % 2, x_to // 2
            to = (lo_to * 2 + (hi ^ hi_to ^ lo_to ^ 1), zz * 2 + hi_to, y_to)
            perm.append((flat(r, c, y, sizes), flat(*to, sizes)))
        rights.append(named(masked[m], axes, perm))
    out = product(parts, [1] * len(parts), per, rights, height, depth, n_layer)

    up = [(y, (y + 1) % n_layer) for y in range(n_layer)]
    down = [(y, (y - 1) % n_layer) for y in range(n_layer)]
    mid = height // 2
    send = lax.optimization_barrier(out[1:].astype(f16))
    far_a = named(send[1, :mid], "layer", up)
    far_b = named(send[1, mid:], "layer", down)
    up_b = named(send[0, mid:], "layer", up)
    down_a = named(send[2, :mid], "layer", down)
    up_a = named((out[1, :mid] + far_a.astype(f32)).astype(f16), "layer", up)
    down_b = named((out[3, mid:] + far_b.astype(f32)).astype(f16), "layer", down)
    total = jnp.concatenate([
        out[0, :mid] + (up_a.astype(f32) + down_a.astype(f32)),
        out[0, mid:] + (up_b.astype(f32) + down_b.astype(f32)),
    ]).astype(f16)

    owner = {}
    for r in range(n_row):
        for c in range(n_col):
            lo, core, hi = r // 2, r % 2, c % 2
            owner[r, c] = (lo * 2 + hi, c // 2 * 2 + (core ^ hi ^ lo ^ 1))
    expanded = named(
        total, ("row", "col"), [(r * n_col + c, o[0] * n_col + o[1]) for (r, c), o in owner.items()])
    summand = total.astype(f32)
    summand = jnp.sum(summand * summand, axis=0)
    weight = 0.0
    for k in range(n_row):
        perm = [(r * n_col + c, (o[0] ^ k) * n_col + o[1]) for (r, c), o in owner.items()]
        weight = weight + named(summand, ("row", "col"), perm)
    expanded = expanded.astype(f32)
    inflated = expanded * expanded
    order = height * n_row
    return order * 1.0 * inflated / weight[None, :]


def solution(mesh):
    sizes = tuple(mesh.shape[a] for a in ("row", "col", "layer"))

    def body(values, tile_mask):
        return shards(sizes, values, tile_mask)

    return jax.shard_map(
        body,
        mesh=mesh,
        in_specs=(P("row", "col"), P("row", "col")),
        out_specs=P("row", ("col", "layer")),
        check_vma=False,
    )
```

profile of v0, /device:TPU:1, one launch (start us, length us, event | category | flops | bytes accessed | tf_op | source)
XLA Modules:
  0.0 147.1 jit_solution(16760688177903439168)
XLA Ops:
  0.0 1.3 copy.3.mask_hbm
  1.3 2.6 %share.1 = bf16[1056,128]{1,0:T(8,128)(2,1)} custom-call(s32[16,4]{1,0:T(8,128)} %copy.3.mask_hbm, bf16[2048,512]{1,0:T(8,128)(2,1)} %values_ref.1), custom_call_target="tpu_custom_call" | custom-call | flops 1048576 | bytes 2097152 | tf_op jit(solution)/shard_map/share/pallas_call | solution.py:73
  4.0 6.8 %collective-permute-start = (bf16[1056,128]{1,0:T(8,128)(2,1)}, bf16[1056,128]{1,0:T(8,128)(2,1)S(1)}, u32[]{:S(2)}, u32[]{:S(2)}) collective-permute-start(bf16[1056,128]{1,0:T(8,128)(2,1)} %share.1), channel_id=1, source_target_pairs={{0,16},{1,8},{2,0},{3,56},{4,112},{5,72},{6,64},{7,120},{8,1},{9,2... | collective-permute-start | bytes 811016 | tf_op jit(solution)/shard_map/ppermute | solution.py:241
  10.8 4.3 %mask_block.1 = (bf16[2,1024,512]{2,1,0:T(8,128)(2,1)}, f32[4,128]{1,0:T(4,128)}) custom-call(s32[16,4]{1,0:T(8,128)} %copy.3.mask_hbm, bf16[2048,512]{1,0:T(8,128)(2,1)} %values_ref.1), custom_call_target="tpu_custom_call" | custom-call | flops 1048576 | bytes 4194304 | tf_op jit(solution)/shard_map/mask_block/pallas_call | solution.py:109
  15.1 1.8 %collective-permute-start.4 = (f32[4,128]{1,0:T(4,128)}, f32[4,128]{1,0:T(4,128)S(1)}, u32[]{:S(2)}, u32[]{:S(2)}) collective-permute-start(f32[4,128]{1,0:T(4,128)} %get-tuple-element.7), channel_id=1, source_target_pairs={{0,148},{1,140},{2,132},{3,188},{4,244},{5,204},{6,196},{7,252},{8... | collective-permute-start | bytes 6152 | tf_op jit(solution)/shard_map/ppermute | solution.py:241
  16.9 1.5 %collective-permute-start.3 = (f32[4,128]{1,0:T(4,128)}, f32[4,128]{1,0:T(4,128)S(1)}, u32[]{:S(2)}, u32[]{:S(2)}) collective-permute-start(f32[4,128]{1,0:T(4,128)} %get-tuple-element.7), channel_id=1, source_target_pairs={{0,144},{1,136},{2,128},{3,184},{4,240},{5,200},{6,192},{7,248},{8... | collective-permute-start | bytes 6152 | tf_op jit(solution)/shard_map/ppermute | solution.py:241
  18.4 3.6 %collective-permute-start.2 = (f32[4,128]{1,0:T(4,128)}, f32[4,128]{1,0:T(4,128)S(1)}, u32[]{:S(2)}, u32[]{:S(2)}) collective-permute-start(f32[4,128]{1,0:T(4,128)} %get-tuple-element.7), channel_id=1, source_target_pairs={{0,20},{1,12},{2,4},{3,60},{4,116},{5,76},{6,68},{7,124},{8,5},{9,... | collective-permute-start | bytes 6152 | tf_op jit(solution)/shard_map/ppermute | solution.py:241
  22.1 2.1 %collective-permute-start.1 = (f32[4,128]{1,0:T(4,128)}, f32[4,128]{1,0:T(4,128)S(1)}, u32[]{:S(2)}, u32[]{:S(2)}) collective-permute-start(f32[4,128]{1,0:T(4,128)} %get-tuple-element.7), channel_id=1, source_target_pairs={{0,16},{1,8},{2,0},{3,56},{4,112},{5,72},{6,64},{7,120},{8,1},{9,2... | collective-permute-start | bytes 6152 | tf_op jit(solution)/shard_map/ppermute | solution.py:241
  24.2 4.2 %collective-permute-done.2.refs_1_ = f32[4,128]{1,0:T(4,128)S(1)} collective-permute-done((f32[4,128]{1,0:T(4,128)}, f32[4,128]{1,0:T(4,128)S(1)}, u32[]{:S(2)}, u32[]{:S(2)}) %collective-permute-start.2) | collective-permute-done | bytes 2080 | tf_op jit(solution)/shard_map/ppermute | solution.py:241
  28.4 0.8 collective-permute-done.1.refs_0_
  30.4 1.7 %scale.1 = bf16[1056,128]{1,0:T(8,128)(2,1)} custom-call(bf16[1056,128]{1,0:T(8,128)(2,1)} %copy-done.1, f32[4,128]{1,0:T(4,128)} %copy-done.5, f32[4,128]{1,0:T(4,128)} %copy-done.4, f32[4,128]{1,0:T(4,128)} %copy-done.3, f32[4,128]{1,0:T(4,128)} %copy-done.2), custom_call_target="tpu_custom_call" | custom-call | flops 1048576 | bytes 1048576 | tf_op jit(solution)/shard_map/scale/pallas_call | solution.py:144
  32.2 1.0 fusion.8
  33.2 0.8 collective-permute-start.20
  33.9 6.2 %collective-permute-start.8 = (bf16[528,128]{1,0:T(8,128)(2,1)S(1)}, bf16[528,128]{1,0:T(8,128)(2,1)S(1)}, u32[]{:S(2)}, u32[]{:S(2)}) collective-permute-start(bf16[528,128]{1,0:T(8,128)(2,1)S(1)} %get-tuple-element.17.refs_1_), channel_id=1, source_target_pairs={{0,56},{4,60},{8,0},{12,4},{16,8},{20,12},{24,16},{28,20},{32,24},... | collective-permute-start | bytes 405512 | tf_op jit(solution)/shard_map/ppermute | solution.py:241
  40.8 3.0 %collective-permute-start.6 = (bf16[528,128]{1,0:T(8,128)(2,1)S(1)}, bf16[528,128]{1,0:T(8,128)(2,1)S(1)}, u32[]{:S(2)}, u32[]{:S(2)}) collective-permute-start(bf16[528,128]{1,0:T(8,128)(2,1)S(1)} %get-tuple-element.18.refs_0_), channel_id=1, source_target_pairs={{0,56},{4,60},{8,0},{12,4},{16,8},{20,12},{24,16},{28,20},{32,24},... | collective-permute-start | bytes 405512 | tf_op jit(solution)/shard_map/ppermute | solution.py:241
  44.2 1.6 %collective-permute-done.7.refs_4_ = bf16[528,128]{1,0:T(8,128)(2,1)S(1)} collective-permute-done((bf16[528,128]{1,0:T(8,128)(2,1)S(1)}, bf16[528,128]{1,0:T(8,128)(2,1)S(1)}, u32[]{:S(2)}, u32[]{:S(2)}) %collective-permute-start.7) | collective-permute-done | bytes 135200 | tf_op jit(solution)/shard_map/ppermute | solution.py:241
  45.8 1.6 %collective-permute-start.12 = (bf16[528,128]{1,0:T(8,128)(2,1)S(1)}, bf16[528,128]{1,0:T(8,128)(2,1)S(1)}, u32[]{:S(2)}, u32[]{:S(2)}) collective-permute-start(bf16[528,128]{1,0:T(8,128)(2,1)S(1)} %collective-permute-done.8.refs_5_), channel_id=1, source_target_pairs={{0,56},{4,60},{8,0},{12,4},{16,8},{20,12},{24,16},{28,20},{32,24},... | collective-permute-start | bytes 405512 | tf_op jit(solution)/shard_map/ppermute | solution.py:241
  47.6 1.7 %slice_bitcast_fusion = (bf16[1024,512]{1,0:T(8,128)(2,1)S(1)}, bf16[1024,512]{1,0:T(8,128)(2,1)S(1)}) fusion(bf16[2,1024,512]{2,1,0:T(8,128)(2,1)} %get-tuple-element.8), kind=kLoop, calls=%fused_computation.3 | loop fusion | bytes 4194304 | tf_op jit(solution)/shard_map/squeeze | solution.py:297
  49.9 1.3 collective-permute-start.35
  51.2 1.5 collective-permute-start.11
  52.7 3.1 %collective-permute-start.22 = (bf16[528,128]{1,0:T(8,128)(2,1)S(1)}, bf16[528,128]{1,0:T(8,128)(2,1)S(1)}, u32[]{:S(2)}, u32[]{:S(2)}) collective-permute-start(bf16[528,128]{1,0:T(8,128)(2,1)S(1)} %collective-permute-done.6.refs_3_), channel_id=1, source_target_pairs={{0,64},{64,0},{128,192},{192,128},{1,65},{65,1},{129,193},{193,129... | collective-permute-start | bytes 405512 | tf_op jit(solution)/shard_map/ppermute | solution.py:241
  55.7 2.2 %collective-permute-start.10 = (bf16[528,128]{1,0:T(8,128)(2,1)S(1)}, bf16[528,128]{1,0:T(8,128)(2,1)S(1)}, u32[]{:S(2)}, u32[]{:S(2)}) collective-permute-start(bf16[528,128]{1,0:T(8,128)(2,1)S(1)} %collective-permute-done.6.refs_3_), channel_id=1, source_target_pairs={{0,56},{4,60},{8,0},{12,4},{16,8},{20,12},{24,16},{28,20},{32,24},... | collective-permute-start | bytes 405512 | tf_op jit(solution)/shard_map/ppermute | solution.py:241
  57.9 3.3 %collective-permute-start.21 = (bf16[528,128]{1,0:T(8,128)(2,1)S(1)}, bf16[528,128]{1,0:T(8,128)(2,1)S(1)}, u32[]{:S(2)}, u32[]{:S(2)}) collective-permute-start(bf16[528,128]{1,0:T(8,128)(2,1)S(1)} %collective-permute-done.5.refs_2_), channel_id=1, source_target_pairs={{0,64},{64,0},{128,192},{192,128},{1,65},{65,1},{129,193},{193,129... | collective-permute-start | bytes 405512 | tf_op jit(solution)/shard_map/ppermute | solution.py:241
  62.2 3.0 %collective-permute-start.16 = (bf16[528,128]{1,0:T(8,128)(2,1)S(1)}, bf16[528,128]{1,0:T(8,128)(2,1)S(1)}, u32[]{:S(2)}, u32[]{:S(2)}) collective-permute-start(bf16[528,128]{1,0:T(8,128)(2,1)S(1)} %collective-permute-done.12.refs_9_), channel_id=1, source_target_pairs={{0,56},{4,60},{8,0},{12,4},{16,8},{20,12},{24,16},{28,20},{32,24},... | collective-permute-start | bytes 405512 | tf_op jit(solution)/shard_map/ppermute | solution.py:241
  65.1 2.4 %collective-permute-done.9.refs_6_ = bf16[528,128]{1,0:T(8,128)(2,1)S(1)} collective-permute-done((bf16[528,128]{1,0:T(8,128)(2,1)S(1)}, bf16[528,128]{1,0:T(8,128)(2,1)S(1)}, u32[]{:S(2)}, u32[]{:S(2)}) %collective-permute-start.9) | collective-permute-done | bytes 135200 | tf_op jit(solution)/shard_map/ppermute | solution.py:241
  67.5 0.9 collective-permute-start.27
  69.4 3.0 %collective-permute-start.14 = (bf16[528,128]{1,0:T(8,128)(2,1)S(1)}, bf16[528,128]{1,0:T(8,128)(2,1)S(1)}, u32[]{:S(2)}, u32[]{:S(2)}) collective-permute-start(bf16[528,128]{1,0:T(8,128)(2,1)S(1)} %collective-permute-done.10.refs_7_), channel_id=1, source_target_pairs={{0,56},{4,60},{8,0},{12,4},{16,8},{20,12},{24,16},{28,20},{32,24},... | collective-permute-start | bytes 405512 | tf_op jit(solution)/shard_map/ppermute | solution.py:241
  72.3 2.4 %collective-permute-done.15.refs_12_ = bf16[528,128]{1,0:T(8,128)(2,1)S(1)} collective-permute-done((bf16[528,128]{1,0:T(8,128)(2,1)S(1)}, bf16[528,128]{1,0:T(8,128)(2,1)S(1)}, u32[]{:S(2)}, u32[]{:S(2)}) %collective-permute-start.15) | collective-permute-done | bytes 135200 | tf_op jit(solution)/shard_map/ppermute | solution.py:241
  74.7 0.9 collective-permute-start.25
  76.6 3.0 %collective-permute-start.18 = (bf16[528,128]{1,0:T(8,128)(2,1)S(1)}, bf16[528,128]{1,0:T(8,128)(2,1)S(1)}, u32[]{:S(2)}, u32[]{:S(2)}) collective-permute-start(bf16[528,128]{1,0:T(8,128)(2,1)S(1)} %collective-permute-done.16.refs_13_), channel_id=1, source_target_pairs={{0,56},{4,60},{8,0},{12,4},{16,8},{20,12},{24,16},{28,20},{32,24},... | collective-permute-start | bytes 405512 | tf_op jit(solution)/shard_map/ppermute | solution.py:241
  79.6 2.4 %collective-permute-done.13.refs_10_ = bf16[528,128]{1,0:T(8,128)(2,1)S(1)} collective-permute-done((bf16[528,128]{1,0:T(8,128)(2,1)S(1)}, bf16[528,128]{1,0:T(8,128)(2,1)S(1)}, u32[]{:S(2)}, u32[]{:S(2)}) %collective-permute-start.13) | collective-permute-done | bytes 135200 | tf_op jit(solution)/shard_map/ppermute | solution.py:241
  82.0 0.9 collective-permute-start.31
  84.4 4.6 %collective-permute-done.17.refs_14_ = bf16[528,128]{1,0:T(8,128)(2,1)S(1)} collective-permute-done((bf16[528,128]{1,0:T(8,128)(2,1)S(1)}, bf16[528,128]{1,0:T(8,128)(2,1)S(1)}, u32[]{:S(2)}, u32[]{:S(2)}) %collective-permute-start.17) | collective-permute-done | bytes 135200 | tf_op jit(solution)/shard_map/ppermute | solution.py:241
  89.0 1.4 collective-permute-start.33
  90.5 1.0 collective-permute-done.33.refs_30_
  91.5 1.0 copy-done.6
  92.4 11.6 %product.1 = f32[4,2048,128]{2,1,0:T(8,128)} custom-call(bf16[528,128]{1,0:T(8,128)(2,1)S(1)} %get-tuple-element.18.refs_0_, bf16[528,128]{1,0:T(8,128)(2,1)S(1)} %get-tuple-element.17.refs_1_, bf16[528,128]{1,0:T(8,128)(2,1)S(1)} %collective-permute-done.5.refs_2_, bf16[528,128]{1,0:T(8,128)(2,1)S(1)} %collective-permute-done.6.refs_3_, ...), custom_call_target="tpu_custom_call" | custom-call | flops 4294967296 | bytes 8388608 | tf_op jit(solution)/shard_map/product/pallas_call | solution.py:211
  104.0 2.2 %slice_convert_fusion = f16[3,2048,128]{2,1,0:T(8,128)(2,1)S(1)} fusion(f32[4,2048,128]{2,1,0:T(8,128)} %product.1), kind=kLoop, calls=%fused_computation | loop fusion | flops 786432 | bytes 4718592 | tf_op jit(solution)/shard_map/convert.2
  106.6 2.7 %collective-permute-start.41 = (f16[1024,128]{1,0:T(8,128)(2,1)S(1)}, f16[1024,128]{1,0:T(8,128)(2,1)S(1)}, u32[]{:S(2)}, u32[]{:S(2)}) collective-permute-start(f16[1024,128]{1,0:T(8,128)(2,1)S(1)} %get-tuple-element.14), channel_id=1, source_target_pairs={{0,3},{1,0},{2,1},{3,2},{4,7},{5,4},{6,5},{7,6},{8,11},{9,8},{10,9... | collective-permute-start | bytes 786440 | tf_op jit(solution)/shard_map/ppermute | solution.py:241
  109.4 5.9 %collective-permute-done.37 = f16[1024,128]{1,0:T(8,128)(2,1)S(1)} collective-permute-done((f16[1024,128]{1,0:T(8,128)(2,1)S(1)}, f16[1024,128]{1,0:T(8,128)(2,1)S(1)}, u32[]{:S(2)}, u32[]{:S(2)}) %collective-permute-start.37) | collective-permute-done | bytes 262176 | tf_op jit(solution)/shard_map/ppermute | solution.py:241
  115.6 4.3 %collective-permute-done.39 = f16[1024,128]{1,0:T(8,128)(2,1)S(1)} collective-permute-done((f16[1024,128]{1,0:T(8,128)(2,1)S(1)}, f16[1024,128]{1,0:T(8,128)(2,1)S(1)}, u32[]{:S(2)}, u32[]{:S(2)}) %collective-permute-start.39) | collective-permute-done | bytes 262176 | tf_op jit(solution)/shard_map/ppermute | solution.py:241
  119.9 3.4 %collective-permute-done.38 = f16[1024,128]{1,0:T(8,128)(2,1)S(1)} collective-permute-done((f16[1024,128]{1,0:T(8,128)(2,1)S(1)}, f16[1024,128]{1,0:T(8,128)(2,1)S(1)}, u32[]{:S(2)}, u32[]{:S(2)}) %collective-permute-start.38) | collective-permute-done | bytes 262176 | tf_op jit(solution)/shard_map/ppermute | solution.py:241
  123.6 5.3 %collective-permute-done.40 = f16[1024,128]{1,0:T(8,128)(2,1)S(1)} collective-permute-done((f16[1024,128]{1,0:T(8,128)(2,1)S(1)}, f16[1024,128]{1,0:T(8,128)(2,1)S(1)}, u32[]{:S(2)}, u32[]{:S(2)}) %collective-permute-start.40) | collective-permute-done | bytes 262176 | tf_op jit(solution)/shard_map/ppermute | solution.py:241
  129.4 6.5 %collective-permute-start.43 = (f16[2048,128]{1,0:T(8,128)(2,1)S(1)}, f16[2048,128]{1,0:T(8,128)(2,1)S(1)}, u32[]{:S(2)}, u32[]{:S(2)}) collective-permute-start(f16[2048,128]{1,0:T(8,128)(2,1)S(1)} %pad_maximum_fusion), channel_id=1, source_target_pairs={{0,4},{4,64},{8,12},{12,72},{16,20},{20,80},{24,28},{28,88},{32,36... | collective-permute-start | bytes 1572872 | tf_op jit(solution)/shard_map/ppermute | solution.py:241
  136.7 1.3 collective-permute-start.46
  138.7 6.5 %collective-permute-start.44 = (f32[128]{0:T(128)S(1)}, f32[128]{0:T(128)S(1)}, u32[]{:S(2)}, u32[]{:S(2)}) collective-permute-start(f32[128]{0:T(128)S(1)} %multiply_reduce_fusion), channel_id=1, source_target_pairs={{0,4},{4,64},{8,12},{12,72},{16,20},{20,80},{24,28},{28,88},{32,36... | collective-permute-start | bytes 1544 | tf_op jit(solution)/shard_map/ppermute | solution.py:241
  145.2 0.8 collective-permute-done.44
  146.0 1.1 multiply_divide_fusion
  (78 shorter events, 10.5 us)
Async XLA Ops:
  4.0 25.2 %collective-permute-start = (bf16[1056,128]{1,0:T(8,128)(2,1)}, bf16[1056,128]{1,0:T(8,128)(2,1)S(1)}, u32[]{:S(2)}, u32[]{:S(2)}) collective-permute-start(bf16[1056,128]{1,0:T(8,128)(2,1)} %share.1), channel_id=1, source_target_pairs={{0,16},{1,8},{2,0},{3,56},{4,112},{5,72},{6,64},{7,120},{8,1},{9,2... | collective-permute-start | bytes 811016 | tf_op jit(solution)/shard_map/ppermute | solution.py:241
  15.1 9.1 %collective-permute-start.4 = (f32[4,128]{1,0:T(4,128)}, f32[4,128]{1,0:T(4,128)S(1)}, u32[]{:S(2)}, u32[]{:S(2)}) collective-permute-start(f32[4,128]{1,0:T(4,128)} %get-tuple-element.7), channel_id=1, source_target_pairs={{0,148},{1,140},{2,132},{3,188},{4,244},{5,204},{6,196},{7,252},{8... | collective-permute-start | bytes 6152 | tf_op jit(solution)/shard_map/ppermute | solution.py:241
  16.9 7.3 %collective-permute-start.3 = (f32[4,128]{1,0:T(4,128)}, f32[4,128]{1,0:T(4,128)S(1)}, u32[]{:S(2)}, u32[]{:S(2)}) collective-permute-start(f32[4,128]{1,0:T(4,128)} %get-tuple-element.7), channel_id=1, source_target_pairs={{0,144},{1,136},{2,128},{3,184},{4,240},{5,200},{6,192},{7,248},{8... | collective-permute-start | bytes 6152 | tf_op jit(solution)/shard_map/ppermute | solution.py:241
  18.4 10.0 %collective-permute-start.2 = (f32[4,128]{1,0:T(4,128)}, f32[4,128]{1,0:T(4,128)S(1)}, u32[]{:S(2)}, u32[]{:S(2)}) collective-permute-start(f32[4,128]{1,0:T(4,128)} %get-tuple-element.7), channel_id=1, source_target_pairs={{0,20},{1,12},{2,4},{3,60},{4,116},{5,76},{6,68},{7,124},{8,5},{9,... | collective-permute-start | bytes 6152 | tf_op jit(solution)/shard_map/ppermute | solution.py:241
  22.1 7.1 %collective-permute-start.1 = (f32[4,128]{1,0:T(4,128)}, f32[4,128]{1,0:T(4,128)S(1)}, u32[]{:S(2)}, u32[]{:S(2)}) collective-permute-start(f32[4,128]{1,0:T(4,128)} %get-tuple-element.7), channel_id=1, source_target_pairs={{0,16},{1,8},{2,0},{3,56},{4,112},{5,72},{6,64},{7,120},{8,1},{9,2... | collective-permute-start | bytes 6152 | tf_op jit(solution)/shard_map/ppermute | solution.py:241
  33.2 10.6 %collective-permute-start.20 = (bf16[528,128]{1,0:T(8,128)(2,1)S(1)}, bf16[528,128]{1,0:T(8,128)(2,1)S(1)}, u32[]{:S(2)}, u32[]{:S(2)}) collective-permute-start(bf16[528,128]{1,0:T(8,128)(2,1)S(1)} %get-tuple-element.17.refs_1_), channel_id=1, source_target_pairs={{0,64},{64,0},{128,192},{192,128},{1,65},{65,1},{129,193},{193,129... | collective-permute-start | bytes 405512 | tf_op jit(solution)/shard_map/ppermute | solution.py:241
  33.9 9.9 %collective-permute-start.8 = (bf16[528,128]{1,0:T(8,128)(2,1)S(1)}, bf16[528,128]{1,0:T(8,128)(2,1)S(1)}, u32[]{:S(2)}, u32[]{:S(2)}) collective-permute-start(bf16[528,128]{1,0:T(8,128)(2,1)S(1)} %get-tuple-element.17.refs_1_), channel_id=1, source_target_pairs={{0,56},{4,60},{8,0},{12,4},{16,8},{20,12},{24,16},{28,20},{32,24},... | collective-permute-start | bytes 405512 | tf_op jit(solution)/shard_map/ppermute | solution.py:241
  40.1 5.7 %collective-permute-start.7 = (bf16[528,128]{1,0:T(8,128)(2,1)S(1)}, bf16[528,128]{1,0:T(8,128)(2,1)S(1)}, u32[]{:S(2)}, u32[]{:S(2)}) collective-permute-start(bf16[528,128]{1,0:T(8,128)(2,1)S(1)} %get-tuple-element.17.refs_1_), channel_id=1, source_target_pairs={{0,8},{4,12},{8,16},{12,20},{16,24},{20,28},{24,32},{28,36},{32,40... | collective-permute-start | bytes 405512 | tf_op jit(solution)/shard_map/ppermute | solution.py:241
  40.1 7.2 %collective-permute-start.19 = (bf16[528,128]{1,0:T(8,128)(2,1)S(1)}, bf16[528,128]{1,0:T(8,128)(2,1)S(1)}, u32[]{:S(2)}, u32[]{:S(2)}) collective-permute-start(bf16[528,128]{1,0:T(8,128)(2,1)S(1)} %get-tuple-element.18.refs_0_), channel_id=1, source_target_pairs={{0,64},{64,0},{128,192},{192,128},{1,65},{65,1},{129,193},{193,129... | collective-permute-start | bytes 405512 | tf_op jit(solution)/shard_map/ppermute | solution.py:241
  40.8 8.5 %collective-permute-start.6 = (bf16[528,128]{1,0:T(8,128)(2,1)S(1)}, bf16[528,128]{1,0:T(8,128)(2,1)S(1)}, u32[]{:S(2)}, u32[]{:S(2)}) collective-permute-start(bf16[528,128]{1,0:T(8,128)(2,1)S(1)} %get-tuple-element.18.refs_0_), channel_id=1, source_target_pairs={{0,56},{4,60},{8,0},{12,4},{16,8},{20,12},{24,16},{28,20},{32,24},... | collective-permute-start | bytes 405512 | tf_op jit(solution)/shard_map/ppermute | solution.py:241
  43.8 6.1 %collective-permute-start.5 = (bf16[528,128]{1,0:T(8,128)(2,1)S(1)}, bf16[528,128]{1,0:T(8,128)(2,1)S(1)}, u32[]{:S(2)}, u32[]{:S(2)}) collective-permute-start(bf16[528,128]{1,0:T(8,128)(2,1)S(1)} %get-tuple-element.18.refs_0_), channel_id=1, source_target_pairs={{0,8},{4,12},{8,16},{12,20},{16,24},{20,28},{24,32},{28,36},{32,40... | collective-permute-start | bytes 405512 | tf_op jit(solution)/shard_map/ppermute | solution.py:241
  43.8 7.4 %collective-permute-start.24 = (bf16[528,128]{1,0:T(8,128)(2,1)S(1)}, bf16[528,128]{1,0:T(8,128)(2,1)S(1)}, u32[]{:S(2)}, u32[]{:S(2)}) collective-permute-start(bf16[528,128]{1,0:T(8,128)(2,1)S(1)} %collective-permute-done.8.refs_5_), channel_id=1, source_target_pairs={{0,64},{64,0},{128,192},{192,128},{1,65},{65,1},{129,193},{193,129... | collective-permute-start | bytes 405512 | tf_op jit(solution)/shard_map/ppermute | solution.py:241
  45.8 6.9 %collective-permute-start.12 = (bf16[528,128]{1,0:T(8,128)(2,1)S(1)}, bf16[528,128]{1,0:T(8,128)(2,1)S(1)}, u32[]{:S(2)}, u32[]{:S(2)}) collective-permute-start(bf16[528,128]{1,0:T(8,128)(2,1)S(1)} %collective-permute-done.8.refs_5_), channel_id=1, source_target_pairs={{0,56},{4,60},{8,0},{12,4},{16,8},{20,12},{24,16},{28,20},{32,24},... | collective-permute-start | bytes 405512 | tf_op jit(solution)/shard_map/ppermute | solution.py:241
  47.4 8.4 %collective-permute-start.23 = (bf16[528,128]{1,0:T(8,128)(2,1)S(1)}, bf16[528,128]{1,0:T(8,128)(2,1)S(1)}, u32[]{:S(2)}, u32[]{:S(2)}) collective-permute-start(bf16[528,128]{1,0:T(8,128)(2,1)S(1)} %collective-permute-done.7.refs_4_), channel_id=1, source_target_pairs={{0,64},{64,0},{128,192},{192,128},{1,65},{65,1},{129,193},{193,129... | collective-permute-start | bytes 405512 | tf_op jit(solution)/shard_map/ppermute | solution.py:241
  49.3 42.1 %collective-permute-start.36 = (bf16[1024,512]{1,0:T(8,128)(2,1)S(1)}, bf16[1024,512]{1,0:T(8,128)(2,1)S(1)}, u32[]{:S(2)}, u32[]{:S(2)}) collective-permute-start(bf16[1024,512]{1,0:T(8,128)(2,1)S(1)} %get-tuple-element.11), channel_id=1, source_target_pairs={{0,197},{1,5},{2,129},{3,65},{4,193},{5,1},{6,133},{7,69},{8,205},... | collective-permute-start | bytes 3145736 | tf_op jit(solution)/shard_map/ppermute | solution.py:241
  49.9 41.6 %collective-permute-start.35 = (bf16[1024,512]{1,0:T(8,128)(2,1)S(1)}, bf16[1024,512]{1,0:T(8,128)(2,1)S(1)}, u32[]{:S(2)}, u32[]{:S(2)}) collective-permute-start(bf16[1024,512]{1,0:T(8,128)(2,1)S(1)} %get-tuple-element.12), channel_id=1, source_target_pairs={{0,4},{1,128},{2,64},{3,196},{4,0},{5,132},{6,68},{7,192},{8,12},{... | collective-permute-start | bytes 3145736 | tf_op jit(solution)/shard_map/ppermute | solution.py:241
  51.2 6.7 %collective-permute-start.11 = (bf16[528,128]{1,0:T(8,128)(2,1)S(1)}, bf16[528,128]{1,0:T(8,128)(2,1)S(1)}, u32[]{:S(2)}, u32[]{:S(2)}) collective-permute-start(bf16[528,128]{1,0:T(8,128)(2,1)S(1)} %collective-permute-done.7.refs_4_), channel_id=1, source_target_pairs={{0,8},{4,12},{8,16},{12,20},{16,24},{20,28},{24,32},{28,36},{32,40... | collective-permute-start | bytes 405512 | tf_op jit(solution)/shard_map/ppermute | solution.py:241
  52.7 8.5 %collective-permute-start.22 = (bf16[528,128]{1,0:T(8,128)(2,1)S(1)}, bf16[528,128]{1,0:T(8,128)(2,1)S(1)}, u32[]{:S(2)}, u32[]{:S(2)}) collective-permute-start(bf16[528,128]{1,0:T(8,128)(2,1)S(1)} %collective-permute-done.6.refs_3_), channel_id=1, source_target_pairs={{0,64},{64,0},{128,192},{192,128},{1,65},{65,1},{129,193},{193,129... | collective-permute-start | bytes 405512 | tf_op jit(solution)/shard_map/ppermute | solution.py:241
  55.7 5.5 %collective-permute-start.10 = (bf16[528,128]{1,0:T(8,128)(2,1)S(1)}, bf16[528,128]{1,0:T(8,128)(2,1)S(1)}, u32[]{:S(2)}, u32[]{:S(2)}) collective-permute-start(bf16[528,128]{1,0:T(8,128)(2,1)S(1)} %collective-permute-done.6.refs_3_), channel_id=1, source_target_pairs={{0,56},{4,60},{8,0},{12,4},{16,8},{20,12},{24,16},{28,20},{32,24},... | collective-permute-start | bytes 405512 | tf_op jit(solution)/shard_map/ppermute | solution.py:241
  57.9 4.2 %collective-permute-start.21 = (bf16[528,128]{1,0:T(8,128)(2,1)S(1)}, bf16[528,128]{1,0:T(8,128)(2,1)S(1)}, u32[]{:S(2)}, u32[]{:S(2)}) collective-permute-start(bf16[528,128]{1,0:T(8,128)(2,1)S(1)} %collective-permute-done.5.refs_2_), channel_id=1, source_target_pairs={{0,64},{64,0},{128,192},{192,128},{1,65},{65,1},{129,193},{193,129... | collective-permute-start | bytes 405512 | tf_op jit(solution)/shard_map/ppermute | solution.py:241
  61.2 6.3 %collective-permute-start.9 = (bf16[528,128]{1,0:T(8,128)(2,1)S(1)}, bf16[528,128]{1,0:T(8,128)(2,1)S(1)}, u32[]{:S(2)}, u32[]{:S(2)}) collective-permute-start(bf16[528,128]{1,0:T(8,128)(2,1)S(1)} %collective-permute-done.5.refs_2_), channel_id=1, source_target_pairs={{0,8},{4,12},{8,16},{12,20},{16,24},{20,28},{24,32},{28,36},{32,40... | collective-permute-start | bytes 405512 | tf_op jit(solution)/shard_map/ppermute | solution.py:241
  61.2 7.2 %collective-permute-start.28 = (bf16[528,128]{1,0:T(8,128)(2,1)S(1)}, bf16[528,128]{1,0:T(8,128)(2,1)S(1)}, u32[]{:S(2)}, u32[]{:S(2)}) collective-permute-start(bf16[528,128]{1,0:T(8,128)(2,1)S(1)} %collective-permute-done.12.refs_9_), channel_id=1, source_target_pairs={{0,64},{64,0},{128,192},{192,128},{1,65},{65,1},{129,193},{193,129... | collective-permute-start | bytes 405512 | tf_op jit(solution)/shard_map/ppermute | solution.py:241
  62.2 6.2 %collective-permute-start.16 = (bf16[528,128]{1,0:T(8,128)(2,1)S(1)}, bf16[528,128]{1,0:T(8,128)(2,1)S(1)}, u32[]{:S(2)}, u32[]{:S(2)}) collective-permute-start(bf16[528,128]{1,0:T(8,128)(2,1)S(1)} %collective-permute-done.12.refs_9_), channel_id=1, source_target_pairs={{0,56},{4,60},{8,0},{12,4},{16,8},{20,12},{24,16},{28,20},{32,24},... | collective-permute-start | bytes 405512 | tf_op jit(solution)/shard_map/ppermute | solution.py:241
  67.5 1.9 %collective-permute-start.27 = (bf16[528,128]{1,0:T(8,128)(2,1)S(1)}, bf16[528,128]{1,0:T(8,128)(2,1)S(1)}, u32[]{:S(2)}, u32[]{:S(2)}) collective-permute-start(bf16[528,128]{1,0:T(8,128)(2,1)S(1)} %collective-permute-done.11.refs_8_), channel_id=1, source_target_pairs={{0,64},{64,0},{128,192},{192,128},{1,65},{65,1},{129,193},{193,129... | collective-permute-start | bytes 405512 | tf_op jit(solution)/shard_map/ppermute | solution.py:241
  68.4 6.3 %collective-permute-start.15 = (bf16[528,128]{1,0:T(8,128)(2,1)S(1)}, bf16[528,128]{1,0:T(8,128)(2,1)S(1)}, u32[]{:S(2)}, u32[]{:S(2)}) collective-permute-start(bf16[528,128]{1,0:T(8,128)(2,1)S(1)} %collective-permute-done.11.refs_8_), channel_id=1, source_target_pairs={{0,8},{4,12},{8,16},{12,20},{16,24},{20,28},{24,32},{28,36},{32,40... | collective-permute-start | bytes 405512 | tf_op jit(solution)/shard_map/ppermute | solution.py:241
  68.4 7.2 %collective-permute-start.26 = (bf16[528,128]{1,0:T(8,128)(2,1)S(1)}, bf16[528,128]{1,0:T(8,128)(2,1)S(1)}, u32[]{:S(2)}, u32[]{:S(2)}) collective-permute-start(bf16[528,128]{1,0:T(8,128)(2,1)S(1)} %collective-permute-done.10.refs_7_), channel_id=1, source_target_pairs={{0,64},{64,0},{128,192},{192,128},{1,65},{65,1},{129,193},{193,129... | collective-permute-start | bytes 405512 | tf_op jit(solution)/shard_map/ppermute | solution.py:241
  69.4 6.2 %collective-permute-start.14 = (bf16[528,128]{1,0:T(8,128)(2,1)S(1)}, bf16[528,128]{1,0:T(8,128)(2,1)S(1)}, u32[]{:S(2)}, u32[]{:S(2)}) collective-permute-start(bf16[528,128]{1,0:T(8,128)(2,1)S(1)} %collective-permute-done.10.refs_7_), channel_id=1, source_target_pairs={{0,56},{4,60},{8,0},{12,4},{16,8},{20,12},{24,16},{28,20},{32,24},... | collective-permute-start | bytes 405512 | tf_op jit(solution)/shard_map/ppermute | solution.py:241
  74.7 1.9 %collective-permute-start.25 = (bf16[528,128]{1,0:T(8,128)(2,1)S(1)}, bf16[528,128]{1,0:T(8,128)(2,1)S(1)}, u32[]{:S(2)}, u32[]{:S(2)}) collective-permute-start(bf16[528,128]{1,0:T(8,128)(2,1)S(1)} %collective-permute-done.9.refs_6_), channel_id=1, source_target_pairs={{0,64},{64,0},{128,192},{192,128},{1,65},{65,1},{129,193},{193,129... | collective-permute-start | bytes 405512 | tf_op jit(solution)/shard_map/ppermute | solution.py:241
  75.6 6.3 %collective-permute-start.13 = (bf16[528,128]{1,0:T(8,128)(2,1)S(1)}, bf16[528,128]{1,0:T(8,128)(2,1)S(1)}, u32[]{:S(2)}, u32[]{:S(2)}) collective-permute-start(bf16[528,128]{1,0:T(8,128)(2,1)S(1)} %collective-permute-done.9.refs_6_), channel_id=1, source_target_pairs={{0,8},{4,12},{8,16},{12,20},{16,24},{20,28},{24,32},{28,36},{32,40... | collective-permute-start | bytes 405512 | tf_op jit(solution)/shard_map/ppermute | solution.py:241
  75.6 7.2 %collective-permute-start.32 = (bf16[528,128]{1,0:T(8,128)(2,1)S(1)}, bf16[528,128]{1,0:T(8,128)(2,1)S(1)}, u32[]{:S(2)}, u32[]{:S(2)}) collective-permute-start(bf16[528,128]{1,0:T(8,128)(2,1)S(1)} %collective-permute-done.16.refs_13_), channel_id=1, source_target_pairs={{0,64},{64,0},{128,192},{192,128},{1,65},{65,1},{129,193},{193,129... | collective-permute-start | bytes 405512 | tf_op jit(solution)/shard_map/ppermute | solution.py:241
  76.6 6.2 %collective-permute-start.18 = (bf16[528,128]{1,0:T(8,128)(2,1)S(1)}, bf16[528,128]{1,0:T(8,128)(2,1)S(1)}, u32[]{:S(2)}, u32[]{:S(2)}) collective-permute-start(bf16[528,128]{1,0:T(8,128)(2,1)S(1)} %collective-permute-done.16.refs_13_), channel_id=1, source_target_pairs={{0,56},{4,60},{8,0},{12,4},{16,8},{20,12},{24,16},{28,20},{32,24},... | collective-permute-start | bytes 405512 | tf_op jit(solution)/shard_map/ppermute | solution.py:241
  82.0 1.9 %collective-permute-start.31 = (bf16[528,128]{1,0:T(8,128)(2,1)S(1)}, bf16[528,128]{1,0:T(8,128)(2,1)S(1)}, u32[]{:S(2)}, u32[]{:S(2)}) collective-permute-start(bf16[528,128]{1,0:T(8,128)(2,1)S(1)} %collective-permute-done.15.refs_12_), channel_id=1, source_target_pairs={{0,64},{64,0},{128,192},{192,128},{1,65},{65,1},{129,193},{193,129... | collective-permute-start | bytes 405512 | tf_op jit(solution)/shard_map/ppermute | solution.py:241
  82.8 1.4 collective-permute-start.30
  82.8 6.2 %collective-permute-start.17 = (bf16[528,128]{1,0:T(8,128)(2,1)S(1)}, bf16[528,128]{1,0:T(8,128)(2,1)S(1)}, u32[]{:S(2)}, u32[]{:S(2)}) collective-permute-start(bf16[528,128]{1,0:T(8,128)(2,1)S(1)} %collective-permute-done.13.refs_10_), channel_id=1, source_target_pairs={{0,8},{4,12},{8,16},{12,20},{16,24},{20,28},{24,32},{28,36},{32,40... | collective-permute-start | bytes 405512 | tf_op jit(solution)/shard_map/ppermute | solution.py:241
  83.8 6.6 %collective-permute-start.29 = (bf16[528,128]{1,0:T(8,128)(2,1)S(1)}, bf16[528,128]{1,0:T(8,128)(2,1)S(1)}, u32[]{:S(2)}, u32[]{:S(2)}) collective-permute-start(bf16[528,128]{1,0:T(8,128)(2,1)S(1)} %collective-permute-done.13.refs_10_), channel_id=1, source_target_pairs={{0,64},{64,0},{128,192},{192,128},{1,65},{65,1},{129,193},{193,129... | collective-permute-start | bytes 405512 | tf_op jit(solution)/shard_map/ppermute | solution.py:241
  84.2 6.3 %collective-permute-start.34 = (bf16[528,128]{1,0:T(8,128)(2,1)S(1)}, bf16[528,128]{1,0:T(8,128)(2,1)S(1)}, u32[]{:S(2)}, u32[]{:S(2)}) collective-permute-start(bf16[528,128]{1,0:T(8,128)(2,1)S(1)} %collective-permute-done.18.refs_15_), channel_id=1, source_target_pairs={{0,64},{64,0},{128,192},{192,128},{1,65},{65,1},{129,193},{193,129... | collective-permute-start | bytes 405512 | tf_op jit(solution)/shard_map/ppermute | solution.py:241
  89.0 2.4 %collective-permute-start.33 = (bf16[528,128]{1,0:T(8,128)(2,1)S(1)}, bf16[528,128]{1,0:T(8,128)(2,1)S(1)}, u32[]{:S(2)}, u32[]{:S(2)}) collective-permute-start(bf16[528,128]{1,0:T(8,128)(2,1)S(1)} %collective-permute-done.17.refs_14_), channel_id=1, source_target_pairs={{0,64},{64,0},{128,192},{192,128},{1,65},{65,1},{129,193},{193,129... | collective-permute-start | bytes 405512 | tf_op jit(solution)/shard_map/ppermute | solution.py:241
  106.5 8.8 %collective-permute-start.37 = (f16[1024,128]{1,0:T(8,128)(2,1)S(1)}, f16[1024,128]{1,0:T(8,128)(2,1)S(1)}, u32[]{:S(2)}, u32[]{:S(2)}) collective-permute-start(f16[1024,128]{1,0:T(8,128)(2,1)S(1)} %get-tuple-element.13), channel_id=1, source_target_pairs={{0,1},{1,2},{2,3},{3,0},{4,5},{5,6},{6,7},{7,4},{8,9},{9,10},{10,1... | collective-permute-start | bytes 786440 | tf_op jit(solution)/shard_map/ppermute | solution.py:241
  106.6 9.0 %collective-permute-start.41 = (f16[1024,128]{1,0:T(8,128)(2,1)S(1)}, f16[1024,128]{1,0:T(8,128)(2,1)S(1)}, u32[]{:S(2)}, u32[]{:S(2)}) collective-permute-start(f16[1024,128]{1,0:T(8,128)(2,1)S(1)} %get-tuple-element.14), channel_id=1, source_target_pairs={{0,3},{1,0},{2,1},{3,2},{4,7},{5,4},{6,5},{7,6},{8,11},{9,8},{10,9... | collective-permute-start | bytes 786440 | tf_op jit(solution)/shard_map/ppermute | solution.py:241
  109.2 10.6 %collective-permute-start.39 = (f16[1024,128]{1,0:T(8,128)(2,1)S(1)}, f16[1024,128]{1,0:T(8,128)(2,1)S(1)}, u32[]{:S(2)}, u32[]{:S(2)}) collective-permute-start(f16[1024,128]{1,0:T(8,128)(2,1)S(1)} %get-tuple-element.16), channel_id=1, source_target_pairs={{0,3},{1,0},{2,1},{3,2},{4,7},{5,4},{6,5},{7,6},{8,11},{9,8},{10,9... | collective-permute-start | bytes 786440 | tf_op jit(solution)/shard_map/ppermute | solution.py:241
  115.4 7.9 %collective-permute-start.38 = (f16[1024,128]{1,0:T(8,128)(2,1)S(1)}, f16[1024,128]{1,0:T(8,128)(2,1)S(1)}, u32[]{:S(2)}, u32[]{:S(2)}) collective-permute-start(f16[1024,128]{1,0:T(8,128)(2,1)S(1)} %fusion.5), channel_id=1, source_target_pairs={{0,1},{1,2},{2,3},{3,0},{4,5},{5,6},{6,7},{7,4},{8,9},{9,10},{10,1... | collective-permute-start | bytes 786440 | tf_op jit(solution)/shard_map/ppermute | solution.py:241
  115.5 13.5 %collective-permute-start.40 = (f16[1024,128]{1,0:T(8,128)(2,1)S(1)}, f16[1024,128]{1,0:T(8,128)(2,1)S(1)}, u32[]{:S(2)}, u32[]{:S(2)}) collective-permute-start(f16[1024,128]{1,0:T(8,128)(2,1)S(1)} %get-tuple-element.15), channel_id=1, source_target_pairs={{0,1},{1,2},{2,3},{3,0},{4,5},{5,6},{6,7},{7,4},{8,9},{9,10},{10,1... | collective-permute-start | bytes 786440 | tf_op jit(solution)/shard_map/ppermute | solution.py:241
  123.5 5.6 %collective-permute-start.42 = (f16[1024,128]{1,0:T(8,128)(2,1)S(1)}, f16[1024,128]{1,0:T(8,128)(2,1)S(1)}, u32[]{:S(2)}, u32[]{:S(2)}) collective-permute-start(f16[1024,128]{1,0:T(8,128)(2,1)S(1)} %get-tuple-element.10), channel_id=1, source_target_pairs={{0,3},{1,0},{2,1},{3,2},{4,7},{5,4},{6,5},{7,6},{8,11},{9,8},{10,9... | collective-permute-start | bytes 786440 | tf_op jit(solution)/shard_map/ppermute | solution.py:241
  129.4 16.6 %collective-permute-start.43 = (f16[2048,128]{1,0:T(8,128)(2,1)S(1)}, f16[2048,128]{1,0:T(8,128)(2,1)S(1)}, u32[]{:S(2)}, u32[]{:S(2)}) collective-permute-start(f16[2048,128]{1,0:T(8,128)(2,1)S(1)} %pad_maximum_fusion), channel_id=1, source_target_pairs={{0,4},{4,64},{8,12},{12,72},{16,20},{20,80},{24,28},{28,88},{32,36... | collective-permute-start | bytes 1572872 | tf_op jit(solution)/shard_map/ppermute | solution.py:241
  136.2 9.0 %collective-permute-start.47 = (f32[128]{0:T(128)S(1)}, f32[128]{0:T(128)S(1)}, u32[]{:S(2)}, u32[]{:S(2)}) collective-permute-start(f32[128]{0:T(128)S(1)} %multiply_reduce_fusion), channel_id=1, source_target_pairs={{0,196},{4,128},{8,204},{12,136},{16,212},{20,144},{24,220},{28,15... | collective-permute-start | bytes 1544 | tf_op jit(solution)/shard_map/ppermute | solution.py:241
  136.7 8.5 %collective-permute-start.46 = (f32[128]{0:T(128)S(1)}, f32[128]{0:T(128)S(1)}, u32[]{:S(2)}, u32[]{:S(2)}) collective-permute-start(f32[128]{0:T(128)S(1)} %multiply_reduce_fusion), channel_id=1, source_target_pairs={{0,132},{4,192},{8,140},{12,200},{16,148},{20,208},{24,156},{28,21... | collective-permute-start | bytes 1544 | tf_op jit(solution)/shard_map/ppermute | solution.py:241
  138.0 7.2 %collective-permute-start.45 = (f32[128]{0:T(128)S(1)}, f32[128]{0:T(128)S(1)}, u32[]{:S(2)}, u32[]{:S(2)}) collective-permute-start(f32[128]{0:T(128)S(1)} %multiply_reduce_fusion), channel_id=1, source_target_pairs={{0,68},{4,0},{8,76},{12,8},{16,84},{20,16},{24,92},{28,24},{32,100... | collective-permute-start | bytes 1544 | tf_op jit(solution)/shard_map/ppermute | solution.py:241
  138.7 7.3 %collective-permute-start.44 = (f32[128]{0:T(128)S(1)}, f32[128]{0:T(128)S(1)}, u32[]{:S(2)}, u32[]{:S(2)}) collective-permute-start(f32[128]{0:T(128)S(1)} %multiply_reduce_fusion), channel_id=1, source_target_pairs={{0,4},{4,64},{8,12},{12,72},{16,20},{20,80},{24,28},{28,88},{32,36... | collective-permute-start | bytes 1544 | tf_op jit(solution)/shard_map/ppermute | solution.py:241
  (7 other events, 24.4 us)
where the time goes:
time: 148 us; the launch traced here: 147 us
  starting transfers between devices  74.3 us (50%)
  waiting for transfers between devices  41.7 us (28%)
  Pallas kernels  20.2 us (14%)
  local copies, waits for them, and re-layouts  6.42 us (4%)
  other arithmetic  4.21 us (3%)
    ppermute x48, starting transfers between devices, named(): return lax.ppermute(array, axes, perm)  74.3 us
    ppermute x48, waiting for transfers between devices, named(): return lax.ppermute(array, axes, perm)  41.7 us
    pallas_call x1, Pallas kernels, product(): pl.pallas_call(functools.partial(product_kernel, n_parts, counts, per), o...  11.6 us
    pallas_call x1, Pallas kernels, mask_block(): pl.pallas_call(mask_kernel, out_shape=(jax.ShapeDtypeStruct((2, height //...  4.27 us
    unnamed x15, local copies, waits for them, and re-layouts  3.55 us
  transfers between devices with their start and end apart: 48, of which 19 were waited for; matrix products, arithmetic and copies ran while one was open for 2% of the time, Pallas kernels for 3%

commit v1 on v0

v1 whole, which is shorter than its diff:
```python
import functools

import jax
import jax.numpy as jnp
from jax import lax
from jax.experimental import pallas as pl
from jax.experimental.pallas import tpu as pltpu
from jax.sharding import PartitionSpec as P


T = 128
HEAD = 16
SCALE = 16.0
GRANT = 16 * 2**20
VMEM = pl.BlockSpec(memory_space=pltpu.VMEM)
HBM = pl.BlockSpec(memory_space=pltpu.HBM)
ANY = pl.BlockSpec(memory_space=pl.ANY)


def share_kernel(halves, per, depth_tiles, mask_hbm, values_hbm, part_ref, mask_ref, table_ref, sem):
    tiles_c, tiles_r = mask_ref.shape
    layer, col = lax.axis_index("layer"), lax.axis_index("col")
    z = lax.div(col, 2)
    section = ((lax.div(z, 4) ^ (z & 1)) * 2) + (col & 1)
    dead = tiles_r * tiles_c
    count = halves * per
    size = HEAD + per * T
    copy = pltpu.make_async_copy(mask_hbm, mask_ref, sem)
    copy.start()
    copy.wait()
    for s in range(count):
        table_ref[s] = dead
    n = -layer * count
    for i in range(tiles_r):
        for c in range(tiles_c):
            live = mask_ref[c, i] != 0
            spot = jnp.where(live & (n >= 0) & (n < count), n, count)
            table_ref[spot] = i * tiles_c + c
            n = n + live.astype(jnp.int32)
    starts = [(s // per) * size + HEAD + (s % per) * T for s in range(count)]

    def fetch(s):
        t = table_ref[s]
        i, c = lax.div(t, tiles_c), lax.rem(t, tiles_c)
        return pltpu.make_async_copy(
            values_hbm.at[pl.ds(pl.multiple_of(i * T, T), T), pl.ds(pl.multiple_of(c * T, T), T)],
            part_ref.at[starts[s]:starts[s] + T, :],
            sem,
        )

    for s in range(count):
        @pl.when(table_ref[s] < dead)
        def _():
            fetch(s).start()

        @pl.when(table_ref[s] >= dead)
        def _():
            part_ref[starts[s]:starts[s] + T, :] = jnp.zeros((T, T), jnp.bfloat16)

    row = lax.broadcasted_iota(jnp.int32, (HEAD, T), 0)
    for h in range(halves):
        head = jnp.full((HEAD, T), tiles_r * depth_tiles, jnp.int32)
        for j in range(per):
            t = table_ref[h * per + j]
            at = lax.div(t, tiles_c) * depth_tiles + section * tiles_c + lax.rem(t, tiles_c)
            head = jnp.where((row == j) & (t < dead), at, head)
        part_ref[h * size:h * size + HEAD, :] = head.astype(jnp.float32).astype(jnp.bfloat16)
    for s in range(count):
        @pl.when(table_ref[s] < dead)
        def _():
            fetch(s).wait()


def share(mask, values, per, halves, depth_tiles):
    return pl.pallas_call(
        functools.partial(share_kernel, halves, per, depth_tiles),
        out_shape=pltpu.VMEM((halves * (HEAD + per * T), T), jnp.bfloat16),
        in_specs=[HBM, HBM],
        out_specs=VMEM,
        scratch_shapes=[
            pltpu.SMEM(mask.shape, jnp.int32),
            pltpu.SMEM((halves * per + 1,), jnp.int32),
            pltpu.SemaphoreType.DMA,
        ],
        cost_estimate=pl.CostEstimate(flops=2**20, bytes_accessed=2 * 2**20, transcendentals=0),
        compiler_params=pltpu.CompilerParams(vmem_limit_bytes=GRANT),
        name="share",
    )(mask, values)


def load(mask_hbm, mask_ref, sem):
    copy = pltpu.make_async_copy(mask_hbm, mask_ref, sem)
    copy.start()
    copy.wait()


def sums_kernel(mask_hbm, values_ref, sums_ref, mask_ref, sem):
    tiles_c, tiles_r = mask_ref.shape
    load(mask_hbm, mask_ref, sem)
    for c in range(tiles_c):
        total = jnp.zeros((8, T), jnp.float32)
        for i in range(tiles_r):
            tile = values_ref[i * T:(i + 1) * T, c * T:(c + 1) * T].astype(jnp.float32)
            part = jnp.sum(tile.reshape(T // 8, 8, T), axis=0)
            total = total + jnp.where(mask_ref[c, i] != 0, part, 0.0)
        sums_ref[c:c + 1, :] = jnp.sum(total, axis=0, keepdims=True)


def column_sums(mask, values):
    return pl.pallas_call(
        sums_kernel,
        out_shape=pltpu.VMEM((mask.shape[0], T), jnp.float32),
        in_specs=[ANY, VMEM],
        out_specs=VMEM,
        scratch_shapes=[pltpu.SMEM(mask.shape, jnp.int32), pltpu.SemaphoreType.DMA],
        cost_estimate=pl.CostEstimate(flops=2**20, bytes_accessed=2 * 2**20, transcendentals=0),
        compiler_params=pltpu.CompilerParams(vmem_limit_bytes=GRANT),
        name="column_sums",
    )(mask, values)


def halves_kernel(mask_hbm, values_ref, *refs):
    out_refs, (mask_ref, sem) = refs[:2], refs[2:]
    tiles_c, tiles_r = mask_ref.shape
    load(mask_hbm, mask_ref, sem)
    x_lo = lax.div(lax.axis_index("row"), 2)
    for m, ref in enumerate(out_refs):
        first = (m ^ x_lo) * (tiles_r // 2)
        for i in range(tiles_r // 2):
            at = pl.ds(pl.multiple_of((first + i) * T, T), T)
            for c in range(tiles_c):
                tile = values_ref[at, c * T:(c + 1) * T]
                ref[i * T:(i + 1) * T, c * T:(c + 1) * T] = jnp.where(
                    mask_ref[c, first + i] != 0, tile, jnp.zeros_like(tile))


def masked_halves(mask, values):
    height, width = values.shape
    return pl.pallas_call(
        halves_kernel,
        out_shape=(pltpu.VMEM((height // 2, width), jnp.bfloat16),) * 2,
        in_specs=[ANY, VMEM],
        out_specs=(VMEM, VMEM),
        scratch_shapes=[pltpu.SMEM(mask.shape, jnp.int32), pltpu.SemaphoreType.DMA],
        cost_estimate=pl.CostEstimate(flops=2**20, bytes_accessed=4 * 2**20, transcendentals=0),
        compiler_params=pltpu.CompilerParams(vmem_limit_bytes=GRANT),
        name="masked_halves",
    )(mask, values)


def scale_kernel(halves, per, raw_ref, mass_ref, part_ref):
    size = HEAD + per * T
    sums = mass_ref[...] / SCALE
    tiles_c = sums.shape[0]
    for h in range(halves):
        head = raw_ref[h * size:h * size + HEAD, :]
        part_ref[h * size:h * size + HEAD, :] = head
        which = lax.rem(head.astype(jnp.float32).astype(jnp.int32), tiles_c)
        for j in range(per):
            mine = which[j:j + 1, :]
            mass = sums[0:1, :]
            for c in range(1, tiles_c):
                mass = jnp.where(mine == c, sums[c:c + 1, :], mass)
            at = slice(h * size + HEAD + j * T, h * size + HEAD + (j + 1) * T)
            part_ref[at, :] = (raw_ref[at, :].astype(jnp.float32) / mass).astype(jnp.bfloat16)


def scale(raw, mass, per, halves):
    return pl.pallas_call(
        functools.partial(scale_kernel, halves, per),
        out_shape=pltpu.VMEM(raw.shape, raw.dtype),
        in_specs=[VMEM, VMEM],
        out_specs=VMEM,
        cost_estimate=pl.CostEstimate(flops=2**20, bytes_accessed=2**20, transcendentals=0),
        compiler_params=pltpu.CompilerParams(vmem_limit_bytes=GRANT),
        name="scale",
    )(raw, mass)


def product_kernel(n_parts, counts, per, again, *refs):
    part_refs = refs[:n_parts]
    right_refs = refs[n_parts:2 + n_parts]
    out_ref = refs[2 + n_parts + again]
    spots, table, sem = refs[3 + n_parts + again:]
    layer = lax.axis_index("layer")
    n_layer, rows, _ = out_ref.shape
    depth = right_refs[0].shape[0]
    kt = 2 * depth // T
    dead = rows // T * kt
    size = HEAD + per * T

    lane = lax.broadcasted_iota(jnp.int32, (8, T), 1)
    found = jnp.zeros((8, T), jnp.int32)
    q = 0
    for ref, count in zip(part_refs, counts, strict=True):
        for h in range(count):
            head = ref[h * size:h * size + HEAD, :].astype(jnp.float32).astype(jnp.int32)
            found = jnp.where(lane == q, head[:8, :], found)
            q += 1
    spots[...] = found
    if not again:
        def zero(i, _):
            out_ref[:, pl.ds(pl.multiple_of(i * T, T), T), :] = jnp.zeros((n_layer, T, T), jnp.float32)
            return 0

        lax.fori_loop(0, rows // T, zero, 0)
    copy = pltpu.make_async_copy(spots, table, sem)
    copy.start()
    copy.wait()
    q = 0
    for ref, count in zip(part_refs, counts, strict=True):
        def add(s, _, ref=ref, q=q):
            h, j = lax.div(s, per), lax.rem(s, per)
            t = table[j, q + h]
            tile = pl.ds(pl.multiple_of(h * size + HEAD + j * T, HEAD), T)
            k = lax.rem(t, kt)
            at = pl.ds(pl.multiple_of(lax.div(t, kt) * T, T), T)
            rows_of = pl.ds(pl.multiple_of(lax.rem(k, kt // 2) * T, T), T)
            for m, right_ref in enumerate(right_refs):
                @pl.when((t < dead) & (lax.div(k, kt // 2) == m))
                def _():
                    out = jnp.dot(ref[tile, :], right_ref[rows_of, :], preferred_element_type=jnp.float32)
                    for g in range(n_layer):
                        chunk = lax.rem(g + n_layer - layer, n_layer)
                        out_ref[chunk, at, :] += out[:, g * T:(g + 1) * T]
            return 0

        lax.fori_loop(0, count * per, add, 0)
        q += count


def product(parts, counts, per, rights, rows, n_layer, total=None):
    n_parts = len(parts)
    width = rights[0].shape[1]
    again = total is not None
    tiles = sum(counts) * per
    return pl.pallas_call(
        functools.partial(product_kernel, n_parts, counts, per, again),
        out_shape=pltpu.VMEM((n_layer, rows, width // n_layer), jnp.float32),
        in_specs=[VMEM] * (n_parts + 2 + again),
        out_specs=VMEM,
        scratch_shapes=[
            pltpu.VMEM((8, T), jnp.int32),
            pltpu.SMEM((8, T), jnp.int32),
            pltpu.SemaphoreType.DMA,
        ],
        input_output_aliases={n_parts + 2: 0} if again else {},
        cost_estimate=pl.CostEstimate(flops=2 * tiles * T * T * width, bytes_accessed=2**20, transcendentals=0),
        compiler_params=pltpu.CompilerParams(vmem_limit_bytes=GRANT),
        name="add_product" if again else "product",
    )(*parts, *rights, *((total,) if again else ()))


def coords(sizes):
    n_row, n_col, n_layer = sizes
    for r in range(n_row):
        for c in range(n_col):
            for y in range(n_layer):
                yield r, c, y


def flat(r, c, y, sizes):
    return (r * sizes[1] + c) * sizes[2] + y


def shards(sizes, values, tile_mask):
    n_row, n_col, n_layer = sizes
    axes = ("row", "col", "layer")
    height, _ = values.shape
    slots = tile_mask.size // 2
    halves = 2
    per = slots // n_layer // halves
    half = HEAD + per * T
    n_z = n_col // 2
    depth = height * n_row // n_layer
    f16, f32 = jnp.float16, jnp.float32

    mask = tile_mask.T
    raw = share(mask, values, per, halves, depth // T)

    spread = {}
    for r, c, y in coords(sizes):
        zz, hi = c // 2, c % 2
        y_to = zz % n_layer
        move = {0: 2 - 4 * hi, 1: 1, 2: 0, 3: -1}[(y - y_to) % n_layer]
        spread[r, c, y] = flat(r // 2 * 2 + hi, (zz + move) % n_z * 2 + r % 2, y_to, sizes)
    table = [(flat(*at, sizes), to) for at, to in spread.items()]
    raw = lax.ppermute(raw, axes, table)
    mass = lax.ppermute(lax.psum(column_sums(mask, values), "row"), axes, table)
    rights = list(masked_halves(mask, values))
    part = scale(raw, mass, per, halves)

    def ring(step):
        return [(c, (c // 2 + step) % n_z * 2 + c % 2) for c in range(n_col)]

    swap = [(r, r ^ 1) for r in range(n_row)]
    last = n_z // 2
    mine = [part]
    up = down = part
    for step in range(1, last + 1):
        if step == last:
            up, down = up[:half], down[half:]
        up = lax.ppermute(up, "col", ring(1))
        down = lax.ppermute(down, "col", ring(-1))
        mine += [up, down]
    parts = [(p, lax.ppermute(p, "row", swap)) for p in mine]

    n_x = n_row // 2 * 2
    for m in range(2):
        perm = []
        for r, c, y in coords(sizes):
            lo, core, zz, hi = r // 2, r % 2, c // 2, c % 2
            y_to = core * 2 + (m ^ lo)
            x_to = (hi * 2 + lo + 2 - (y - y_to)) % n_x
            lo_to, hi_to = x_to % 2, x_to // 2
            to = (lo_to * 2 + (hi ^ hi_to ^ lo_to ^ 1), zz * 2 + hi_to, y_to)
            perm.append((flat(r, c, y, sizes), flat(*to, sizes)))
        rights[m] = lax.ppermute(rights[m], axes, perm)
    early = [p for pair in parts[:2 * last - 3] for p in pair]
    late = [p for pair in parts[2 * last - 3:] for p in pair]
    out = product(early, [p.shape[0] // half for p in early], per, rights, height, n_layer)
    out = product(late, [p.shape[0] // half for p in late], per, rights, height, n_layer, out)

    up = [(y, (y + 1) % n_layer) for y in range(n_layer)]
    down = [(y, (y - 1) % n_layer) for y in range(n_layer)]
    mid = height // 2
    send = lax.optimization_barrier(out[1:].astype(f16))
    far_a = lax.ppermute(send[1, :mid], "layer", up)
    far_b = lax.ppermute(send[1, mid:], "layer", down)
    up_b = lax.ppermute(send[0, mid:], "layer", up)
    down_a = lax.ppermute(send[2, :mid], "layer", down)
    up_a = (out[1, :mid] + far_a.astype(f32)).astype(f16)
    down_b = (out[3, mid:] + far_b.astype(f32)).astype(f16)
    up_a, down_b = lax.optimization_barrier((up_a, down_b))
    up_a = lax.ppermute(up_a, "layer", up)
    down_b = lax.ppermute(down_b, "layer", down)
    total = jnp.concatenate([
        out[0, :mid] + (up_a.astype(f32) + down_a.astype(f32)),
        out[0, mid:] + (up_b.astype(f32) + down_b.astype(f32)),
    ]).astype(f16)

    owner = {}
    for r in range(n_row):
        for c in range(n_col):
            lo, core, hi = r // 2, r % 2, c % 2
            owner[r, c] = (lo * 2 + hi, c // 2 * 2 + (core ^ hi ^ lo ^ 1))
    expanded = lax.ppermute(
        total, ("row", "col"), [(r * n_col + c, o[0] * n_col + o[1]) for (r, c), o in owner.items()])
    summand = total.astype(f32)
    summand = jnp.sum(summand * summand, axis=0)
    weights = []
    for k in range(1, n_row):
        perm = [(r * n_col + c, (o[0] ^ k) * n_col + o[1]) for (r, c), o in owner.items()]
        weights.append(lax.ppermute(summand, ("row", "col"), perm))
    expanded = expanded.astype(f32)
    inflated = expanded * expanded
    weight = jnp.sum(inflated, axis=0) + (weights[0] + (weights[1] + weights[2]))
    order = height * n_row
    return order * 1.0 * inflated / weight[None, :]


def solution(mesh):
    sizes = tuple(mesh.shape[a] for a in ("row", "col", "layer"))

    def body(values, tile_mask):
        return shards(sizes, values, tile_mask)

    return jax.shard_map(
        body,
        mesh=mesh,
        in_specs=(P("row", "col"), P("row", "col")),
        out_specs=P("row", ("col", "layer")),
        check_vma=False,
    )
```

time: 148 us -> 129 us (0.87)
  starting transfers between devices: 74.3 us -> 50.1 us
  Pallas kernels: 20.2 us -> 27.6 us
  blocking collectives: 0 us -> 5.76 us
  local copies, waits for them, and re-layouts: 6.42 us -> 2.51 us
  other arithmetic: 4.21 us -> 2.38 us
  waiting for transfers between devices: 41.7 us -> 39.9 us
    ppermute x48 -> x31, starting transfers between devices: 74.3 us -> 50.1 us  [the longest x9 10 us: shards(): parts = [(p, lax.ppermute(p, 'row', swap)) for p in mine]]
    pallas_call x3 -> x5, Pallas kernels: 17.6 us -> 26.4 us  [the longest x2 24.4 us: product(): pl.pallas_call(functools.partial(product_kernel, n_parts, counts, per, ag...]
    psum x0 -> x1, blocking collectives: none -> 5.76 us  [shards(): mass = lax.ppermute(lax.psum(column_sums(mask, values), 'row'), axes, table)]
    another operation x3 -> x2, other arithmetic: 2.58 us -> 0.41 us
    ppermute x48 -> x31, waiting for transfers between devices: 41.7 us -> 39.9 us  [the longest x4 15.2 us: shards(): up = lax.ppermute(up, 'col', ring(1))]
    squeeze x2 -> x1, local copies, waits for them, and re-layouts: 1.88 us -> 0.21 us  [shards(): down_a = lax.ppermute(send[2, :mid], 'layer', down)]
    pallas_call x1, Pallas kernels: 2.64 us -> 1.11 us  [share(): pl.pallas_call(functools.partial(share_kernel, halves, per, depth_tiles),...]
    unnamed x15 -> x8, local copies, waits for them, and re-layouts: 3.55 us -> 2.28 us
  transfers between devices with their start and end apart: 48 -> 31, of which waited for: 19 -> 13; matrix products, arithmetic and copies ran while one was open for 2% -> 1% of each run, Pallas kernels for 3% -> 16%
where the time goes in v1:
time: 129 us; the launch traced here: 128 us
  starting transfers between devices  50.1 us (39%)
  waiting for transfers between devices  39.9 us (31%)
  Pallas kernels  27.6 us (21%)
  blocking collectives  5.76 us (4%)
  local copies, waits for them, and re-layouts  2.51 us (2%)
  other arithmetic  2.38 us (2%)
    pallas_call x2, Pallas kernels, product(): pl.pallas_call(functools.partial(product_kernel, n_parts, counts, per, ag...  24.4 us
    ppermute x4, waiting for transfers between devices, shards(): up = lax.ppermute(up, 'col', ring(1))  15.2 us
    ppermute x9, starting transfers between devices, shards(): parts = [(p, lax.ppermute(p, 'row', swap)) for p in mine]  10 us
    ppermute x4, starting transfers between devices, shards(): down = lax.ppermute(down, 'col', ring(-1))  8.93 us
    ppermute x1, starting transfers between devices, shards(): raw = lax.ppermute(raw, axes, table)  6.86 us
    psum x1, blocking collectives, shards(): mass = lax.ppermute(lax.psum(column_sums(mask, values), 'row'), axes, table)  5.76 us
    ppermute x1, waiting for transfers between devices, shards(): up_a = lax.ppermute(up_a, 'layer', up)  5.62 us
    ppermute x2, starting transfers between devices, shards(): rights[m] = lax.ppermute(rights[m], axes, perm)  5.6 us
  transfers between devices with their start and end apart: 31, of which 13 were waited for; matrix products, arithmetic and copies ran while one was open for 1% of the time, Pallas kernels for 16%

profile of v1, /device:TPU:1, one launch (start us, length us, event | category | flops | bytes accessed | tf_op | source)
XLA Modules:
  0.0 128.5 jit_solution(15022833746716526492)
XLA Ops:
  0.0 1.6 %copy-done = bf16[2048,512]{1,0:T(8,128)(2,1)S(1)} copy-done((bf16[2048,512]{1,0:T(8,128)(2,1)S(1)}, bf16[2048,512]{1,0:T(8,128)(2,1)}, u32[]{:S(2)}) %copy-start) | copy-done | bytes 2097176
  1.6 0.7 copy-done.2
  2.3 1.1 share.1
  3.4 6.9 %collective-permute-start = (bf16[1056,128]{1,0:T(8,128)(2,1)S(1)}, bf16[1056,128]{1,0:T(8,128)(2,1)S(1)}, u32[]{:S(2)}, u32[]{:S(2)}) collective-permute-start(bf16[1056,128]{1,0:T(8,128)(2,1)S(1)} %share.1), channel_id=1, source_target_pairs={{0,16},{1,8},{2,0},{3,56},{4,112},{5,72},{6,64},{7,120},{8,1},{9,2... | collective-permute-start | bytes 811016 | tf_op jit(solution)/shard_map/ppermute | solution.py:288
  10.3 0.9 column_sums.1
  11.1 5.8 %psum.7 = f32[4,128]{1,0:T(4,128)S(1)} all-reduce(f32[4,128]{1,0:T(4,128)S(1)} %column_sums.1), channel_id=1, replica_groups=mesh['row'=4,'col'=16,'layer'=4] {'row'}, use_global_device_ids=true, to_apply=%region_0.0 | all-reduce | flops 512 | bytes 4096 | tf_op jit(solution)/shard_map/psum | solution.py:289
  16.9 5.2 %collective-permute-start.1 = (f32[4,128]{1,0:T(4,128)S(1)}, f32[4,128]{1,0:T(4,128)S(1)}, u32[]{:S(2)}, u32[]{:S(2)}) collective-permute-start(f32[4,128]{1,0:T(4,128)S(1)} %psum.7), channel_id=1, source_target_pairs={{0,16},{1,8},{2,0},{3,56},{4,112},{5,72},{6,64},{7,120},{8,1},{9,2... | collective-permute-start | bytes 6152 | tf_op jit(solution)/shard_map/ppermute | solution.py:289
  22.2 1.7 %collective-permute-done.1.mass_ref = f32[4,128]{1,0:T(4,128)S(1)} collective-permute-done((f32[4,128]{1,0:T(4,128)S(1)}, f32[4,128]{1,0:T(4,128)S(1)}, u32[]{:S(2)}, u32[]{:S(2)}) %collective-permute-start.1) | collective-permute-done | bytes 2080 | tf_op jit(solution)/shard_map/ppermute | solution.py:289
  23.9 3.7 %collective-permute-start.6 = (bf16[1056,128]{1,0:T(8,128)(2,1)S(1)}, bf16[1056,128]{1,0:T(8,128)(2,1)S(1)}, u32[]{:S(2)}, u32[]{:S(2)}) collective-permute-start(bf16[1056,128]{1,0:T(8,128)(2,1)S(1)} %scale.1.refs_0_), channel_id=1, source_target_pairs={{0,56},{4,60},{8,0},{12,4},{16,8},{20,12},{24,16},{28,20},{32,24},... | collective-permute-start | bytes 811016 | tf_op jit(solution)/shard_map/ppermute | solution.py:304
  27.6 1.1 masked_halves.1
  28.7 2.1 %collective-permute-start.14 = (bf16[1024,512]{1,0:T(8,128)(2,1)S(1)}, bf16[1024,512]{1,0:T(8,128)(2,1)S(1)}, u32[]{:S(2)}, u32[]{:S(2)}) collective-permute-start(bf16[1024,512]{1,0:T(8,128)(2,1)S(1)} %get-tuple-element.9), channel_id=1, source_target_pairs={{0,4},{1,128},{2,64},{3,196},{4,0},{5,132},{6,68},{7,192},{8,12},{... | collective-permute-start | bytes 3145736 | tf_op jit(solution)/shard_map/ppermute | solution.py:318
  30.8 3.5 %collective-permute-start.15 = (bf16[1024,512]{1,0:T(8,128)(2,1)S(1)}, bf16[1024,512]{1,0:T(8,128)(2,1)S(1)}, u32[]{:S(2)}, u32[]{:S(2)}) collective-permute-start(bf16[1024,512]{1,0:T(8,128)(2,1)S(1)} %get-tuple-element.10), channel_id=1, source_target_pairs={{0,197},{1,5},{2,129},{3,65},{4,193},{5,1},{6,133},{7,69},{8,205},... | collective-permute-start | bytes 3145736 | tf_op jit(solution)/shard_map/ppermute | solution.py:318
  34.3 1.2 collective-permute-start.16
  35.6 2.0 %collective-permute-start.7 = (bf16[1056,128]{1,0:T(8,128)(2,1)S(1)}, bf16[1056,128]{1,0:T(8,128)(2,1)S(1)}, u32[]{:S(2)}, u32[]{:S(2)}) collective-permute-start(bf16[1056,128]{1,0:T(8,128)(2,1)S(1)} %collective-permute-done.6.refs_4_), channel_id=1, source_target_pairs={{0,56},{4,60},{8,0},{12,4},{16,8},{20,12},{24,16},{28,20},{32,24},... | collective-permute-start | bytes 811016 | tf_op jit(solution)/shard_map/ppermute | solution.py:304
  37.5 5.8 %collective-permute-done.2.refs_2_ = bf16[1056,128]{1,0:T(8,128)(2,1)S(1)} collective-permute-done((bf16[1056,128]{1,0:T(8,128)(2,1)S(1)}, bf16[1056,128]{1,0:T(8,128)(2,1)S(1)}, u32[]{:S(2)}, u32[]{:S(2)}) %collective-permute-start.2) | collective-permute-done | bytes 270368 | tf_op jit(solution)/shard_map/ppermute | solution.py:303
  43.3 1.1 collective-permute-start.18
  44.4 3.0 %collective-permute-start.8 = (bf16[1056,128]{1,0:T(8,128)(2,1)S(1)}, bf16[1056,128]{1,0:T(8,128)(2,1)S(1)}, u32[]{:S(2)}, u32[]{:S(2)}) collective-permute-start(bf16[1056,128]{1,0:T(8,128)(2,1)S(1)} %collective-permute-done.7.refs_8_), channel_id=1, source_target_pairs={{0,56},{4,60},{8,0},{12,4},{16,8},{20,12},{24,16},{28,20},{32,24},... | collective-permute-start | bytes 811016 | tf_op jit(solution)/shard_map/ppermute | solution.py:304
  47.4 4.1 %collective-permute-done.3.refs_6_ = bf16[1056,128]{1,0:T(8,128)(2,1)S(1)} collective-permute-done((bf16[1056,128]{1,0:T(8,128)(2,1)S(1)}, bf16[1056,128]{1,0:T(8,128)(2,1)S(1)}, u32[]{:S(2)}, u32[]{:S(2)}) %collective-permute-start.3) | collective-permute-done | bytes 270368 | tf_op jit(solution)/shard_map/ppermute | solution.py:303
  51.5 2.0 %collective-permute-start.17 = (bf16[1056,128]{1,0:T(8,128)(2,1)S(1)}, bf16[1056,128]{1,0:T(8,128)(2,1)S(1)}, u32[]{:S(2)}, u32[]{:S(2)}) collective-permute-start(bf16[1056,128]{1,0:T(8,128)(2,1)S(1)} %collective-permute-done.2.refs_2_), channel_id=1, source_target_pairs={{0,64},{64,0},{128,192},{192,128},{1,65},{65,1},{129,193},{193,129... | collective-permute-start | bytes 811016 | tf_op jit(solution)/shard_map/ppermute | solution.py:306
  53.4 0.6 collective-permute-start.20
  54.1 4.7 %collective-permute-done.4.refs_0_ = bf16[1056,128]{1,0:T(8,128)(2,1)S(1)} collective-permute-done((bf16[1056,128]{1,0:T(8,128)(2,1)S(1)}, bf16[1056,128]{1,0:T(8,128)(2,1)S(1)}, u32[]{:S(2)}, u32[]{:S(2)}) %collective-permute-start.4) | collective-permute-done | bytes 270368 | tf_op jit(solution)/shard_map/ppermute | solution.py:303
  58.8 2.8 %collective-permute-start.19 = (bf16[1056,128]{1,0:T(8,128)(2,1)S(1)}, bf16[1056,128]{1,0:T(8,128)(2,1)S(1)}, u32[]{:S(2)}, u32[]{:S(2)}) collective-permute-start(bf16[1056,128]{1,0:T(8,128)(2,1)S(1)} %collective-permute-done.3.refs_6_), channel_id=1, source_target_pairs={{0,64},{64,0},{128,192},{192,128},{1,65},{65,1},{129,193},{193,129... | collective-permute-start | bytes 811016 | tf_op jit(solution)/shard_map/ppermute | solution.py:306
  61.6 0.3 collective-permute-start.12
  62.1 1.3 collective-permute-start.10
  63.4 0.6 collective-permute-start.9
  64.0 3.0 %collective-permute-done.12.refs_6_ = bf16[528,128]{1,0:T(8,128)(2,1)S(1)} collective-permute-done((bf16[528,128]{1,0:T(8,128)(2,1)S(1)}, bf16[528,128]{1,0:T(8,128)(2,1)S(1)}, u32[]{:S(2)}, u32[]{:S(2)}) %collective-permute-start.12) | collective-permute-done | bytes 135200 | tf_op jit(solution)/shard_map/ppermute | solution.py:304
  67.0 0.9 collective-permute-start.13
  67.9 0.7 collective-permute-done.10.refs_4_
  68.5 0.8 collective-permute-start.11
  69.3 18.1 %product.1.refs_10_ = f32[4,2048,128]{2,1,0:T(8,128)S(1)} custom-call(bf16[1056,128]{1,0:T(8,128)(2,1)S(1)} %scale.1.refs_0_, bf16[1056,128]{1,0:T(8,128)(2,1)S(1)} %collective-permute-done.16.refs_1_, bf16[1056,128]{1,0:T(8,128)(2,1)S(1)} %collective-permute-done.2.refs_2_, bf16[1056,128]{1,0:T(8,128)(2,1)S(1)} %collective-permute-done.17.refs_3_, ...), custom_call_target="tpu_custom_call" | custom-call | flops 1342177280 | bytes 1048576 | tf_op jit(solution)/shard_map/product/pallas_call | solution.py:237
  87.4 6.3 %add_product.1 = f32[4,2048,128]{2,1,0:T(8,128)S(1)} custom-call(bf16[1056,128]{1,0:T(8,128)(2,1)S(1)} %collective-permute-done.4.refs_0_, bf16[1056,128]{1,0:T(8,128)(2,1)S(1)} %collective-permute-done.5.refs_1_, bf16[1056,128]{1,0:T(8,128)(2,1)S(1)} %collective-permute-done.8.refs_2_, ...), custom_call_target="tpu_custom_call", output_to_operand_aliasing={{}: (10, {})} | custom-call | flops 805306368 | bytes 1048576 | tf_op jit(solution)/shard_map/add_product/pallas_call | solution.py:237
  94.0 0.2 slice_bitcast_fusion.5
  94.3 1.5 %collective-permute-start.21 = (f16[1024,128]{1,0:T(8,128)(2,1)S(1)}, f16[1024,128]{1,0:T(8,128)(2,1)S(1)}, u32[]{:S(2)}, u32[]{:S(2)}) collective-permute-start(f16[1024,128]{1,0:T(8,128)(2,1)S(1)} %get-tuple-element.20), channel_id=1, source_target_pairs={{0,1},{1,2},{2,3},{3,0},{4,5},{5,6},{6,7},{7,4},{8,9},{9,10},{10,1... | collective-permute-start | bytes 786440 | tf_op jit(solution)/shard_map/ppermute | solution.py:328
  95.8 1.3 %collective-permute-start.24 = (f16[1024,128]{1,0:T(8,128)(2,1)S(1)}, f16[1024,128]{1,0:T(8,128)(2,1)S(1)}, u32[]{:S(2)}, u32[]{:S(2)}) collective-permute-start(f16[1024,128]{1,0:T(8,128)(2,1)S(1)} %get-tuple-element.17), channel_id=1, source_target_pairs={{0,3},{1,0},{2,1},{3,2},{4,7},{5,4},{6,5},{7,6},{8,11},{9,8},{10,9... | collective-permute-start | bytes 786440 | tf_op jit(solution)/shard_map/ppermute | solution.py:331
  97.2 4.9 %collective-permute-done.22 = f16[1024,128]{1,0:T(8,128)(2,1)S(1)} collective-permute-done((f16[1024,128]{1,0:T(8,128)(2,1)S(1)}, f16[1024,128]{1,0:T(8,128)(2,1)S(1)}, u32[]{:S(2)}, u32[]{:S(2)}) %collective-permute-start.22) | collective-permute-done | bytes 262176 | tf_op jit(solution)/shard_map/ppermute | solution.py:329
  102.1 1.3 %collective-permute-done.21 = f16[1024,128]{1,0:T(8,128)(2,1)S(1)} collective-permute-done((f16[1024,128]{1,0:T(8,128)(2,1)S(1)}, f16[1024,128]{1,0:T(8,128)(2,1)S(1)}, u32[]{:S(2)}, u32[]{:S(2)}) %collective-permute-start.21) | collective-permute-done | bytes 262176 | tf_op jit(solution)/shard_map/ppermute | solution.py:328
  103.7 2.7 %collective-permute-start.26 = (f16[1024,128]{1,0:T(8,128)(2,1)S(1)}, f16[1024,128]{1,0:T(8,128)(2,1)S(1)}, u32[]{:S(2)}, u32[]{:S(2)}) collective-permute-start(f16[1024,128]{1,0:T(8,128)(2,1)S(1)} %get-tuple-element.12), channel_id=1, source_target_pairs={{0,3},{1,0},{2,1},{3,2},{4,7},{5,4},{6,5},{7,6},{8,11},{9,8},{10,9... | collective-permute-start | bytes 786440 | tf_op jit(solution)/shard_map/ppermute | solution.py:336
  106.3 1.4 %collective-permute-done.24 = f16[1024,128]{1,0:T(8,128)(2,1)S(1)} collective-permute-done((f16[1024,128]{1,0:T(8,128)(2,1)S(1)}, f16[1024,128]{1,0:T(8,128)(2,1)S(1)}, u32[]{:S(2)}, u32[]{:S(2)}) %collective-permute-start.24) | collective-permute-done | bytes 262176 | tf_op jit(solution)/shard_map/ppermute | solution.py:331
  107.7 1.3 %collective-permute-done.25 = f16[1024,128]{1,0:T(8,128)(2,1)S(1)} collective-permute-done((f16[1024,128]{1,0:T(8,128)(2,1)S(1)}, f16[1024,128]{1,0:T(8,128)(2,1)S(1)}, u32[]{:S(2)}, u32[]{:S(2)}) %collective-permute-start.25) | collective-permute-done | bytes 262176 | tf_op jit(solution)/shard_map/ppermute | solution.py:330
  109.0 5.6 %collective-permute-done.23 = f16[1024,128]{1,0:T(8,128)(2,1)S(1)} collective-permute-done((f16[1024,128]{1,0:T(8,128)(2,1)S(1)}, f16[1024,128]{1,0:T(8,128)(2,1)S(1)}, u32[]{:S(2)}, u32[]{:S(2)}) %collective-permute-start.23) | collective-permute-done | bytes 262176 | tf_op jit(solution)/shard_map/ppermute | solution.py:335
  114.7 0.2 fusion.8
  115.0 2.8 %collective-permute-start.27 = (f16[2048,128]{1,0:T(8,128)(2,1)S(1)}, f16[2048,128]{1,0:T(8,128)(2,1)S(1)}, u32[]{:S(2)}, u32[]{:S(2)}) collective-permute-start(f16[2048,128]{1,0:T(8,128)(2,1)S(1)} %pad_maximum_fusion), channel_id=1, source_target_pairs={{0,4},{4,64},{8,12},{12,72},{16,20},{20,80},{24,28},{28,88},{32,36... | collective-permute-start | bytes 1572872 | tf_op jit(solution)/shard_map/ppermute | solution.py:347
  117.8 0.3 multiply_reduce_fusion
  118.1 3.0 %collective-permute-start.30 = (f32[128]{0:T(128)S(1)}, f32[128]{0:T(128)S(1)}, u32[]{:S(2)}, u32[]{:S(2)}) collective-permute-start(f32[128]{0:T(128)S(1)} %multiply_reduce_fusion), channel_id=1, source_target_pairs={{0,196},{4,128},{8,204},{12,136},{16,212},{20,144},{24,220},{28,15... | collective-permute-start | bytes 1544 | tf_op jit(solution)/shard_map/ppermute | solution.py:354
  121.1 0.7 collective-permute-start.28
  121.8 5.3 %collective-permute-done.27 = f16[2048,128]{1,0:T(8,128)(2,1)S(1)} collective-permute-done((f16[2048,128]{1,0:T(8,128)(2,1)S(1)}, f16[2048,128]{1,0:T(8,128)(2,1)S(1)}, u32[]{:S(2)}, u32[]{:S(2)}) %collective-permute-start.27) | collective-permute-done | bytes 524320 | tf_op jit(solution)/shard_map/ppermute | solution.py:347
  127.1 0.3 fusion
  127.4 1.1 multiply_divide_fusion
  (40 shorter events, 1.3 us)
Async XLA Ops:
  0.0 1.6 %copy-start = (bf16[2048,512]{1,0:T(8,128)(2,1)S(1)}, bf16[2048,512]{1,0:T(8,128)(2,1)}, u32[]{:S(2)}) copy-start(bf16[2048,512]{1,0:T(8,128)(2,1)} %values_ref.3) | copy-start | bytes 6291460
  1.6 0.7 copy-start.2
  2.3 25.4 %copy-start.1 = (bf16[2048,512]{1,0:T(8,128)(2,1)S(1)}, bf16[2048,512]{1,0:T(8,128)(2,1)}, u32[]{:S(2)}) copy-start(bf16[2048,512]{1,0:T(8,128)(2,1)} %values_ref.3) | copy-start | bytes 6291460
  2.3 25.4 %copy-start.3 = (s32[16,4]{0,1:T(4,128)S(1)}, s32[16,4]{0,1:T(4,128)}, u32[]{:S(2)}) copy-start(s32[16,4]{0,1:T(4,128)} %param.3) | copy-start | bytes 772
  3.4 20.4 %collective-permute-start = (bf16[1056,128]{1,0:T(8,128)(2,1)S(1)}, bf16[1056,128]{1,0:T(8,128)(2,1)S(1)}, u32[]{:S(2)}, u32[]{:S(2)}) collective-permute-start(bf16[1056,128]{1,0:T(8,128)(2,1)S(1)} %share.1), channel_id=1, source_target_pairs={{0,16},{1,8},{2,0},{3,56},{4,112},{5,72},{6,64},{7,120},{8,1},{9,2... | collective-permute-start | bytes 811016 | tf_op jit(solution)/shard_map/ppermute | solution.py:288
  16.9 6.9 %collective-permute-start.1 = (f32[4,128]{1,0:T(4,128)S(1)}, f32[4,128]{1,0:T(4,128)S(1)}, u32[]{:S(2)}, u32[]{:S(2)}) collective-permute-start(f32[4,128]{1,0:T(4,128)S(1)} %psum.7), channel_id=1, source_target_pairs={{0,16},{1,8},{2,0},{3,56},{4,112},{5,72},{6,64},{7,120},{8,1},{9,2... | collective-permute-start | bytes 6152 | tf_op jit(solution)/shard_map/ppermute | solution.py:289
  23.9 11.7 %collective-permute-start.6 = (bf16[1056,128]{1,0:T(8,128)(2,1)S(1)}, bf16[1056,128]{1,0:T(8,128)(2,1)S(1)}, u32[]{:S(2)}, u32[]{:S(2)}) collective-permute-start(bf16[1056,128]{1,0:T(8,128)(2,1)S(1)} %scale.1.refs_0_), channel_id=1, source_target_pairs={{0,56},{4,60},{8,0},{12,4},{16,8},{20,12},{24,16},{28,20},{32,24},... | collective-permute-start | bytes 811016 | tf_op jit(solution)/shard_map/ppermute | solution.py:304
  28.7 33.4 %collective-permute-start.14 = (bf16[1024,512]{1,0:T(8,128)(2,1)S(1)}, bf16[1024,512]{1,0:T(8,128)(2,1)S(1)}, u32[]{:S(2)}, u32[]{:S(2)}) collective-permute-start(bf16[1024,512]{1,0:T(8,128)(2,1)S(1)} %get-tuple-element.9), channel_id=1, source_target_pairs={{0,4},{1,128},{2,64},{3,196},{4,0},{5,132},{6,68},{7,192},{8,12},{... | collective-permute-start | bytes 3145736 | tf_op jit(solution)/shard_map/ppermute | solution.py:318
  30.8 32.5 %collective-permute-start.15 = (bf16[1024,512]{1,0:T(8,128)(2,1)S(1)}, bf16[1024,512]{1,0:T(8,128)(2,1)S(1)}, u32[]{:S(2)}, u32[]{:S(2)}) collective-permute-start(bf16[1024,512]{1,0:T(8,128)(2,1)S(1)} %get-tuple-element.10), channel_id=1, source_target_pairs={{0,197},{1,5},{2,129},{3,65},{4,193},{5,1},{6,133},{7,69},{8,205},... | collective-permute-start | bytes 3145736 | tf_op jit(solution)/shard_map/ppermute | solution.py:318
  34.3 9.0 %collective-permute-start.2 = (bf16[1056,128]{1,0:T(8,128)(2,1)S(1)}, bf16[1056,128]{1,0:T(8,128)(2,1)S(1)}, u32[]{:S(2)}, u32[]{:S(2)}) collective-permute-start(bf16[1056,128]{1,0:T(8,128)(2,1)S(1)} %scale.1.refs_0_), channel_id=1, source_target_pairs={{0,8},{4,12},{8,16},{12,20},{16,24},{20,28},{24,32},{28,36},{32,40... | collective-permute-start | bytes 811016 | tf_op jit(solution)/shard_map/ppermute | solution.py:303
  34.3 9.0 %collective-permute-start.16 = (bf16[1056,128]{1,0:T(8,128)(2,1)S(1)}, bf16[1056,128]{1,0:T(8,128)(2,1)S(1)}, u32[]{:S(2)}, u32[]{:S(2)}) collective-permute-start(bf16[1056,128]{1,0:T(8,128)(2,1)S(1)} %scale.1.refs_0_), channel_id=1, source_target_pairs={{0,64},{64,0},{128,192},{192,128},{1,65},{65,1},{129,193},{193,129... | collective-permute-start | bytes 811016 | tf_op jit(solution)/shard_map/ppermute | solution.py:306
  35.6 8.9 %collective-permute-start.7 = (bf16[1056,128]{1,0:T(8,128)(2,1)S(1)}, bf16[1056,128]{1,0:T(8,128)(2,1)S(1)}, u32[]{:S(2)}, u32[]{:S(2)}) collective-permute-start(bf16[1056,128]{1,0:T(8,128)(2,1)S(1)} %collective-permute-done.6.refs_4_), channel_id=1, source_target_pairs={{0,56},{4,60},{8,0},{12,4},{16,8},{20,12},{24,16},{28,20},{32,24},... | collective-permute-start | bytes 811016 | tf_op jit(solution)/shard_map/ppermute | solution.py:304
  43.3 8.1 %collective-permute-start.3 = (bf16[1056,128]{1,0:T(8,128)(2,1)S(1)}, bf16[1056,128]{1,0:T(8,128)(2,1)S(1)}, u32[]{:S(2)}, u32[]{:S(2)}) collective-permute-start(bf16[1056,128]{1,0:T(8,128)(2,1)S(1)} %collective-permute-done.2.refs_2_), channel_id=1, source_target_pairs={{0,8},{4,12},{8,16},{12,20},{16,24},{20,28},{24,32},{28,36},{32,40... | collective-permute-start | bytes 811016 | tf_op jit(solution)/shard_map/ppermute | solution.py:303
  43.3 8.1 %collective-permute-start.18 = (bf16[1056,128]{1,0:T(8,128)(2,1)S(1)}, bf16[1056,128]{1,0:T(8,128)(2,1)S(1)}, u32[]{:S(2)}, u32[]{:S(2)}) collective-permute-start(bf16[1056,128]{1,0:T(8,128)(2,1)S(1)} %collective-permute-done.6.refs_4_), channel_id=1, source_target_pairs={{0,64},{64,0},{128,192},{192,128},{1,65},{65,1},{129,193},{193,129... | collective-permute-start | bytes 811016 | tf_op jit(solution)/shard_map/ppermute | solution.py:306
  44.4 9.0 %collective-permute-start.8 = (bf16[1056,128]{1,0:T(8,128)(2,1)S(1)}, bf16[1056,128]{1,0:T(8,128)(2,1)S(1)}, u32[]{:S(2)}, u32[]{:S(2)}) collective-permute-start(bf16[1056,128]{1,0:T(8,128)(2,1)S(1)} %collective-permute-done.7.refs_8_), channel_id=1, source_target_pairs={{0,56},{4,60},{8,0},{12,4},{16,8},{20,12},{24,16},{28,20},{32,24},... | collective-permute-start | bytes 811016 | tf_op jit(solution)/shard_map/ppermute | solution.py:304
  51.5 7.3 %collective-permute-start.4 = (bf16[1056,128]{1,0:T(8,128)(2,1)S(1)}, bf16[1056,128]{1,0:T(8,128)(2,1)S(1)}, u32[]{:S(2)}, u32[]{:S(2)}) collective-permute-start(bf16[1056,128]{1,0:T(8,128)(2,1)S(1)} %collective-permute-done.3.refs_6_), channel_id=1, source_target_pairs={{0,8},{4,12},{8,16},{12,20},{16,24},{20,28},{24,32},{28,36},{32,40... | collective-permute-start | bytes 811016 | tf_op jit(solution)/shard_map/ppermute | solution.py:303
  51.5 10.1 %collective-permute-start.17 = (bf16[1056,128]{1,0:T(8,128)(2,1)S(1)}, bf16[1056,128]{1,0:T(8,128)(2,1)S(1)}, u32[]{:S(2)}, u32[]{:S(2)}) collective-permute-start(bf16[1056,128]{1,0:T(8,128)(2,1)S(1)} %collective-permute-done.2.refs_2_), channel_id=1, source_target_pairs={{0,64},{64,0},{128,192},{192,128},{1,65},{65,1},{129,193},{193,129... | collective-permute-start | bytes 811016 | tf_op jit(solution)/shard_map/ppermute | solution.py:306
  53.4 10.5 %collective-permute-start.20 = (bf16[1056,128]{1,0:T(8,128)(2,1)S(1)}, bf16[1056,128]{1,0:T(8,128)(2,1)S(1)}, u32[]{:S(2)}, u32[]{:S(2)}) collective-permute-start(bf16[1056,128]{1,0:T(8,128)(2,1)S(1)} %collective-permute-done.7.refs_8_), channel_id=1, source_target_pairs={{0,64},{64,0},{128,192},{192,128},{1,65},{65,1},{129,193},{193,129... | collective-permute-start | bytes 811016 | tf_op jit(solution)/shard_map/ppermute | solution.py:306
  58.8 10.5 %collective-permute-start.19 = (bf16[1056,128]{1,0:T(8,128)(2,1)S(1)}, bf16[1056,128]{1,0:T(8,128)(2,1)S(1)}, u32[]{:S(2)}, u32[]{:S(2)}) collective-permute-start(bf16[1056,128]{1,0:T(8,128)(2,1)S(1)} %collective-permute-done.3.refs_6_), channel_id=1, source_target_pairs={{0,64},{64,0},{128,192},{192,128},{1,65},{65,1},{129,193},{193,129... | collective-permute-start | bytes 811016 | tf_op jit(solution)/shard_map/ppermute | solution.py:306
  61.6 5.4 %collective-permute-start.12 = (bf16[528,128]{1,0:T(8,128)(2,1)S(1)}, bf16[528,128]{1,0:T(8,128)(2,1)S(1)}, u32[]{:S(2)}, u32[]{:S(2)}) collective-permute-start(bf16[528,128]{1,0:T(8,128)(2,1)S(1)} %slice.46), channel_id=1, source_target_pairs={{0,56},{4,60},{8,0},{12,4},{16,8},{20,12},{24,16},{28,20},{32,24},... | collective-permute-start | bytes 405512 | tf_op jit(solution)/shard_map/ppermute | solution.py:304
  62.1 6.5 %collective-permute-start.10 = (bf16[528,128]{1,0:T(8,128)(2,1)S(1)}, bf16[528,128]{1,0:T(8,128)(2,1)S(1)}, u32[]{:S(2)}, u32[]{:S(2)}) collective-permute-start(bf16[528,128]{1,0:T(8,128)(2,1)S(1)} %slice.45), channel_id=1, source_target_pairs={{0,8},{4,12},{8,16},{12,20},{16,24},{20,28},{24,32},{28,36},{32,40... | collective-permute-start | bytes 405512 | tf_op jit(solution)/shard_map/ppermute | solution.py:303
  63.4 24.1 %collective-permute-start.9 = (bf16[1056,128]{1,0:T(8,128)(2,1)S(1)}, bf16[1056,128]{1,0:T(8,128)(2,1)S(1)}, u32[]{:S(2)}, u32[]{:S(2)}) collective-permute-start(bf16[1056,128]{1,0:T(8,128)(2,1)S(1)} %collective-permute-done.8.refs_2_), channel_id=1, source_target_pairs={{0,64},{64,0},{128,192},{192,128},{1,65},{65,1},{129,193},{193,129... | collective-permute-start | bytes 811016 | tf_op jit(solution)/shard_map/ppermute | solution.py:306
  63.9 23.5 %collective-permute-start.5 = (bf16[1056,128]{1,0:T(8,128)(2,1)S(1)}, bf16[1056,128]{1,0:T(8,128)(2,1)S(1)}, u32[]{:S(2)}, u32[]{:S(2)}) collective-permute-start(bf16[1056,128]{1,0:T(8,128)(2,1)S(1)} %collective-permute-done.4.refs_0_), channel_id=1, source_target_pairs={{0,64},{64,0},{128,192},{192,128},{1,65},{65,1},{129,193},{193,129... | collective-permute-start | bytes 811016 | tf_op jit(solution)/shard_map/ppermute | solution.py:306
  67.0 20.4 %collective-permute-start.13 = (bf16[528,128]{1,0:T(8,128)(2,1)S(1)}, bf16[528,128]{1,0:T(8,128)(2,1)S(1)}, u32[]{:S(2)}, u32[]{:S(2)}) collective-permute-start(bf16[528,128]{1,0:T(8,128)(2,1)S(1)} %collective-permute-done.12.refs_6_), channel_id=1, source_target_pairs={{0,64},{64,0},{128,192},{192,128},{1,65},{65,1},{129,193},{193,129... | collective-permute-start | bytes 405512 | tf_op jit(solution)/shard_map/ppermute | solution.py:306
  68.5 18.9 %collective-permute-start.11 = (bf16[528,128]{1,0:T(8,128)(2,1)S(1)}, bf16[528,128]{1,0:T(8,128)(2,1)S(1)}, u32[]{:S(2)}, u32[]{:S(2)}) collective-permute-start(bf16[528,128]{1,0:T(8,128)(2,1)S(1)} %collective-permute-done.10.refs_4_), channel_id=1, source_target_pairs={{0,64},{64,0},{128,192},{192,128},{1,65},{65,1},{129,193},{193,129... | collective-permute-start | bytes 405512 | tf_op jit(solution)/shard_map/ppermute | solution.py:306
  94.2 7.9 %collective-permute-start.22 = (f16[1024,128]{1,0:T(8,128)(2,1)S(1)}, f16[1024,128]{1,0:T(8,128)(2,1)S(1)}, u32[]{:S(2)}, u32[]{:S(2)}) collective-permute-start(f16[1024,128]{1,0:T(8,128)(2,1)S(1)} %get-tuple-element.19), channel_id=1, source_target_pairs={{0,3},{1,0},{2,1},{3,2},{4,7},{5,4},{6,5},{7,6},{8,11},{9,8},{10,9... | collective-permute-start | bytes 786440 | tf_op jit(solution)/shard_map/ppermute | solution.py:329
  94.3 9.1 %collective-permute-start.21 = (f16[1024,128]{1,0:T(8,128)(2,1)S(1)}, f16[1024,128]{1,0:T(8,128)(2,1)S(1)}, u32[]{:S(2)}, u32[]{:S(2)}) collective-permute-start(f16[1024,128]{1,0:T(8,128)(2,1)S(1)} %get-tuple-element.20), channel_id=1, source_target_pairs={{0,1},{1,2},{2,3},{3,0},{4,5},{5,6},{6,7},{7,4},{8,9},{9,10},{10,1... | collective-permute-start | bytes 786440 | tf_op jit(solution)/shard_map/ppermute | solution.py:328
  95.8 12.0 %collective-permute-start.24 = (f16[1024,128]{1,0:T(8,128)(2,1)S(1)}, f16[1024,128]{1,0:T(8,128)(2,1)S(1)}, u32[]{:S(2)}, u32[]{:S(2)}) collective-permute-start(f16[1024,128]{1,0:T(8,128)(2,1)S(1)} %get-tuple-element.17), channel_id=1, source_target_pairs={{0,3},{1,0},{2,1},{3,2},{4,7},{5,4},{6,5},{7,6},{8,11},{9,8},{10,9... | collective-permute-start | bytes 786440 | tf_op jit(solution)/shard_map/ppermute | solution.py:331
  97.1 12.0 %collective-permute-start.25 = (f16[1024,128]{1,0:T(8,128)(2,1)S(1)}, f16[1024,128]{1,0:T(8,128)(2,1)S(1)}, u32[]{:S(2)}, u32[]{:S(2)}) collective-permute-start(f16[1024,128]{1,0:T(8,128)(2,1)S(1)} %get-tuple-element.18), channel_id=1, source_target_pairs={{0,1},{1,2},{2,3},{3,0},{4,5},{5,6},{6,7},{7,4},{8,9},{9,10},{10,1... | collective-permute-start | bytes 786440 | tf_op jit(solution)/shard_map/ppermute | solution.py:330
  103.6 11.1 %collective-permute-start.23 = (f16[1024,128]{1,0:T(8,128)(2,1)S(1)}, f16[1024,128]{1,0:T(8,128)(2,1)S(1)}, u32[]{:S(2)}, u32[]{:S(2)}) collective-permute-start(f16[1024,128]{1,0:T(8,128)(2,1)S(1)} %get-tuple-element.11), channel_id=1, source_target_pairs={{0,1},{1,2},{2,3},{3,0},{4,5},{5,6},{6,7},{7,4},{8,9},{9,10},{10,1... | collective-permute-start | bytes 786440 | tf_op jit(solution)/shard_map/ppermute | solution.py:335
  103.7 11.0 %collective-permute-start.26 = (f16[1024,128]{1,0:T(8,128)(2,1)S(1)}, f16[1024,128]{1,0:T(8,128)(2,1)S(1)}, u32[]{:S(2)}, u32[]{:S(2)}) collective-permute-start(f16[1024,128]{1,0:T(8,128)(2,1)S(1)} %get-tuple-element.12), channel_id=1, source_target_pairs={{0,3},{1,0},{2,1},{3,2},{4,7},{5,4},{6,5},{7,6},{8,11},{9,8},{10,9... | collective-permute-start | bytes 786440 | tf_op jit(solution)/shard_map/ppermute | solution.py:336
  115.0 12.0 %collective-permute-start.27 = (f16[2048,128]{1,0:T(8,128)(2,1)S(1)}, f16[2048,128]{1,0:T(8,128)(2,1)S(1)}, u32[]{:S(2)}, u32[]{:S(2)}) collective-permute-start(f16[2048,128]{1,0:T(8,128)(2,1)S(1)} %pad_maximum_fusion), channel_id=1, source_target_pairs={{0,4},{4,64},{8,12},{12,72},{16,20},{20,80},{24,28},{28,88},{32,36... | collective-permute-start | bytes 1572872 | tf_op jit(solution)/shard_map/ppermute | solution.py:347
  118.1 9.2 %collective-permute-start.30 = (f32[128]{0:T(128)S(1)}, f32[128]{0:T(128)S(1)}, u32[]{:S(2)}, u32[]{:S(2)}) collective-permute-start(f32[128]{0:T(128)S(1)} %multiply_reduce_fusion), channel_id=1, source_target_pairs={{0,196},{4,128},{8,204},{12,136},{16,212},{20,144},{24,220},{28,15... | collective-permute-start | bytes 1544 | tf_op jit(solution)/shard_map/ppermute | solution.py:354
  121.1 6.2 %collective-permute-start.29 = (f32[128]{0:T(128)S(1)}, f32[128]{0:T(128)S(1)}, u32[]{:S(2)}, u32[]{:S(2)}) collective-permute-start(f32[128]{0:T(128)S(1)} %multiply_reduce_fusion), channel_id=1, source_target_pairs={{0,132},{4,192},{8,140},{12,200},{16,148},{20,208},{24,156},{28,21... | collective-permute-start | bytes 1544 | tf_op jit(solution)/shard_map/ppermute | solution.py:354
  121.1 6.2 %collective-permute-start.28 = (f32[128]{0:T(128)S(1)}, f32[128]{0:T(128)S(1)}, u32[]{:S(2)}, u32[]{:S(2)}) collective-permute-start(f32[128]{0:T(128)S(1)} %multiply_reduce_fusion), channel_id=1, source_target_pairs={{0,68},{4,0},{8,76},{12,8},{16,84},{20,16},{24,92},{28,24},{32,100... | collective-permute-start | bytes 1544 | tf_op jit(solution)/shard_map/ppermute | solution.py:354

commit v2 on v1

--- a/solution.py
+++ b/solution.py
@@ -179,14 +179,13 @@
 
 def product_kernel(n_parts, counts, per, again, *refs):
     part_refs = refs[:n_parts]
-    right_refs = refs[n_parts:2 + n_parts]
-    out_ref = refs[2 + n_parts + again]
-    spots, table, sem = refs[3 + n_parts + again:]
+    right_ref = refs[n_parts]
+    out_ref = refs[1 + n_parts + again]
+    spots, table, sem = refs[2 + n_parts + again:]
     layer = lax.axis_index("layer")
     n_layer, rows, _ = out_ref.shape
-    depth = right_refs[0].shape[0]
-    kt = 2 * depth // T
-    dead = rows // T * kt
+    kt = right_ref.shape[0] // T
+    chunks = [lax.rem(g + n_layer - layer, n_layer) for g in range(n_layer)]
     size = HEAD + per * T
 
     lane = lax.broadcasted_iota(jnp.int32, (8, T), 1)
@@ -209,46 +208,38 @@
     copy.wait()
     q = 0
     for ref, count in zip(part_refs, counts, strict=True):
-        def add(s, _, ref=ref, q=q):
-            h, j = lax.div(s, per), lax.rem(s, per)
-            t = table[j, q + h]
-            tile = pl.ds(pl.multiple_of(h * size + HEAD + j * T, HEAD), T)
-            k = lax.rem(t, kt)
-            at = pl.ds(pl.multiple_of(lax.div(t, kt) * T, T), T)
-            rows_of = pl.ds(pl.multiple_of(lax.rem(k, kt // 2) * T, T), T)
-            for m, right_ref in enumerate(right_refs):
-                @pl.when((t < dead) & (lax.div(k, kt // 2) == m))
-                def _():
-                    out = jnp.dot(ref[tile, :], right_ref[rows_of, :], preferred_element_type=jnp.float32)
-                    for g in range(n_layer):
-                        chunk = lax.rem(g + n_layer - layer, n_layer)
-                        out_ref[chunk, at, :] += out[:, g * T:(g + 1) * T]
-            return 0
-
-        lax.fori_loop(0, count * per, add, 0)
-        q += count
-
-
-def product(parts, counts, per, rights, rows, n_layer, total=None):
+        for h in range(count):
+            for j in range(per):
+                t = table[j, q]
+                at = pl.ds(pl.multiple_of(lax.div(t, kt) * T, T), T)
+                rows_of = pl.ds(pl.multiple_of(lax.rem(t, kt) * T, T), T)
+                tile = ref[h * size + HEAD + j * T:h * size + HEAD + (j + 1) * T, :]
+                out = jnp.dot(tile, right_ref[rows_of, :], preferred_element_type=jnp.float32)
+                for g, chunk in enumerate(chunks):
+                    out_ref[chunk, at, :] += out[:, g * T:(g + 1) * T]
+            q += 1
+
+
+def product(parts, counts, per, right, rows, n_layer, total=None):
     n_parts = len(parts)
-    width = rights[0].shape[1]
+    width = right.shape[1]
     again = total is not None
     tiles = sum(counts) * per
     return pl.pallas_call(
         functools.partial(product_kernel, n_parts, counts, per, again),
-        out_shape=pltpu.VMEM((n_layer, rows, width // n_layer), jnp.float32),
-        in_specs=[VMEM] * (n_parts + 2 + again),
+        out_shape=pltpu.VMEM((n_layer, rows + T, width // n_layer), jnp.float32),
+        in_specs=[VMEM] * (n_parts + 1 + again),
         out_specs=VMEM,
         scratch_shapes=[
             pltpu.VMEM((8, T), jnp.int32),
             pltpu.SMEM((8, T), jnp.int32),
             pltpu.SemaphoreType.DMA,
         ],
-        input_output_aliases={n_parts + 2: 0} if again else {},
+        input_output_aliases={n_parts + 1: 0} if again else {},
         cost_estimate=pl.CostEstimate(flops=2 * tiles * T * T * width, bytes_accessed=2**20, transcendentals=0),
         compiler_params=pltpu.CompilerParams(vmem_limit_bytes=GRANT),
         name="add_product" if again else "product",
-    )(*parts, *rights, *((total,) if again else ()))
+    )(*parts, right, *((total,) if again else ()))
 
 
 def coords(sizes):
@@ -276,7 +267,8 @@
     f16, f32 = jnp.float16, jnp.float32
 
     mask = tile_mask.T
-    raw = share(mask, values, per, halves, depth // T)
+    hbm = functools.partial(pltpu.with_memory_space_constraint, memory_space=pltpu.HBM)
+    raw = share(hbm(mask), hbm(values), per, halves, depth // T)
 
     spread = {}
     for r, c, y in coords(sizes):
@@ -316,27 +308,28 @@
             to = (lo_to * 2 + (hi ^ hi_to ^ lo_to ^ 1), zz * 2 + hi_to, y_to)
             perm.append((flat(r, c, y, sizes), flat(*to, sizes)))
         rights[m] = lax.ppermute(rights[m], axes, perm)
+    right = jnp.concatenate(rights)
     early = [p for pair in parts[:2 * last - 3] for p in pair]
     late = [p for pair in parts[2 * last - 3:] for p in pair]
-    out = product(early, [p.shape[0] // half for p in early], per, rights, height, n_layer)
-    out = product(late, [p.shape[0] // half for p in late], per, rights, height, n_layer, out)
+    out = product(early, [p.shape[0] // half for p in early], per, right, height, n_layer)
+    out = product(late, [p.shape[0] // half for p in late], per, right, height, n_layer, out)
 
     up = [(y, (y + 1) % n_layer) for y in range(n_layer)]
     down = [(y, (y - 1) % n_layer) for y in range(n_layer)]
     mid = height // 2
-    send = lax.optimization_barrier(out[1:].astype(f16))
+    send = lax.optimization_barrier(out[1:, :height].astype(f16))
     far_a = lax.ppermute(send[1, :mid], "layer", up)
     far_b = lax.ppermute(send[1, mid:], "layer", down)
     up_b = lax.ppermute(send[0, mid:], "layer", up)
     down_a = lax.ppermute(send[2, :mid], "layer", down)
     up_a = (out[1, :mid] + far_a.astype(f32)).astype(f16)
-    down_b = (out[3, mid:] + far_b.astype(f32)).astype(f16)
+    down_b = (out[3, mid:height] + far_b.astype(f32)).astype(f16)
     up_a, down_b = lax.optimization_barrier((up_a, down_b))
     up_a = lax.ppermute(up_a, "layer", up)
     down_b = lax.ppermute(down_b, "layer", down)
     total = jnp.concatenate([
         out[0, :mid] + (up_a.astype(f32) + down_a.astype(f32)),
-        out[0, mid:] + (up_b.astype(f32) + down_b.astype(f32)),
+        out[0, mid:height] + (up_b.astype(f32) + down_b.astype(f32)),
     ]).astype(f16)
 
     owner = {}
@@ -348,13 +341,14 @@
         total, ("row", "col"), [(r * n_col + c, o[0] * n_col + o[1]) for (r, c), o in owner.items()])
     summand = total.astype(f32)
     summand = jnp.sum(summand * summand, axis=0)
-    weights = []
-    for k in range(1, n_row):
-        perm = [(r * n_col + c, (o[0] ^ k) * n_col + o[1]) for (r, c), o in owner.items()]
-        weights.append(lax.ppermute(summand, ("row", "col"), perm))
+    row, x_hi = lax.axis_index("row"), lax.axis_index("col") % 2
+    which = (row % 2) ^ x_hi ^ (row // 2) ^ 1
+    pair = jnp.where(lax.broadcasted_iota(jnp.int32, (2, T), 0) == which, summand, 0.0)
+    pair = lax.psum(pair, "row")
+    pair = pair + lax.ppermute(pair, "col", [(c, c ^ 1) for c in range(n_col)])
+    weight = jnp.where(x_hi == 0, pair[0], pair[1])
     expanded = expanded.astype(f32)
     inflated = expanded * expanded
-    weight = jnp.sum(inflated, axis=0) + (weights[0] + (weights[1] + weights[2]))
     order = height * n_row
     return order * 1.0 * inflated / weight[None, :]
 

time: 129 us -> 117 us (0.907)
  Pallas kernels: 27.6 us -> 10.8 us
  blocking collectives: 5.76 us -> 18 us
  waiting for transfers between devices: 39.9 us -> 31.2 us
  starting transfers between devices: 50.1 us -> 52.3 us
  local copies, waits for them, and re-layouts: 2.51 us -> 0.38 us
    pallas_call x2, Pallas kernels: 24.4 us -> 6.83 us  [product(): pl.pallas_call(functools.partial(product_kernel, n_parts, counts, per, ag...]
    psum x0 -> x1, blocking collectives: none -> 12.2 us  [shards(): pair = lax.psum(pair, 'row')]
    ppermute x4, waiting for transfers between devices: 15.2 us -> 3.44 us  [shards(): up = lax.ppermute(up, 'col', ring(1))]
    ppermute x2, waiting for transfers between devices: 0.2 us -> 5.5 us  [shards(): rights[m] = lax.ppermute(rights[m], axes, perm)]
    ppermute x1, waiting for transfers between devices: 5.28 us -> 0.01 us  [shards(): lax.ppermute(total, ('row', 'col'), [(r * n_col + c, o[0] * n_col + o[1])...]
    ppermute x1, waiting for transfers between devices: 4.91 us -> 0.01 us  [shards(): far_b = lax.ppermute(send[1, mid:], 'layer', down)]
    ppermute x3 -> x1, waiting for transfers between devices: 0.01 us -> 3.78 us  [shards(): pair = pair + lax.ppermute(pair, 'col', [(c, c ^ 1) for c in range(n_col)])]
    ppermute x3 -> x1, starting transfers between devices: 3.65 us -> 0.22 us  [shards(): pair = pair + lax.ppermute(pair, 'col', [(c, c ^ 1) for c in range(n_col)])]
  transfers between devices with their start and end apart: 31 -> 29, of which waited for: 13 -> 11; matrix products, arithmetic and copies ran while one was open for 1% -> 1% of each run, Pallas kernels for 16% -> 5%
where the time goes in v2:
time: 117 us; the launch traced here: 116 us
  starting transfers between devices  52.3 us (45%)
  waiting for transfers between devices  31.2 us (27%)
  blocking collectives  18 us (15%)
  Pallas kernels  10.8 us (9%)
  other arithmetic  3.41 us (3%)
    psum x1, blocking collectives, shards(): pair = lax.psum(pair, 'row')  12.2 us
    ppermute x4, starting transfers between devices, shards(): down = lax.ppermute(down, 'col', ring(-1))  11.2 us
    ppermute x9, starting transfers between devices, shards(): parts = [(p, lax.ppermute(p, 'row', swap)) for p in mine]  10.9 us
    ppermute x1, starting transfers between devices, shards(): raw = lax.ppermute(raw, axes, table)  6.83 us
    pallas_call x2, Pallas kernels, product(): pl.pallas_call(functools.partial(product_kernel, n_parts, counts, per, ag...  6.83 us
    ppermute x2, starting transfers between devices, shards(): rights[m] = lax.ppermute(rights[m], axes, perm)  6.09 us
    psum x1, blocking collectives, shards(): mass = lax.ppermute(lax.psum(column_sums(mask, values), 'row'), axes, table)  5.76 us
    ppermute x1, waiting for transfers between devices, shards(): up_a = lax.ppermute(up_a, 'layer', up)  5.62 us
  transfers between devices with their start and end apart: 29, of which 11 were waited for; matrix products, arithmetic and copies ran while one was open for 1% of the time, Pallas kernels for 5%

profile of v2, /device:TPU:1, one launch (start us, length us, event | category | flops | bytes accessed | tf_op | source)
XLA Modules:
  0.0 116.4 jit_solution(4487422396104039900)
XLA Ops:
  0.0 2.0 %share.1 = bf16[1056,128]{1,0:T(8,128)(2,1)S(1)} custom-call(s32[4,16]{1,0:T(4,128)} %bitcast.35, bf16[2048,512]{1,0:T(8,128)(2,1)} %values_ref.3), custom_call_target="tpu_custom_call" | custom-call | flops 1048576 | bytes 2097152 | tf_op jit(solution)/shard_map/share/pallas_call | solution.py:75
  2.0 6.8 %collective-permute-start = (bf16[1056,128]{1,0:T(8,128)(2,1)S(1)}, bf16[1056,128]{1,0:T(8,128)(2,1)S(1)}, u32[]{:S(2)}, u32[]{:S(2)}) collective-permute-start(bf16[1056,128]{1,0:T(8,128)(2,1)S(1)} %share.1), channel_id=1, source_target_pairs={{0,16},{1,8},{2,0},{3,56},{4,112},{5,72},{6,64},{7,120},{8,1},{9,2... | collective-permute-start | bytes 811016 | tf_op jit(solution)/shard_map/ppermute | solution.py:280
  8.8 0.9 column_sums.1
  9.7 5.8 %psum.14 = f32[4,128]{1,0:T(4,128)S(1)} all-reduce(f32[4,128]{1,0:T(4,128)S(1)} %column_sums.1), channel_id=1, replica_groups=mesh['row'=4,'col'=16,'layer'=4] {'row'}, use_global_device_ids=true, to_apply=%region_0.0 | all-reduce | flops 512 | bytes 4096 | tf_op jit(solution)/shard_map/psum | solution.py:281
  15.5 4.0 %collective-permute-start.1 = (f32[4,128]{1,0:T(4,128)S(1)}, f32[4,128]{1,0:T(4,128)S(1)}, u32[]{:S(2)}, u32[]{:S(2)}) collective-permute-start(f32[4,128]{1,0:T(4,128)S(1)} %psum.14), channel_id=1, source_target_pairs={{0,16},{1,8},{2,0},{3,56},{4,112},{5,72},{6,64},{7,120},{8,1},{9,2... | collective-permute-start | bytes 6152 | tf_op jit(solution)/shard_map/ppermute | solution.py:281
  19.5 2.9 %collective-permute-done.1.mass_ref = f32[4,128]{1,0:T(4,128)S(1)} collective-permute-done((f32[4,128]{1,0:T(4,128)S(1)}, f32[4,128]{1,0:T(4,128)S(1)}, u32[]{:S(2)}, u32[]{:S(2)}) %collective-permute-start.1) | collective-permute-done | bytes 2080 | tf_op jit(solution)/shard_map/ppermute | solution.py:281
  22.5 0.1 collective-permute-start.2
  22.6 3.8 %collective-permute-start.6 = (bf16[1056,128]{1,0:T(8,128)(2,1)S(1)}, bf16[1056,128]{1,0:T(8,128)(2,1)S(1)}, u32[]{:S(2)}, u32[]{:S(2)}) collective-permute-start(bf16[1056,128]{1,0:T(8,128)(2,1)S(1)} %scale.1.refs_0_), channel_id=1, source_target_pairs={{0,56},{4,60},{8,0},{12,4},{16,8},{20,12},{24,16},{28,20},{32,24},... | collective-permute-start | bytes 811016 | tf_op jit(solution)/shard_map/ppermute | solution.py:296
  26.3 1.1 masked_halves.1
  27.4 1.5 %collective-permute-start.14 = (bf16[1024,512]{1,0:T(8,128)(2,1)S(1)}, bf16[1024,512]{1,0:T(8,128)(2,1)S(1)}, u32[]{:S(2)}, u32[]{:S(2)}) collective-permute-start(bf16[1024,512]{1,0:T(8,128)(2,1)S(1)} %get-tuple-element.9), channel_id=1, source_target_pairs={{0,4},{1,128},{2,64},{3,196},{4,0},{5,132},{6,68},{7,192},{8,12},{... | collective-permute-start | bytes 3145736 | tf_op jit(solution)/shard_map/ppermute | solution.py:310
  28.9 4.6 %collective-permute-start.15 = (bf16[1024,512]{1,0:T(8,128)(2,1)S(1)}, bf16[1024,512]{1,0:T(8,128)(2,1)S(1)}, u32[]{:S(2)}, u32[]{:S(2)}) collective-permute-start(bf16[1024,512]{1,0:T(8,128)(2,1)S(1)} %get-tuple-element.10), channel_id=1, source_target_pairs={{0,197},{1,5},{2,129},{3,65},{4,193},{5,1},{6,133},{7,69},{8,205},... | collective-permute-start | bytes 3145736 | tf_op jit(solution)/shard_map/ppermute | solution.py:310
  33.5 2.7 %collective-permute-start.7 = (bf16[1056,128]{1,0:T(8,128)(2,1)S(1)}, bf16[1056,128]{1,0:T(8,128)(2,1)S(1)}, u32[]{:S(2)}, u32[]{:S(2)}) collective-permute-start(bf16[1056,128]{1,0:T(8,128)(2,1)S(1)} %collective-permute-done.6.refs_4_), channel_id=1, source_target_pairs={{0,56},{4,60},{8,0},{12,4},{16,8},{20,12},{24,16},{28,20},{32,24},... | collective-permute-start | bytes 811016 | tf_op jit(solution)/shard_map/ppermute | solution.py:296
  36.2 2.4 %collective-permute-start.16 = (bf16[1056,128]{1,0:T(8,128)(2,1)S(1)}, bf16[1056,128]{1,0:T(8,128)(2,1)S(1)}, u32[]{:S(2)}, u32[]{:S(2)}) collective-permute-start(bf16[1056,128]{1,0:T(8,128)(2,1)S(1)} %scale.1.refs_0_), channel_id=1, source_target_pairs={{0,64},{64,0},{128,192},{192,128},{1,65},{65,1},{129,193},{193,129... | collective-permute-start | bytes 811016 | tf_op jit(solution)/shard_map/ppermute | solution.py:298
  38.6 2.3 %collective-permute-done.3.refs_6_ = bf16[1056,128]{1,0:T(8,128)(2,1)S(1)} collective-permute-done((bf16[1056,128]{1,0:T(8,128)(2,1)S(1)}, bf16[1056,128]{1,0:T(8,128)(2,1)S(1)}, u32[]{:S(2)}, u32[]{:S(2)}) %collective-permute-start.3) | collective-permute-done | bytes 270368 | tf_op jit(solution)/shard_map/ppermute | solution.py:295
  40.9 1.3 %collective-permute-start.4 = (bf16[1056,128]{1,0:T(8,128)(2,1)S(1)}, bf16[1056,128]{1,0:T(8,128)(2,1)S(1)}, u32[]{:S(2)}, u32[]{:S(2)}) collective-permute-start(bf16[1056,128]{1,0:T(8,128)(2,1)S(1)} %collective-permute-done.3.refs_6_), channel_id=1, source_target_pairs={{0,8},{4,12},{8,16},{12,20},{16,24},{20,28},{24,32},{28,36},{32,40... | collective-permute-start | bytes 811016 | tf_op jit(solution)/shard_map/ppermute | solution.py:295
  42.2 1.6 %collective-permute-done.7.refs_8_ = bf16[1056,128]{1,0:T(8,128)(2,1)S(1)} collective-permute-done((bf16[1056,128]{1,0:T(8,128)(2,1)S(1)}, bf16[1056,128]{1,0:T(8,128)(2,1)S(1)}, u32[]{:S(2)}, u32[]{:S(2)}) %collective-permute-start.7) | collective-permute-done | bytes 270368 | tf_op jit(solution)/shard_map/ppermute | solution.py:296
  43.8 3.0 %collective-permute-start.17 = (bf16[1056,128]{1,0:T(8,128)(2,1)S(1)}, bf16[1056,128]{1,0:T(8,128)(2,1)S(1)}, u32[]{:S(2)}, u32[]{:S(2)}) collective-permute-start(bf16[1056,128]{1,0:T(8,128)(2,1)S(1)} %collective-permute-done.2.refs_2_), channel_id=1, source_target_pairs={{0,64},{64,0},{128,192},{192,128},{1,65},{65,1},{129,193},{193,129... | collective-permute-start | bytes 811016 | tf_op jit(solution)/shard_map/ppermute | solution.py:298
  46.9 1.1 collective-permute-done.4.refs_0_
  48.0 3.3 %collective-permute-start.18 = (bf16[1056,128]{1,0:T(8,128)(2,1)S(1)}, bf16[1056,128]{1,0:T(8,128)(2,1)S(1)}, u32[]{:S(2)}, u32[]{:S(2)}) collective-permute-start(bf16[1056,128]{1,0:T(8,128)(2,1)S(1)} %collective-permute-done.6.refs_4_), channel_id=1, source_target_pairs={{0,64},{64,0},{128,192},{192,128},{1,65},{65,1},{129,193},{193,129... | collective-permute-start | bytes 811016 | tf_op jit(solution)/shard_map/ppermute | solution.py:298
  51.3 1.4 %collective-permute-start.19 = (bf16[1056,128]{1,0:T(8,128)(2,1)S(1)}, bf16[1056,128]{1,0:T(8,128)(2,1)S(1)}, u32[]{:S(2)}, u32[]{:S(2)}) collective-permute-start(bf16[1056,128]{1,0:T(8,128)(2,1)S(1)} %collective-permute-done.3.refs_6_), channel_id=1, source_target_pairs={{0,64},{64,0},{128,192},{192,128},{1,65},{65,1},{129,193},{193,129... | collective-permute-start | bytes 811016 | tf_op jit(solution)/shard_map/ppermute | solution.py:298
  52.7 0.1 collective-permute-start.20
  52.9 1.4 %collective-permute-start.10 = (bf16[528,128]{1,0:T(8,128)(2,1)S(1)}, bf16[528,128]{1,0:T(8,128)(2,1)S(1)}, u32[]{:S(2)}, u32[]{:S(2)}) collective-permute-start(bf16[528,128]{1,0:T(8,128)(2,1)S(1)} %slice.53), channel_id=1, source_target_pairs={{0,8},{4,12},{8,16},{12,20},{16,24},{20,28},{24,32},{28,36},{32,40... | collective-permute-start | bytes 405512 | tf_op jit(solution)/shard_map/ppermute | solution.py:295
  54.3 5.5 %collective-permute-done.14 = bf16[1024,512]{1,0:T(8,128)(2,1)S(1)} collective-permute-done((bf16[1024,512]{1,0:T(8,128)(2,1)S(1)}, bf16[1024,512]{1,0:T(8,128)(2,1)S(1)}, u32[]{:S(2)}, u32[]{:S(2)}) %collective-permute-start.14) | collective-permute-done | bytes 1048608 | tf_op jit(solution)/shard_map/ppermute | solution.py:310
  59.8 4.7 %collective-permute-start.12 = (bf16[528,128]{1,0:T(8,128)(2,1)S(1)}, bf16[528,128]{1,0:T(8,128)(2,1)S(1)}, u32[]{:S(2)}, u32[]{:S(2)}) collective-permute-start(bf16[528,128]{1,0:T(8,128)(2,1)S(1)} %slice.54), channel_id=1, source_target_pairs={{0,56},{4,60},{8,0},{12,4},{16,8},{20,12},{24,16},{28,20},{32,24},... | collective-permute-start | bytes 405512 | tf_op jit(solution)/shard_map/ppermute | solution.py:296
  64.6 0.5 collective-permute-start.9
  65.1 0.2 collective-permute-start.11
  65.3 1.2 %collective-permute-done.12.refs_6_ = bf16[528,128]{1,0:T(8,128)(2,1)S(1)} collective-permute-done((bf16[528,128]{1,0:T(8,128)(2,1)S(1)}, bf16[528,128]{1,0:T(8,128)(2,1)S(1)}, u32[]{:S(2)}, u32[]{:S(2)}) %collective-permute-start.12) | collective-permute-done | bytes 135200 | tf_op jit(solution)/shard_map/ppermute | solution.py:296
  66.6 4.2 %product.1.refs_9_ = f32[4,2176,128]{2,1,0:T(8,128)S(1)} custom-call(bf16[1056,128]{1,0:T(8,128)(2,1)S(1)} %scale.1.refs_0_, bf16[1056,128]{1,0:T(8,128)(2,1)S(1)} %collective-permute-done.16.refs_1_, bf16[1056,128]{1,0:T(8,128)(2,1)S(1)} %collective-permute-done.2.refs_2_, bf16[1056,128]{1,0:T(8,128)(2,1)S(1)} %collective-permute-done.17.refs_3_, ...), custom_call_target="tpu_custom_call" | custom-call | flops 1342177280 | bytes 1048576 | tf_op jit(solution)/shard_map/product/pallas_call | solution.py:228
  70.8 2.7 %add_product.1 = f32[4,2176,128]{2,1,0:T(8,128)S(1)} custom-call(bf16[1056,128]{1,0:T(8,128)(2,1)S(1)} %collective-permute-done.4.refs_0_, bf16[1056,128]{1,0:T(8,128)(2,1)S(1)} %collective-permute-done.5.refs_1_, bf16[1056,128]{1,0:T(8,128)(2,1)S(1)} %collective-permute-done.8.refs_2_, ...), custom_call_target="tpu_custom_call", output_to_operand_aliasing={{}: (9, {})} | custom-call | flops 805306368 | bytes 1048576 | tf_op jit(solution)/shard_map/add_product/pallas_call | solution.py:228
  73.5 0.2 slice_convert_fusion
  73.7 0.2 slice_bitcast_fusion.5
  74.0 2.7 %collective-permute-start.22 = (f16[1024,128]{1,0:T(8,128)(2,1)S(1)}, f16[1024,128]{1,0:T(8,128)(2,1)S(1)}, u32[]{:S(2)}, u32[]{:S(2)}) collective-permute-start(f16[1024,128]{1,0:T(8,128)(2,1)S(1)} %get-tuple-element.19), channel_id=1, source_target_pairs={{0,3},{1,0},{2,1},{3,2},{4,7},{5,4},{6,5},{7,6},{8,11},{9,8},{10,9... | collective-permute-start | bytes 786440 | tf_op jit(solution)/shard_map/ppermute | solution.py:322
  76.7 1.4 %collective-permute-start.25 = (f16[1024,128]{1,0:T(8,128)(2,1)S(1)}, f16[1024,128]{1,0:T(8,128)(2,1)S(1)}, u32[]{:S(2)}, u32[]{:S(2)}) collective-permute-start(f16[1024,128]{1,0:T(8,128)(2,1)S(1)} %get-tuple-element.18), channel_id=1, source_target_pairs={{0,1},{1,2},{2,3},{3,0},{4,5},{5,6},{6,7},{7,4},{8,9},{9,10},{10,1... | collective-permute-start | bytes 786440 | tf_op jit(solution)/shard_map/ppermute | solution.py:323
  78.2 4.4 %collective-permute-done.21 = f16[1024,128]{1,0:T(8,128)(2,1)S(1)} collective-permute-done((f16[1024,128]{1,0:T(8,128)(2,1)S(1)}, f16[1024,128]{1,0:T(8,128)(2,1)S(1)}, u32[]{:S(2)}, u32[]{:S(2)}) %collective-permute-start.21) | collective-permute-done | bytes 262176 | tf_op jit(solution)/shard_map/ppermute | solution.py:321
  82.6 0.2 fusion.3
  82.8 0.1 collective-permute-start.23
  82.8 2.7 %collective-permute-start.26 = (f16[1024,128]{1,0:T(8,128)(2,1)S(1)}, f16[1024,128]{1,0:T(8,128)(2,1)S(1)}, u32[]{:S(2)}, u32[]{:S(2)}) collective-permute-start(f16[1024,128]{1,0:T(8,128)(2,1)S(1)} %get-tuple-element.12), channel_id=1, source_target_pairs={{0,3},{1,0},{2,1},{3,2},{4,7},{5,4},{6,5},{7,6},{8,11},{9,8},{10,9... | collective-permute-start | bytes 786440 | tf_op jit(solution)/shard_map/ppermute | solution.py:329
  85.5 1.7 %collective-permute-done.24 = f16[1024,128]{1,0:T(8,128)(2,1)S(1)} collective-permute-done((f16[1024,128]{1,0:T(8,128)(2,1)S(1)}, f16[1024,128]{1,0:T(8,128)(2,1)S(1)}, u32[]{:S(2)}, u32[]{:S(2)}) %collective-permute-start.24) | collective-permute-done | bytes 262176 | tf_op jit(solution)/shard_map/ppermute | solution.py:324
  87.2 1.0 collective-permute-done.25
  88.2 5.6 %collective-permute-done.23 = f16[1024,128]{1,0:T(8,128)(2,1)S(1)} collective-permute-done((f16[1024,128]{1,0:T(8,128)(2,1)S(1)}, f16[1024,128]{1,0:T(8,128)(2,1)S(1)}, u32[]{:S(2)}, u32[]{:S(2)}) %collective-permute-start.23) | collective-permute-done | bytes 262176 | tf_op jit(solution)/shard_map/ppermute | solution.py:328
  93.8 1.4 %fusion.7 = (f16[1024,128]{1,0:T(8,128)(2,1)S(1)}, f16[1024,128]{1,0:T(8,128)(2,1)S(1)}) fusion(f32[4,2176,128]{2,1,0:T(8,128)} %copy-done, f16[1024,128]{1,0:T(8,128)(2,1)S(1)} %collective-permute-done.24, f16[1024,128]{1,0:T(8,128)(2,1)S(1)} %collective-permute-done.23, f16[1024,128]{1,0:T(8,128)(2,1)S(1)} %collective-permute-done.26, ...), kind=kLoop, calls=%fused_computation.14 | loop fusion | flops 1310720 | bytes 2621440 | tf_op jit(solution)/shard_map/convert
  95.2 0.1 pad_maximum_fusion
  95.4 3.3 %collective-permute-start.27 = (f16[2048,128]{1,0:T(8,128)(2,1)S(1)}, f16[2048,128]{1,0:T(8,128)(2,1)S(1)}, u32[]{:S(2)}, u32[]{:S(2)}) collective-permute-start(f16[2048,128]{1,0:T(8,128)(2,1)S(1)} %pad_maximum_fusion), channel_id=1, source_target_pairs={{0,4},{4,64},{8,12},{12,72},{16,20},{20,80},{24,28},{28,88},{32,36... | collective-permute-start | bytes 1572872 | tf_op jit(solution)/shard_map/ppermute | solution.py:340
  98.7 0.3 multiply_reduce_fusion
  99.0 12.2 %psum.15 = f32[2,128]{1,0:T(2,128)S(1)} all-reduce(f32[2,128]{1,0:T(2,128)S(1)} %broadcast_select_fusion), channel_id=1, replica_groups=mesh['row'=4,'col'=16,'layer'=4] {'row'}, use_global_device_ids=true, to_apply=%region_2.3 | all-reduce | flops 256 | bytes 2048 | tf_op jit(solution)/shard_map/psum | solution.py:347
  111.3 0.2 collective-permute-start.28
  111.5 3.8 %collective-permute-done.28 = f32[2,128]{1,0:T(2,128)S(1)} collective-permute-done((f32[2,128]{1,0:T(2,128)S(1)}, f32[2,128]{1,0:T(2,128)S(1)}, u32[]{:S(2)}, u32[]{:S(2)}) %collective-permute-start.28) | collective-permute-done | bytes 1056 | tf_op jit(solution)/shard_map/ppermute | solution.py:348
  115.3 1.1 multiply_divide_fusion
  (39 shorter events, 0.5 us)
Async XLA Ops:
  0.0 8.8 %copy-start.2 = (s32[16,4]{0,1:T(4,128)S(1)}, s32[16,4]{0,1:T(4,128)}, u32[]{:S(2)}) copy-start(s32[16,4]{0,1:T(4,128)} %param.3) | copy-start | bytes 772
  0.0 8.8 %copy-start.1 = (bf16[2048,512]{1,0:T(8,128)(2,1)S(1)}, bf16[2048,512]{1,0:T(8,128)(2,1)}, u32[]{:S(2)}) copy-start(bf16[2048,512]{1,0:T(8,128)(2,1)} %values_ref.3) | copy-start | bytes 6291460
  2.0 20.4 %collective-permute-start = (bf16[1056,128]{1,0:T(8,128)(2,1)S(1)}, bf16[1056,128]{1,0:T(8,128)(2,1)S(1)}, u32[]{:S(2)}, u32[]{:S(2)}) collective-permute-start(bf16[1056,128]{1,0:T(8,128)(2,1)S(1)} %share.1), channel_id=1, source_target_pairs={{0,16},{1,8},{2,0},{3,56},{4,112},{5,72},{6,64},{7,120},{8,1},{9,2... | collective-permute-start | bytes 811016 | tf_op jit(solution)/shard_map/ppermute | solution.py:280
  15.5 6.9 %collective-permute-start.1 = (f32[4,128]{1,0:T(4,128)S(1)}, f32[4,128]{1,0:T(4,128)S(1)}, u32[]{:S(2)}, u32[]{:S(2)}) collective-permute-start(f32[4,128]{1,0:T(4,128)S(1)} %psum.14), channel_id=1, source_target_pairs={{0,16},{1,8},{2,0},{3,56},{4,112},{5,72},{6,64},{7,120},{8,1},{9,2... | collective-permute-start | bytes 6152 | tf_op jit(solution)/shard_map/ppermute | solution.py:281
  22.5 11.0 %collective-permute-start.2 = (bf16[1056,128]{1,0:T(8,128)(2,1)S(1)}, bf16[1056,128]{1,0:T(8,128)(2,1)S(1)}, u32[]{:S(2)}, u32[]{:S(2)}) collective-permute-start(bf16[1056,128]{1,0:T(8,128)(2,1)S(1)} %scale.1.refs_0_), channel_id=1, source_target_pairs={{0,8},{4,12},{8,16},{12,20},{16,24},{20,28},{24,32},{28,36},{32,40... | collective-permute-start | bytes 811016 | tf_op jit(solution)/shard_map/ppermute | solution.py:295
  22.6 10.9 %collective-permute-start.6 = (bf16[1056,128]{1,0:T(8,128)(2,1)S(1)}, bf16[1056,128]{1,0:T(8,128)(2,1)S(1)}, u32[]{:S(2)}, u32[]{:S(2)}) collective-permute-start(bf16[1056,128]{1,0:T(8,128)(2,1)S(1)} %scale.1.refs_0_), channel_id=1, source_target_pairs={{0,56},{4,60},{8,0},{12,4},{16,8},{20,12},{24,16},{28,20},{32,24},... | collective-permute-start | bytes 811016 | tf_op jit(solution)/shard_map/ppermute | solution.py:296
  27.4 32.4 %collective-permute-start.14 = (bf16[1024,512]{1,0:T(8,128)(2,1)S(1)}, bf16[1024,512]{1,0:T(8,128)(2,1)S(1)}, u32[]{:S(2)}, u32[]{:S(2)}) collective-permute-start(bf16[1024,512]{1,0:T(8,128)(2,1)S(1)} %get-tuple-element.9), channel_id=1, source_target_pairs={{0,4},{1,128},{2,64},{3,196},{4,0},{5,132},{6,68},{7,192},{8,12},{... | collective-permute-start | bytes 3145736 | tf_op jit(solution)/shard_map/ppermute | solution.py:310
  28.9 35.7 %collective-permute-start.15 = (bf16[1024,512]{1,0:T(8,128)(2,1)S(1)}, bf16[1024,512]{1,0:T(8,128)(2,1)S(1)}, u32[]{:S(2)}, u32[]{:S(2)}) collective-permute-start(bf16[1024,512]{1,0:T(8,128)(2,1)S(1)} %get-tuple-element.10), channel_id=1, source_target_pairs={{0,197},{1,5},{2,129},{3,65},{4,193},{5,1},{6,133},{7,69},{8,205},... | collective-permute-start | bytes 3145736 | tf_op jit(solution)/shard_map/ppermute | solution.py:310
  33.5 7.4 %collective-permute-start.3 = (bf16[1056,128]{1,0:T(8,128)(2,1)S(1)}, bf16[1056,128]{1,0:T(8,128)(2,1)S(1)}, u32[]{:S(2)}, u32[]{:S(2)}) collective-permute-start(bf16[1056,128]{1,0:T(8,128)(2,1)S(1)} %collective-permute-done.2.refs_2_), channel_id=1, source_target_pairs={{0,8},{4,12},{8,16},{12,20},{16,24},{20,28},{24,32},{28,36},{32,40... | collective-permute-start | bytes 811016 | tf_op jit(solution)/shard_map/ppermute | solution.py:295
  33.5 10.3 %collective-permute-start.7 = (bf16[1056,128]{1,0:T(8,128)(2,1)S(1)}, bf16[1056,128]{1,0:T(8,128)(2,1)S(1)}, u32[]{:S(2)}, u32[]{:S(2)}) collective-permute-start(bf16[1056,128]{1,0:T(8,128)(2,1)S(1)} %collective-permute-done.6.refs_4_), channel_id=1, source_target_pairs={{0,56},{4,60},{8,0},{12,4},{16,8},{20,12},{24,16},{28,20},{32,24},... | collective-permute-start | bytes 811016 | tf_op jit(solution)/shard_map/ppermute | solution.py:296
  36.2 7.7 %collective-permute-start.16 = (bf16[1056,128]{1,0:T(8,128)(2,1)S(1)}, bf16[1056,128]{1,0:T(8,128)(2,1)S(1)}, u32[]{:S(2)}, u32[]{:S(2)}) collective-permute-start(bf16[1056,128]{1,0:T(8,128)(2,1)S(1)} %scale.1.refs_0_), channel_id=1, source_target_pairs={{0,64},{64,0},{128,192},{192,128},{1,65},{65,1},{129,193},{193,129... | collective-permute-start | bytes 811016 | tf_op jit(solution)/shard_map/ppermute | solution.py:298
  40.9 7.1 %collective-permute-start.4 = (bf16[1056,128]{1,0:T(8,128)(2,1)S(1)}, bf16[1056,128]{1,0:T(8,128)(2,1)S(1)}, u32[]{:S(2)}, u32[]{:S(2)}) collective-permute-start(bf16[1056,128]{1,0:T(8,128)(2,1)S(1)} %collective-permute-done.3.refs_6_), channel_id=1, source_target_pairs={{0,8},{4,12},{8,16},{12,20},{16,24},{20,28},{24,32},{28,36},{32,40... | collective-permute-start | bytes 811016 | tf_op jit(solution)/shard_map/ppermute | solution.py:295
  43.8 7.5 %collective-permute-start.8 = (bf16[1056,128]{1,0:T(8,128)(2,1)S(1)}, bf16[1056,128]{1,0:T(8,128)(2,1)S(1)}, u32[]{:S(2)}, u32[]{:S(2)}) collective-permute-start(bf16[1056,128]{1,0:T(8,128)(2,1)S(1)} %collective-permute-done.7.refs_8_), channel_id=1, source_target_pairs={{0,56},{4,60},{8,0},{12,4},{16,8},{20,12},{24,16},{28,20},{32,24},... | collective-permute-start | bytes 811016 | tf_op jit(solution)/shard_map/ppermute | solution.py:296
  43.8 8.9 %collective-permute-start.17 = (bf16[1056,128]{1,0:T(8,128)(2,1)S(1)}, bf16[1056,128]{1,0:T(8,128)(2,1)S(1)}, u32[]{:S(2)}, u32[]{:S(2)}) collective-permute-start(bf16[1056,128]{1,0:T(8,128)(2,1)S(1)} %collective-permute-done.2.refs_2_), channel_id=1, source_target_pairs={{0,64},{64,0},{128,192},{192,128},{1,65},{65,1},{129,193},{193,129... | collective-permute-start | bytes 811016 | tf_op jit(solution)/shard_map/ppermute | solution.py:298
  48.0 4.9 %collective-permute-start.18 = (bf16[1056,128]{1,0:T(8,128)(2,1)S(1)}, bf16[1056,128]{1,0:T(8,128)(2,1)S(1)}, u32[]{:S(2)}, u32[]{:S(2)}) collective-permute-start(bf16[1056,128]{1,0:T(8,128)(2,1)S(1)} %collective-permute-done.6.refs_4_), channel_id=1, source_target_pairs={{0,64},{64,0},{128,192},{192,128},{1,65},{65,1},{129,193},{193,129... | collective-permute-start | bytes 811016 | tf_op jit(solution)/shard_map/ppermute | solution.py:298
  51.3 13.3 %collective-permute-start.19 = (bf16[1056,128]{1,0:T(8,128)(2,1)S(1)}, bf16[1056,128]{1,0:T(8,128)(2,1)S(1)}, u32[]{:S(2)}, u32[]{:S(2)}) collective-permute-start(bf16[1056,128]{1,0:T(8,128)(2,1)S(1)} %collective-permute-done.3.refs_6_), channel_id=1, source_target_pairs={{0,64},{64,0},{128,192},{192,128},{1,65},{65,1},{129,193},{193,129... | collective-permute-start | bytes 811016 | tf_op jit(solution)/shard_map/ppermute | solution.py:298
  52.7 13.9 %collective-permute-start.20 = (bf16[1056,128]{1,0:T(8,128)(2,1)S(1)}, bf16[1056,128]{1,0:T(8,128)(2,1)S(1)}, u32[]{:S(2)}, u32[]{:S(2)}) collective-permute-start(bf16[1056,128]{1,0:T(8,128)(2,1)S(1)} %collective-permute-done.7.refs_8_), channel_id=1, source_target_pairs={{0,64},{64,0},{128,192},{192,128},{1,65},{65,1},{129,193},{193,129... | collective-permute-start | bytes 811016 | tf_op jit(solution)/shard_map/ppermute | solution.py:298
  52.9 12.3 %collective-permute-start.10 = (bf16[528,128]{1,0:T(8,128)(2,1)S(1)}, bf16[528,128]{1,0:T(8,128)(2,1)S(1)}, u32[]{:S(2)}, u32[]{:S(2)}) collective-permute-start(bf16[528,128]{1,0:T(8,128)(2,1)S(1)} %slice.53), channel_id=1, source_target_pairs={{0,8},{4,12},{8,16},{12,20},{16,24},{20,28},{24,32},{28,36},{32,40... | collective-permute-start | bytes 405512 | tf_op jit(solution)/shard_map/ppermute | solution.py:295
  59.8 6.7 %collective-permute-start.12 = (bf16[528,128]{1,0:T(8,128)(2,1)S(1)}, bf16[528,128]{1,0:T(8,128)(2,1)S(1)}, u32[]{:S(2)}, u32[]{:S(2)}) collective-permute-start(bf16[528,128]{1,0:T(8,128)(2,1)S(1)} %slice.54), channel_id=1, source_target_pairs={{0,56},{4,60},{8,0},{12,4},{16,8},{20,12},{24,16},{28,20},{32,24},... | collective-permute-start | bytes 405512 | tf_op jit(solution)/shard_map/ppermute | solution.py:296
  64.5 6.3 %collective-permute-start.5 = (bf16[1056,128]{1,0:T(8,128)(2,1)S(1)}, bf16[1056,128]{1,0:T(8,128)(2,1)S(1)}, u32[]{:S(2)}, u32[]{:S(2)}) collective-permute-start(bf16[1056,128]{1,0:T(8,128)(2,1)S(1)} %collective-permute-done.4.refs_0_), channel_id=1, source_target_pairs={{0,64},{64,0},{128,192},{192,128},{1,65},{65,1},{129,193},{193,129... | collective-permute-start | bytes 811016 | tf_op jit(solution)/shard_map/ppermute | solution.py:298
  64.6 6.3 %collective-permute-start.9 = (bf16[1056,128]{1,0:T(8,128)(2,1)S(1)}, bf16[1056,128]{1,0:T(8,128)(2,1)S(1)}, u32[]{:S(2)}, u32[]{:S(2)}) collective-permute-start(bf16[1056,128]{1,0:T(8,128)(2,1)S(1)} %collective-permute-done.8.refs_2_), channel_id=1, source_target_pairs={{0,64},{64,0},{128,192},{192,128},{1,65},{65,1},{129,193},{193,129... | collective-permute-start | bytes 811016 | tf_op jit(solution)/shard_map/ppermute | solution.py:298
  65.1 5.6 %collective-permute-start.11 = (bf16[528,128]{1,0:T(8,128)(2,1)S(1)}, bf16[528,128]{1,0:T(8,128)(2,1)S(1)}, u32[]{:S(2)}, u32[]{:S(2)}) collective-permute-start(bf16[528,128]{1,0:T(8,128)(2,1)S(1)} %collective-permute-done.10.refs_4_), channel_id=1, source_target_pairs={{0,64},{64,0},{128,192},{192,128},{1,65},{65,1},{129,193},{193,129... | collective-permute-start | bytes 405512 | tf_op jit(solution)/shard_map/ppermute | solution.py:298
  66.5 4.3 %collective-permute-start.13 = (bf16[528,128]{1,0:T(8,128)(2,1)S(1)}, bf16[528,128]{1,0:T(8,128)(2,1)S(1)}, u32[]{:S(2)}, u32[]{:S(2)}) collective-permute-start(bf16[528,128]{1,0:T(8,128)(2,1)S(1)} %collective-permute-done.12.refs_6_), channel_id=1, source_target_pairs={{0,64},{64,0},{128,192},{192,128},{1,65},{65,1},{129,193},{193,129... | collective-permute-start | bytes 405512 | tf_op jit(solution)/shard_map/ppermute | solution.py:298
  73.5 9.1 %copy-start = (f32[4,2176,128]{2,1,0:T(8,128)}, f32[4,2176,128]{2,1,0:T(8,128)S(1)}, u32[]{:S(2)}) copy-start(f32[4,2176,128]{2,1,0:T(8,128)S(1)} %add_product.1) | copy-start | bytes 13369348
  73.9 8.6 %collective-permute-start.21 = (f16[1024,128]{1,0:T(8,128)(2,1)S(1)}, f16[1024,128]{1,0:T(8,128)(2,1)S(1)}, u32[]{:S(2)}, u32[]{:S(2)}) collective-permute-start(f16[1024,128]{1,0:T(8,128)(2,1)S(1)} %get-tuple-element.20), channel_id=1, source_target_pairs={{0,1},{1,2},{2,3},{3,0},{4,5},{5,6},{6,7},{7,4},{8,9},{9,10},{10,1... | collective-permute-start | bytes 786440 | tf_op jit(solution)/shard_map/ppermute | solution.py:321
  74.0 8.6 %collective-permute-start.22 = (f16[1024,128]{1,0:T(8,128)(2,1)S(1)}, f16[1024,128]{1,0:T(8,128)(2,1)S(1)}, u32[]{:S(2)}, u32[]{:S(2)}) collective-permute-start(f16[1024,128]{1,0:T(8,128)(2,1)S(1)} %get-tuple-element.19), channel_id=1, source_target_pairs={{0,3},{1,0},{2,1},{3,2},{4,7},{5,4},{6,5},{7,6},{8,11},{9,8},{10,9... | collective-permute-start | bytes 786440 | tf_op jit(solution)/shard_map/ppermute | solution.py:322
  76.7 10.5 %collective-permute-start.24 = (f16[1024,128]{1,0:T(8,128)(2,1)S(1)}, f16[1024,128]{1,0:T(8,128)(2,1)S(1)}, u32[]{:S(2)}, u32[]{:S(2)}) collective-permute-start(f16[1024,128]{1,0:T(8,128)(2,1)S(1)} %get-tuple-element.17), channel_id=1, source_target_pairs={{0,3},{1,0},{2,1},{3,2},{4,7},{5,4},{6,5},{7,6},{8,11},{9,8},{10,9... | collective-permute-start | bytes 786440 | tf_op jit(solution)/shard_map/ppermute | solution.py:324
  76.7 11.5 %collective-permute-start.25 = (f16[1024,128]{1,0:T(8,128)(2,1)S(1)}, f16[1024,128]{1,0:T(8,128)(2,1)S(1)}, u32[]{:S(2)}, u32[]{:S(2)}) collective-permute-start(f16[1024,128]{1,0:T(8,128)(2,1)S(1)} %get-tuple-element.18), channel_id=1, source_target_pairs={{0,1},{1,2},{2,3},{3,0},{4,5},{5,6},{6,7},{7,4},{8,9},{9,10},{10,1... | collective-permute-start | bytes 786440 | tf_op jit(solution)/shard_map/ppermute | solution.py:323
  82.8 11.1 %collective-permute-start.23 = (f16[1024,128]{1,0:T(8,128)(2,1)S(1)}, f16[1024,128]{1,0:T(8,128)(2,1)S(1)}, u32[]{:S(2)}, u32[]{:S(2)}) collective-permute-start(f16[1024,128]{1,0:T(8,128)(2,1)S(1)} %get-tuple-element.11), channel_id=1, source_target_pairs={{0,1},{1,2},{2,3},{3,0},{4,5},{5,6},{6,7},{7,4},{8,9},{9,10},{10,1... | collective-permute-start | bytes 786440 | tf_op jit(solution)/shard_map/ppermute | solution.py:328
  82.8 11.0 %collective-permute-start.26 = (f16[1024,128]{1,0:T(8,128)(2,1)S(1)}, f16[1024,128]{1,0:T(8,128)(2,1)S(1)}, u32[]{:S(2)}, u32[]{:S(2)}) collective-permute-start(f16[1024,128]{1,0:T(8,128)(2,1)S(1)} %get-tuple-element.12), channel_id=1, source_target_pairs={{0,3},{1,0},{2,1},{3,2},{4,7},{5,4},{6,5},{7,6},{8,11},{9,8},{10,9... | collective-permute-start | bytes 786440 | tf_op jit(solution)/shard_map/ppermute | solution.py:329
  95.4 19.9 %collective-permute-start.27 = (f16[2048,128]{1,0:T(8,128)(2,1)S(1)}, f16[2048,128]{1,0:T(8,128)(2,1)S(1)}, u32[]{:S(2)}, u32[]{:S(2)}) collective-permute-start(f16[2048,128]{1,0:T(8,128)(2,1)S(1)} %pad_maximum_fusion), channel_id=1, source_target_pairs={{0,4},{4,64},{8,12},{12,72},{16,20},{20,80},{24,28},{28,88},{32,36... | collective-permute-start | bytes 1572872 | tf_op jit(solution)/shard_map/ppermute | solution.py:340
  111.3 4.0 %collective-permute-start.28 = (f32[2,128]{1,0:T(2,128)S(1)}, f32[2,128]{1,0:T(2,128)S(1)}, u32[]{:S(2)}, u32[]{:S(2)}) collective-permute-start(f32[2,128]{1,0:T(2,128)S(1)} %psum.15), channel_id=1, source_target_pairs={{0,4},{4,0},{8,12},{12,8},{16,20},{20,16},{24,28},{28,24},{32,36},... | collective-permute-start | bytes 3080 | tf_op jit(solution)/shard_map/ppermute | solution.py:348

commit v3 on v2

--- a/solution.py
+++ b/solution.py
@@ -19,9 +19,8 @@
 
 def share_kernel(halves, per, depth_tiles, mask_hbm, values_hbm, part_ref, mask_ref, table_ref, sem):
     tiles_c, tiles_r = mask_ref.shape
-    layer, col = lax.axis_index("layer"), lax.axis_index("col")
-    z = lax.div(col, 2)
-    section = ((lax.div(z, 4) ^ (z & 1)) * 2) + (col & 1)
+    layer, row, z = lax.axis_index("layer"), lax.axis_index("row"), lax.div(lax.axis_index("col"), 2)
+    section = lax.div(z, 2) ^ row
     dead = tiles_r * tiles_c
     count = halves * per
     size = HEAD + per * T
@@ -119,32 +118,30 @@
     )(mask, values)
 
 
-def halves_kernel(mask_hbm, values_ref, *refs):
-    out_refs, (mask_ref, sem) = refs[:2], refs[2:]
-    tiles_c, tiles_r = mask_ref.shape
+def quarter_kernel(mask_hbm, values_ref, out_ref, mask_ref, sem):
+    tiles_c, _ = mask_ref.shape
     load(mask_hbm, mask_ref, sem)
-    x_lo = lax.div(lax.axis_index("row"), 2)
-    for m, ref in enumerate(out_refs):
-        first = (m ^ x_lo) * (tiles_r // 2)
-        for i in range(tiles_r // 2):
-            at = pl.ds(pl.multiple_of((first + i) * T, T), T)
-            for c in range(tiles_c):
-                tile = values_ref[at, c * T:(c + 1) * T]
-                ref[i * T:(i + 1) * T, c * T:(c + 1) * T] = jnp.where(
-                    mask_ref[c, first + i] != 0, tile, jnp.zeros_like(tile))
-
-
-def masked_halves(mask, values):
+    layer = lax.axis_index("layer")
+    first = ((layer & 1) * 2 + lax.div(layer, 2)) * tiles_c
+    for i in range(out_ref.shape[0] // T):
+        at = pl.ds(pl.multiple_of((first + i) * T, T), T)
+        for c in range(tiles_c):
+            tile = values_ref[at, c * T:(c + 1) * T]
+            out_ref[i * T:(i + 1) * T, c * T:(c + 1) * T] = jnp.where(
+                mask_ref[c, first + i] != 0, tile, jnp.zeros_like(tile))
+
+
+def masked_quarter(mask, values, n_layer):
     height, width = values.shape
     return pl.pallas_call(
-        halves_kernel,
-        out_shape=(pltpu.VMEM((height // 2, width), jnp.bfloat16),) * 2,
+        quarter_kernel,
+        out_shape=pltpu.VMEM((height // n_layer, width), jnp.bfloat16),
         in_specs=[ANY, VMEM],
-        out_specs=(VMEM, VMEM),
+        out_specs=VMEM,
         scratch_shapes=[pltpu.SMEM(mask.shape, jnp.int32), pltpu.SemaphoreType.DMA],
-        cost_estimate=pl.CostEstimate(flops=2**20, bytes_accessed=4 * 2**20, transcendentals=0),
-        compiler_params=pltpu.CompilerParams(vmem_limit_bytes=GRANT),
-        name="masked_halves",
+        cost_estimate=pl.CostEstimate(flops=2**18, bytes_accessed=2**20, transcendentals=0),
+        compiler_params=pltpu.CompilerParams(vmem_limit_bytes=GRANT),
+        name="masked_quarter",
     )(mask, values)
 
 
@@ -273,13 +270,13 @@
     spread = {}
     for r, c, y in coords(sizes):
         zz, hi = c // 2, c % 2
-        y_to = zz % n_layer
-        move = {0: 2 - 4 * hi, 1: 1, 2: 0, 3: -1}[(y - y_to) % n_layer]
-        spread[r, c, y] = flat(r // 2 * 2 + hi, (zz + move) % n_z * 2 + r % 2, y_to, sizes)
+        y_to = hi * 2 + zz % 2
+        move, core = {0: (1, 0), 1: (-1, 1), 2: (0, 0), 3: (0, 1)}[(y - y_to) % n_layer]
+        spread[r, c, y] = flat(r // 2 * 2 + core, (zz + move) % n_z * 2 + r % 2, y_to, sizes)
     table = [(flat(*at, sizes), to) for at, to in spread.items()]
     raw = lax.ppermute(raw, axes, table)
     mass = lax.ppermute(lax.psum(column_sums(mask, values), "row"), axes, table)
-    rights = list(masked_halves(mask, values))
+    quarter = masked_quarter(mask, values, n_layer)
     part = scale(raw, mass, per, halves)
 
     def ring(step):
@@ -297,17 +294,15 @@
         mine += [up, down]
     parts = [(p, lax.ppermute(p, "row", swap)) for p in mine]
 
-    n_x = n_row // 2 * 2
-    for m in range(2):
+    rights = []
+    for m in range(n_row):
         perm = []
         for r, c, y in coords(sizes):
             lo, core, zz, hi = r // 2, r % 2, c // 2, c % 2
-            y_to = core * 2 + (m ^ lo)
-            x_to = (hi * 2 + lo + 2 - (y - y_to)) % n_x
-            lo_to, hi_to = x_to % 2, x_to // 2
-            to = (lo_to * 2 + (hi ^ hi_to ^ lo_to ^ 1), zz * 2 + hi_to, y_to)
+            lo_to, hi_to = lo ^ m // 2, core ^ m % 2
+            to = (lo_to * 2 + (hi ^ hi_to ^ lo_to ^ 1), zz * 2 + hi_to, y)
             perm.append((flat(r, c, y, sizes), flat(*to, sizes)))
-        rights[m] = lax.ppermute(rights[m], axes, perm)
+        rights.append(lax.ppermute(quarter, axes, perm))
     right = jnp.concatenate(rights)
     early = [p for pair in parts[:2 * last - 3] for p in pair]
     late = [p for pair in parts[2 * last - 3:] for p in pair]
@@ -341,14 +336,13 @@
         total, ("row", "col"), [(r * n_col + c, o[0] * n_col + o[1]) for (r, c), o in owner.items()])
     summand = total.astype(f32)
     summand = jnp.sum(summand * summand, axis=0)
-    row, x_hi = lax.axis_index("row"), lax.axis_index("col") % 2
-    which = (row % 2) ^ x_hi ^ (row // 2) ^ 1
-    pair = jnp.where(lax.broadcasted_iota(jnp.int32, (2, T), 0) == which, summand, 0.0)
-    pair = lax.psum(pair, "row")
-    pair = pair + lax.ppermute(pair, "col", [(c, c ^ 1) for c in range(n_col)])
-    weight = jnp.where(x_hi == 0, pair[0], pair[1])
+    weights = []
+    for k in range(1, n_row):
+        perm = [(r * n_col + c, (o[0] ^ k) * n_col + o[1]) for (r, c), o in owner.items()]
+        weights.append(lax.ppermute(summand, ("row", "col"), perm))
     expanded = expanded.astype(f32)
     inflated = expanded * expanded
+    weight = jnp.sum(inflated, axis=0) + (weights[0] + (weights[1] + weights[2]))
     order = height * n_row
     return order * 1.0 * inflated / weight[None, :]
 

time: 117 us -> 110 us (0.940)
  blocking collectives: 18 us -> 8.58 us
  waiting for transfers between devices: 31.2 us -> 36.9 us
  starting transfers between devices: 52.3 us -> 51 us
    psum x1 -> x0, blocking collectives: 12.2 us -> none  [shards(): pair = lax.psum(pair, 'row')]
    ppermute x4, waiting for transfers between devices: 2.85 us -> 12.4 us  [shards(): down = lax.ppermute(down, 'col', ring(-1))]
    ppermute x3 -> x7, waiting for transfers between devices: 9.28 us -> 0.02 us  [the longest x4 0.01 us: shards(): rights.append(lax.ppermute(quarter, axes, perm))]
    ppermute x1, waiting for transfers between devices: 0.01 us -> 6.3 us  [shards(): lax.ppermute(total, ('row', 'col'), [(r * n_col + c, o[0] * n_col + o[1])...]
    ppermute x1, waiting for transfers between devices: 0.01 us -> 4.93 us  [shards(): far_b = lax.ppermute(send[1, mid:], 'layer', down)]
    ppermute x4, starting transfers between devices: 11.2 us -> 15.6 us  [shards(): down = lax.ppermute(down, 'col', ring(-1))]
    ppermute x9, starting transfers between devices: 10.9 us -> 6.66 us  [shards(): parts = [(p, lax.ppermute(p, 'row', swap)) for p in mine]]
    ppermute x1, waiting for transfers between devices: 4.42 us -> 1.3 us  [shards(): far_a = lax.ppermute(send[1, :mid], 'layer', up)]
  transfers between devices with their start and end apart: 29 -> 33, of which waited for: 11 -> 14; matrix products, arithmetic and copies ran while one was open for 1% -> 1% of each run, Pallas kernels for 5% -> 5%
where the time goes in v3:
time: 110 us
  starting transfers between devices  51 us (46%)
  waiting for transfers between devices  36.9 us (34%)
  Pallas kernels  10.4 us (9%)
  blocking collectives  8.58 us (8%)
  other arithmetic  2.4 us (2%)
    ppermute x4, starting transfers between devices, shards(): down = lax.ppermute(down, 'col', ring(-1))  15.6 us
    ppermute x4, waiting for transfers between devices, shards(): down = lax.ppermute(down, 'col', ring(-1))  12.4 us
    psum x1, blocking collectives, shards(): mass = lax.ppermute(lax.psum(column_sums(mask, values), 'row'), axes, table)  8.58 us
    pallas_call x2, Pallas kernels, product(): pl.pallas_call(functools.partial(product_kernel, n_parts, counts, per, ag...  6.73 us
    ppermute x9, starting transfers between devices, shards(): parts = [(p, lax.ppermute(p, 'row', swap)) for p in mine]  6.66 us
    ppermute x1, waiting for transfers between devices, shards(): lax.ppermute(total, ('row', 'col'), [(r * n_col + c, o[0] * n_col + o[1])...  6.3 us
    ppermute x4, starting transfers between devices, shards(): rights.append(lax.ppermute(quarter, axes, perm))  5.81 us
    ppermute x1, waiting for transfers between devices, shards(): up_a = lax.ppermute(up_a, 'layer', up)  5.62 us
  transfers between devices with their start and end apart: 33, of which 14 were waited for; matrix products, arithmetic and copies ran while one was open for 1% of the time, Pallas kernels for 5%

profile of v3, /device:TPU:1, one launch (start us, length us, event | category | flops | bytes accessed | tf_op | source)
XLA Modules:
  0.0 109.9 jit_solution(16428105749639916244)
XLA Ops:
  0.0 2.0 %share.1 = bf16[1056,128]{1,0:T(8,128)(2,1)S(1)} custom-call(s32[4,16]{1,0:T(4,128)} %bitcast.33, bf16[2048,512]{1,0:T(8,128)(2,1)} %values_ref.3), custom_call_target="tpu_custom_call" | custom-call | flops 1048576 | bytes 2097152 | tf_op jit(solution)/shard_map/share/pallas_call | solution.py:74
  2.0 5.6 %collective-permute-start = (bf16[1056,128]{1,0:T(8,128)(2,1)S(1)}, bf16[1056,128]{1,0:T(8,128)(2,1)S(1)}, u32[]{:S(2)}, u32[]{:S(2)}) collective-permute-start(bf16[1056,128]{1,0:T(8,128)(2,1)S(1)} %share.1), channel_id=1, source_target_pairs={{0,8},{1,120},{2,0},{3,64},{4,2},{5,66},{6,10},{7,122},{8,73},{9,1... | collective-permute-start | bytes 811016 | tf_op jit(solution)/shard_map/ppermute | solution.py:277
  7.5 0.7 masked_quarter.1
  8.4 0.9 column_sums.1
  9.3 8.6 %psum.7 = f32[4,128]{1,0:T(4,128)S(1)} all-reduce(f32[4,128]{1,0:T(4,128)S(1)} %column_sums.1), channel_id=1, replica_groups=mesh['row'=4,'col'=16,'layer'=4] {'row'}, use_global_device_ids=true, to_apply=%region_0.0 | all-reduce | flops 512 | bytes 4096 | tf_op jit(solution)/shard_map/psum | solution.py:278
  17.8 4.7 %collective-permute-start.1 = (f32[4,128]{1,0:T(4,128)S(1)}, f32[4,128]{1,0:T(4,128)S(1)}, u32[]{:S(2)}, u32[]{:S(2)}) collective-permute-start(f32[4,128]{1,0:T(4,128)S(1)} %psum.7), channel_id=1, source_target_pairs={{0,8},{1,120},{2,0},{3,64},{4,2},{5,66},{6,10},{7,122},{8,73},{9,1... | collective-permute-start | bytes 6152 | tf_op jit(solution)/shard_map/ppermute | solution.py:278
  22.6 0.7 collective-permute-done.1.mass_ref
  23.4 8.3 %collective-permute-start.6 = (bf16[1056,128]{1,0:T(8,128)(2,1)S(1)}, bf16[1056,128]{1,0:T(8,128)(2,1)S(1)}, u32[]{:S(2)}, u32[]{:S(2)}) collective-permute-start(bf16[1056,128]{1,0:T(8,128)(2,1)S(1)} %scale.1.refs_0_), channel_id=1, source_target_pairs={{0,56},{4,60},{8,0},{12,4},{16,8},{20,12},{24,16},{28,20},{32,24},... | collective-permute-start | bytes 811016 | tf_op jit(solution)/shard_map/ppermute | solution.py:293
  31.7 1.1 collective-permute-start.16
  32.8 4.0 %collective-permute-start.14 = (bf16[512,512]{1,0:T(8,128)(2,1)S(1)}, bf16[512,512]{1,0:T(8,128)(2,1)S(1)}, u32[]{:S(2)}, u32[]{:S(2)}) collective-permute-start(bf16[512,512]{1,0:T(8,128)(2,1)S(1)} %masked_quarter.1), channel_id=1, source_target_pairs={{0,64},{1,65},{2,66},{3,67},{4,0},{5,1},{6,2},{7,3},{8,72},{9,73},... | collective-permute-start | bytes 1572872 | tf_op jit(solution)/shard_map/ppermute | solution.py:305
  36.8 0.3 collective-permute-done.6.refs_4_
  37.0 3.8 %collective-permute-start.7 = (bf16[1056,128]{1,0:T(8,128)(2,1)S(1)}, bf16[1056,128]{1,0:T(8,128)(2,1)S(1)}, u32[]{:S(2)}, u32[]{:S(2)}) collective-permute-start(bf16[1056,128]{1,0:T(8,128)(2,1)S(1)} %collective-permute-done.6.refs_4_), channel_id=1, source_target_pairs={{0,56},{4,60},{8,0},{12,4},{16,8},{20,12},{24,16},{28,20},{32,24},... | collective-permute-start | bytes 811016 | tf_op jit(solution)/shard_map/ppermute | solution.py:293
  40.8 0.7 collective-permute-start.15
  41.5 5.1 %collective-permute-done.7.refs_8_ = bf16[1056,128]{1,0:T(8,128)(2,1)S(1)} collective-permute-done((bf16[1056,128]{1,0:T(8,128)(2,1)S(1)}, bf16[1056,128]{1,0:T(8,128)(2,1)S(1)}, u32[]{:S(2)}, u32[]{:S(2)}) %collective-permute-start.7) | collective-permute-done | bytes 270368 | tf_op jit(solution)/shard_map/ppermute | solution.py:293
  46.6 3.4 %collective-permute-start.8 = (bf16[1056,128]{1,0:T(8,128)(2,1)S(1)}, bf16[1056,128]{1,0:T(8,128)(2,1)S(1)}, u32[]{:S(2)}, u32[]{:S(2)}) collective-permute-start(bf16[1056,128]{1,0:T(8,128)(2,1)S(1)} %collective-permute-done.7.refs_8_), channel_id=1, source_target_pairs={{0,56},{4,60},{8,0},{12,4},{16,8},{20,12},{24,16},{28,20},{32,24},... | collective-permute-start | bytes 811016 | tf_op jit(solution)/shard_map/ppermute | solution.py:293
  50.1 0.4 collective-permute-done.3.refs_6_
  50.5 0.5 collective-permute-start.18
  51.0 4.9 %collective-permute-done.8.refs_2_ = bf16[1056,128]{1,0:T(8,128)(2,1)S(1)} collective-permute-done((bf16[1056,128]{1,0:T(8,128)(2,1)S(1)}, bf16[1056,128]{1,0:T(8,128)(2,1)S(1)}, u32[]{:S(2)}, u32[]{:S(2)}) %collective-permute-start.8) | collective-permute-done | bytes 270368 | tf_op jit(solution)/shard_map/ppermute | solution.py:293
  56.0 0.8 collective-permute-start.19
  56.8 2.5 %collective-permute-done.4.refs_0_ = bf16[1056,128]{1,0:T(8,128)(2,1)S(1)} collective-permute-done((bf16[1056,128]{1,0:T(8,128)(2,1)S(1)}, bf16[1056,128]{1,0:T(8,128)(2,1)S(1)}, u32[]{:S(2)}, u32[]{:S(2)}) %collective-permute-start.4) | collective-permute-done | bytes 270368 | tf_op jit(solution)/shard_map/ppermute | solution.py:292
  59.2 1.3 %collective-permute-start.22 = (bf16[1056,128]{1,0:T(8,128)(2,1)S(1)}, bf16[1056,128]{1,0:T(8,128)(2,1)S(1)}, u32[]{:S(2)}, u32[]{:S(2)}) collective-permute-start(bf16[1056,128]{1,0:T(8,128)(2,1)S(1)} %collective-permute-done.7.refs_8_), channel_id=1, source_target_pairs={{0,64},{64,0},{128,192},{192,128},{1,65},{65,1},{129,193},{193,129... | collective-permute-start | bytes 811016 | tf_op jit(solution)/shard_map/ppermute | solution.py:295
  60.6 0.3 collective-permute-start.21
  61.0 1.4 %collective-permute-start.10 = (bf16[528,128]{1,0:T(8,128)(2,1)S(1)}, bf16[528,128]{1,0:T(8,128)(2,1)S(1)}, u32[]{:S(2)}, u32[]{:S(2)}) collective-permute-start(bf16[528,128]{1,0:T(8,128)(2,1)S(1)} %slice.45), channel_id=1, source_target_pairs={{0,8},{4,12},{8,16},{12,20},{16,24},{20,28},{24,32},{28,36},{32,40... | collective-permute-start | bytes 405512 | tf_op jit(solution)/shard_map/ppermute | solution.py:292
  62.5 1.1 collective-permute-start.9
  63.7 2.0 %collective-permute-done.12.refs_6_ = bf16[528,128]{1,0:T(8,128)(2,1)S(1)} collective-permute-done((bf16[528,128]{1,0:T(8,128)(2,1)S(1)}, bf16[528,128]{1,0:T(8,128)(2,1)S(1)}, u32[]{:S(2)}, u32[]{:S(2)}) %collective-permute-start.12) | collective-permute-done | bytes 135200 | tf_op jit(solution)/shard_map/ppermute | solution.py:293
  65.7 1.3 %collective-permute-start.13 = (bf16[528,128]{1,0:T(8,128)(2,1)S(1)}, bf16[528,128]{1,0:T(8,128)(2,1)S(1)}, u32[]{:S(2)}, u32[]{:S(2)}) collective-permute-start(bf16[528,128]{1,0:T(8,128)(2,1)S(1)} %collective-permute-done.12.refs_6_), channel_id=1, source_target_pairs={{0,64},{64,0},{128,192},{192,128},{1,65},{65,1},{129,193},{193,129... | collective-permute-start | bytes 405512 | tf_op jit(solution)/shard_map/ppermute | solution.py:295
  67.1 1.3 %collective-permute-start.11 = (bf16[528,128]{1,0:T(8,128)(2,1)S(1)}, bf16[528,128]{1,0:T(8,128)(2,1)S(1)}, u32[]{:S(2)}, u32[]{:S(2)}) collective-permute-start(bf16[528,128]{1,0:T(8,128)(2,1)S(1)} %collective-permute-done.10.refs_4_), channel_id=1, source_target_pairs={{0,64},{64,0},{128,192},{192,128},{1,65},{65,1},{129,193},{193,129... | collective-permute-start | bytes 405512 | tf_op jit(solution)/shard_map/ppermute | solution.py:295
  68.4 4.1 %product.1.refs_9_ = f32[4,2176,128]{2,1,0:T(8,128)S(1)} custom-call(bf16[1056,128]{1,0:T(8,128)(2,1)S(1)} %scale.1.refs_0_, bf16[1056,128]{1,0:T(8,128)(2,1)S(1)} %collective-permute-done.18.refs_1_, bf16[1056,128]{1,0:T(8,128)(2,1)S(1)} %collective-permute-done.2.refs_2_, bf16[1056,128]{1,0:T(8,128)(2,1)S(1)} %collective-permute-done.19.refs_3_, ...), custom_call_target="tpu_custom_call" | custom-call | flops 1342177280 | bytes 1048576 | tf_op jit(solution)/shard_map/product/pallas_call | solution.py:225
  72.5 2.6 %add_product.1 = f32[4,2176,128]{2,1,0:T(8,128)S(1)} custom-call(bf16[1056,128]{1,0:T(8,128)(2,1)S(1)} %collective-permute-done.4.refs_0_, bf16[1056,128]{1,0:T(8,128)(2,1)S(1)} %collective-permute-done.5.refs_1_, bf16[1056,128]{1,0:T(8,128)(2,1)S(1)} %collective-permute-done.8.refs_2_, ...), custom_call_target="tpu_custom_call", output_to_operand_aliasing={{}: (9, {})} | custom-call | flops 805306368 | bytes 1048576 | tf_op jit(solution)/shard_map/add_product/pallas_call | solution.py:225
  75.2 0.2 slice_convert_fusion
  75.4 0.2 slice_bitcast_fusion.5
  75.7 1.5 %collective-permute-start.23 = (f16[1024,128]{1,0:T(8,128)(2,1)S(1)}, f16[1024,128]{1,0:T(8,128)(2,1)S(1)}, u32[]{:S(2)}, u32[]{:S(2)}) collective-permute-start(f16[1024,128]{1,0:T(8,128)(2,1)S(1)} %get-tuple-element.16), channel_id=1, source_target_pairs={{0,1},{1,2},{2,3},{3,0},{4,5},{5,6},{6,7},{7,4},{8,9},{9,10},{10,1... | collective-permute-start | bytes 786440 | tf_op jit(solution)/shard_map/ppermute | solution.py:316
  77.1 1.3 %collective-permute-start.26 = (f16[1024,128]{1,0:T(8,128)(2,1)S(1)}, f16[1024,128]{1,0:T(8,128)(2,1)S(1)}, u32[]{:S(2)}, u32[]{:S(2)}) collective-permute-start(f16[1024,128]{1,0:T(8,128)(2,1)S(1)} %get-tuple-element.13), channel_id=1, source_target_pairs={{0,3},{1,0},{2,1},{3,2},{4,7},{5,4},{6,5},{7,6},{8,11},{9,8},{10,9... | collective-permute-start | bytes 786440 | tf_op jit(solution)/shard_map/ppermute | solution.py:319
  78.4 0.2 collective-permute-start.27
  78.6 4.9 %collective-permute-done.24 = f16[1024,128]{1,0:T(8,128)(2,1)S(1)} collective-permute-done((f16[1024,128]{1,0:T(8,128)(2,1)S(1)}, f16[1024,128]{1,0:T(8,128)(2,1)S(1)}, u32[]{:S(2)}, u32[]{:S(2)}) %collective-permute-start.24) | collective-permute-done | bytes 262176 | tf_op jit(solution)/shard_map/ppermute | solution.py:317
  83.5 1.3 %collective-permute-done.23 = f16[1024,128]{1,0:T(8,128)(2,1)S(1)} collective-permute-done((f16[1024,128]{1,0:T(8,128)(2,1)S(1)}, f16[1024,128]{1,0:T(8,128)(2,1)S(1)}, u32[]{:S(2)}, u32[]{:S(2)}) %collective-permute-start.23) | collective-permute-done | bytes 262176 | tf_op jit(solution)/shard_map/ppermute | solution.py:316
  85.1 2.7 %collective-permute-start.28 = (f16[1024,128]{1,0:T(8,128)(2,1)S(1)}, f16[1024,128]{1,0:T(8,128)(2,1)S(1)}, u32[]{:S(2)}, u32[]{:S(2)}) collective-permute-start(f16[1024,128]{1,0:T(8,128)(2,1)S(1)} %get-tuple-element.8), channel_id=1, source_target_pairs={{0,3},{1,0},{2,1},{3,2},{4,7},{5,4},{6,5},{7,6},{8,11},{9,8},{10,9... | collective-permute-start | bytes 786440 | tf_op jit(solution)/shard_map/ppermute | solution.py:324
  87.7 1.4 %collective-permute-done.26 = f16[1024,128]{1,0:T(8,128)(2,1)S(1)} collective-permute-done((f16[1024,128]{1,0:T(8,128)(2,1)S(1)}, f16[1024,128]{1,0:T(8,128)(2,1)S(1)}, u32[]{:S(2)}, u32[]{:S(2)}) %collective-permute-start.26) | collective-permute-done | bytes 262176 | tf_op jit(solution)/shard_map/ppermute | solution.py:319
  89.1 1.3 %collective-permute-done.27 = f16[1024,128]{1,0:T(8,128)(2,1)S(1)} collective-permute-done((f16[1024,128]{1,0:T(8,128)(2,1)S(1)}, f16[1024,128]{1,0:T(8,128)(2,1)S(1)}, u32[]{:S(2)}, u32[]{:S(2)}) %collective-permute-start.27) | collective-permute-done | bytes 262176 | tf_op jit(solution)/shard_map/ppermute | solution.py:318
  90.4 5.6 %collective-permute-done.25 = f16[1024,128]{1,0:T(8,128)(2,1)S(1)} collective-permute-done((f16[1024,128]{1,0:T(8,128)(2,1)S(1)}, f16[1024,128]{1,0:T(8,128)(2,1)S(1)}, u32[]{:S(2)}, u32[]{:S(2)}) %collective-permute-start.25) | collective-permute-done | bytes 262176 | tf_op jit(solution)/shard_map/ppermute | solution.py:323
  96.1 0.2 fusion.8
  96.4 2.8 %collective-permute-start.29 = (f16[2048,128]{1,0:T(8,128)(2,1)S(1)}, f16[2048,128]{1,0:T(8,128)(2,1)S(1)}, u32[]{:S(2)}, u32[]{:S(2)}) collective-permute-start(f16[2048,128]{1,0:T(8,128)(2,1)S(1)} %pad_maximum_fusion), channel_id=1, source_target_pairs={{0,4},{4,64},{8,12},{12,72},{16,20},{20,80},{24,28},{28,88},{32,36... | collective-permute-start | bytes 1572872 | tf_op jit(solution)/shard_map/ppermute | solution.py:335
  99.2 0.3 multiply_reduce_fusion
  99.5 2.0 %collective-permute-start.32 = (f32[128]{0:T(128)S(1)}, f32[128]{0:T(128)S(1)}, u32[]{:S(2)}, u32[]{:S(2)}) collective-permute-start(f32[128]{0:T(128)S(1)} %multiply_reduce_fusion), channel_id=1, source_target_pairs={{0,196},{4,128},{8,204},{12,136},{16,212},{20,144},{24,220},{28,15... | collective-permute-start | bytes 1544 | tf_op jit(solution)/shard_map/ppermute | solution.py:342
  101.5 0.7 collective-permute-start.30
  102.1 6.3 %collective-permute-done.29 = f16[2048,128]{1,0:T(8,128)(2,1)S(1)} collective-permute-done((f16[2048,128]{1,0:T(8,128)(2,1)S(1)}, f16[2048,128]{1,0:T(8,128)(2,1)S(1)}, u32[]{:S(2)}, u32[]{:S(2)}) %collective-permute-start.29) | collective-permute-done | bytes 524320 | tf_op jit(solution)/shard_map/ppermute | solution.py:335
  108.4 0.3 fusion
  108.8 1.1 %multiply_divide_fusion = f32[2048,128]{1,0:T(8,128)} fusion(f16[2048,128]{1,0:T(8,128)(2,1)S(1)} %collective-permute-done.29, f32[128]{0:T(128)S(1)} %add_add_fusion), kind=kLoop, calls=%fused_computation.2 | loop fusion | flops 1048576 | bytes 1573376 | tf_op jit(solution)/shard_map/div | solution.py:347
  (44 shorter events, 1.2 us)
Async XLA Ops:
  0.0 7.5 %copy-start = (bf16[2048,512]{1,0:T(8,128)(2,1)S(1)}, bf16[2048,512]{1,0:T(8,128)(2,1)}, u32[]{:S(2)}) copy-start(bf16[2048,512]{1,0:T(8,128)(2,1)} %values_ref.3) | copy-start | bytes 6291460
  0.0 7.5 %copy-start.1 = (s32[16,4]{0,1:T(4,128)S(1)}, s32[16,4]{0,1:T(4,128)}, u32[]{:S(2)}) copy-start(s32[16,4]{0,1:T(4,128)} %param.3) | copy-start | bytes 772
  2.0 21.3 %collective-permute-start = (bf16[1056,128]{1,0:T(8,128)(2,1)S(1)}, bf16[1056,128]{1,0:T(8,128)(2,1)S(1)}, u32[]{:S(2)}, u32[]{:S(2)}) collective-permute-start(bf16[1056,128]{1,0:T(8,128)(2,1)S(1)} %share.1), channel_id=1, source_target_pairs={{0,8},{1,120},{2,0},{3,64},{4,2},{5,66},{6,10},{7,122},{8,73},{9,1... | collective-permute-start | bytes 811016 | tf_op jit(solution)/shard_map/ppermute | solution.py:277
  8.3 32.6 %collective-permute-start.17 = (bf16[512,512]{1,0:T(8,128)(2,1)S(1)}, bf16[512,512]{1,0:T(8,128)(2,1)S(1)}, u32[]{:S(2)}, u32[]{:S(2)}) collective-permute-start(bf16[512,512]{1,0:T(8,128)(2,1)S(1)} %masked_quarter.1), channel_id=1, source_target_pairs={{0,196},{1,197},{2,198},{3,199},{4,132},{5,133},{6,134},{7,135},{8... | collective-permute-start | bytes 1572872 | tf_op jit(solution)/shard_map/ppermute | solution.py:305
  17.8 5.5 %collective-permute-start.1 = (f32[4,128]{1,0:T(4,128)S(1)}, f32[4,128]{1,0:T(4,128)S(1)}, u32[]{:S(2)}, u32[]{:S(2)}) collective-permute-start(f32[4,128]{1,0:T(4,128)S(1)} %psum.7), channel_id=1, source_target_pairs={{0,8},{1,120},{2,0},{3,64},{4,2},{5,66},{6,10},{7,122},{8,73},{9,1... | collective-permute-start | bytes 6152 | tf_op jit(solution)/shard_map/ppermute | solution.py:278
  23.4 13.7 %collective-permute-start.6 = (bf16[1056,128]{1,0:T(8,128)(2,1)S(1)}, bf16[1056,128]{1,0:T(8,128)(2,1)S(1)}, u32[]{:S(2)}, u32[]{:S(2)}) collective-permute-start(bf16[1056,128]{1,0:T(8,128)(2,1)S(1)} %scale.1.refs_0_), channel_id=1, source_target_pairs={{0,56},{4,60},{8,0},{12,4},{16,8},{20,12},{24,16},{28,20},{32,24},... | collective-permute-start | bytes 811016 | tf_op jit(solution)/shard_map/ppermute | solution.py:293
  31.7 9.1 %collective-permute-start.2 = (bf16[1056,128]{1,0:T(8,128)(2,1)S(1)}, bf16[1056,128]{1,0:T(8,128)(2,1)S(1)}, u32[]{:S(2)}, u32[]{:S(2)}) collective-permute-start(bf16[1056,128]{1,0:T(8,128)(2,1)S(1)} %scale.1.refs_0_), channel_id=1, source_target_pairs={{0,8},{4,12},{8,16},{12,20},{16,24},{20,28},{24,32},{28,36},{32,40... | collective-permute-start | bytes 811016 | tf_op jit(solution)/shard_map/ppermute | solution.py:292
  31.7 18.7 %collective-permute-start.16 = (bf16[512,512]{1,0:T(8,128)(2,1)S(1)}, bf16[512,512]{1,0:T(8,128)(2,1)S(1)}, u32[]{:S(2)}, u32[]{:S(2)}) collective-permute-start(bf16[512,512]{1,0:T(8,128)(2,1)S(1)} %masked_quarter.1), channel_id=1, source_target_pairs={{0,128},{1,129},{2,130},{3,131},{4,192},{5,193},{6,194},{7,195},{8... | collective-permute-start | bytes 1572872 | tf_op jit(solution)/shard_map/ppermute | solution.py:305
  32.8 18.2 %collective-permute-start.14 = (bf16[512,512]{1,0:T(8,128)(2,1)S(1)}, bf16[512,512]{1,0:T(8,128)(2,1)S(1)}, u32[]{:S(2)}, u32[]{:S(2)}) collective-permute-start(bf16[512,512]{1,0:T(8,128)(2,1)S(1)} %masked_quarter.1), channel_id=1, source_target_pairs={{0,64},{1,65},{2,66},{3,67},{4,0},{5,1},{6,2},{7,3},{8,72},{9,73},... | collective-permute-start | bytes 1572872 | tf_op jit(solution)/shard_map/ppermute | solution.py:305
  37.0 9.6 %collective-permute-start.7 = (bf16[1056,128]{1,0:T(8,128)(2,1)S(1)}, bf16[1056,128]{1,0:T(8,128)(2,1)S(1)}, u32[]{:S(2)}, u32[]{:S(2)}) collective-permute-start(bf16[1056,128]{1,0:T(8,128)(2,1)S(1)} %collective-permute-done.6.refs_4_), channel_id=1, source_target_pairs={{0,56},{4,60},{8,0},{12,4},{16,8},{20,12},{24,16},{28,20},{32,24},... | collective-permute-start | bytes 811016 | tf_op jit(solution)/shard_map/ppermute | solution.py:293
  40.8 9.6 %collective-permute-start.3 = (bf16[1056,128]{1,0:T(8,128)(2,1)S(1)}, bf16[1056,128]{1,0:T(8,128)(2,1)S(1)}, u32[]{:S(2)}, u32[]{:S(2)}) collective-permute-start(bf16[1056,128]{1,0:T(8,128)(2,1)S(1)} %collective-permute-done.2.refs_2_), channel_id=1, source_target_pairs={{0,8},{4,12},{8,16},{12,20},{16,24},{20,28},{24,32},{28,36},{32,40... | collective-permute-start | bytes 811016 | tf_op jit(solution)/shard_map/ppermute | solution.py:292
  40.8 19.8 %collective-permute-start.15 = (bf16[512,512]{1,0:T(8,128)(2,1)S(1)}, bf16[512,512]{1,0:T(8,128)(2,1)S(1)}, u32[]{:S(2)}, u32[]{:S(2)}) collective-permute-start(bf16[512,512]{1,0:T(8,128)(2,1)S(1)} %masked_quarter.1), channel_id=1, source_target_pairs={{0,4},{1,5},{2,6},{3,7},{4,68},{5,69},{6,70},{7,71},{8,12},{9,13},... | collective-permute-start | bytes 1572872 | tf_op jit(solution)/shard_map/ppermute | solution.py:305
  46.6 9.3 %collective-permute-start.8 = (bf16[1056,128]{1,0:T(8,128)(2,1)S(1)}, bf16[1056,128]{1,0:T(8,128)(2,1)S(1)}, u32[]{:S(2)}, u32[]{:S(2)}) collective-permute-start(bf16[1056,128]{1,0:T(8,128)(2,1)S(1)} %collective-permute-done.7.refs_8_), channel_id=1, source_target_pairs={{0,56},{4,60},{8,0},{12,4},{16,8},{20,12},{24,16},{28,20},{32,24},... | collective-permute-start | bytes 811016 | tf_op jit(solution)/shard_map/ppermute | solution.py:293
  50.4 8.8 %collective-permute-start.4 = (bf16[1056,128]{1,0:T(8,128)(2,1)S(1)}, bf16[1056,128]{1,0:T(8,128)(2,1)S(1)}, u32[]{:S(2)}, u32[]{:S(2)}) collective-permute-start(bf16[1056,128]{1,0:T(8,128)(2,1)S(1)} %collective-permute-done.3.refs_6_), channel_id=1, source_target_pairs={{0,8},{4,12},{8,16},{12,20},{16,24},{20,28},{24,32},{28,36},{32,40... | collective-permute-start | bytes 811016 | tf_op jit(solution)/shard_map/ppermute | solution.py:292
  50.5 10.5 %collective-permute-start.18 = (bf16[1056,128]{1,0:T(8,128)(2,1)S(1)}, bf16[1056,128]{1,0:T(8,128)(2,1)S(1)}, u32[]{:S(2)}, u32[]{:S(2)}) collective-permute-start(bf16[1056,128]{1,0:T(8,128)(2,1)S(1)} %scale.1.refs_0_), channel_id=1, source_target_pairs={{0,64},{64,0},{128,192},{192,128},{1,65},{65,1},{129,193},{193,129... | collective-permute-start | bytes 811016 | tf_op jit(solution)/shard_map/ppermute | solution.py:295
  50.9 10.1 %collective-permute-start.20 = (bf16[1056,128]{1,0:T(8,128)(2,1)S(1)}, bf16[1056,128]{1,0:T(8,128)(2,1)S(1)}, u32[]{:S(2)}, u32[]{:S(2)}) collective-permute-start(bf16[1056,128]{1,0:T(8,128)(2,1)S(1)} %collective-permute-done.6.refs_4_), channel_id=1, source_target_pairs={{0,64},{64,0},{128,192},{192,128},{1,65},{65,1},{129,193},{193,129... | collective-permute-start | bytes 811016 | tf_op jit(solution)/shard_map/ppermute | solution.py:295
  56.0 6.5 %collective-permute-start.19 = (bf16[1056,128]{1,0:T(8,128)(2,1)S(1)}, bf16[1056,128]{1,0:T(8,128)(2,1)S(1)}, u32[]{:S(2)}, u32[]{:S(2)}) collective-permute-start(bf16[1056,128]{1,0:T(8,128)(2,1)S(1)} %collective-permute-done.2.refs_2_), channel_id=1, source_target_pairs={{0,64},{64,0},{128,192},{192,128},{1,65},{65,1},{129,193},{193,129... | collective-permute-start | bytes 811016 | tf_op jit(solution)/shard_map/ppermute | solution.py:295
  59.2 4.4 %collective-permute-start.22 = (bf16[1056,128]{1,0:T(8,128)(2,1)S(1)}, bf16[1056,128]{1,0:T(8,128)(2,1)S(1)}, u32[]{:S(2)}, u32[]{:S(2)}) collective-permute-start(bf16[1056,128]{1,0:T(8,128)(2,1)S(1)} %collective-permute-done.7.refs_8_), channel_id=1, source_target_pairs={{0,64},{64,0},{128,192},{192,128},{1,65},{65,1},{129,193},{193,129... | collective-permute-start | bytes 811016 | tf_op jit(solution)/shard_map/ppermute | solution.py:295
  60.6 7.7 %collective-permute-start.21 = (bf16[1056,128]{1,0:T(8,128)(2,1)S(1)}, bf16[1056,128]{1,0:T(8,128)(2,1)S(1)}, u32[]{:S(2)}, u32[]{:S(2)}) collective-permute-start(bf16[1056,128]{1,0:T(8,128)(2,1)S(1)} %collective-permute-done.3.refs_6_), channel_id=1, source_target_pairs={{0,64},{64,0},{128,192},{192,128},{1,65},{65,1},{129,193},{193,129... | collective-permute-start | bytes 811016 | tf_op jit(solution)/shard_map/ppermute | solution.py:295
  60.9 4.8 %collective-permute-start.12 = (bf16[528,128]{1,0:T(8,128)(2,1)S(1)}, bf16[528,128]{1,0:T(8,128)(2,1)S(1)}, u32[]{:S(2)}, u32[]{:S(2)}) collective-permute-start(bf16[528,128]{1,0:T(8,128)(2,1)S(1)} %slice.46), channel_id=1, source_target_pairs={{0,56},{4,60},{8,0},{12,4},{16,8},{20,12},{24,16},{28,20},{32,24},... | collective-permute-start | bytes 405512 | tf_op jit(solution)/shard_map/ppermute | solution.py:293
  61.0 6.0 %collective-permute-start.10 = (bf16[528,128]{1,0:T(8,128)(2,1)S(1)}, bf16[528,128]{1,0:T(8,128)(2,1)S(1)}, u32[]{:S(2)}, u32[]{:S(2)}) collective-permute-start(bf16[528,128]{1,0:T(8,128)(2,1)S(1)} %slice.45), channel_id=1, source_target_pairs={{0,8},{4,12},{8,16},{12,20},{16,24},{20,28},{24,32},{28,36},{32,40... | collective-permute-start | bytes 405512 | tf_op jit(solution)/shard_map/ppermute | solution.py:292
  62.5 10.0 %collective-permute-start.9 = (bf16[1056,128]{1,0:T(8,128)(2,1)S(1)}, bf16[1056,128]{1,0:T(8,128)(2,1)S(1)}, u32[]{:S(2)}, u32[]{:S(2)}) collective-permute-start(bf16[1056,128]{1,0:T(8,128)(2,1)S(1)} %collective-permute-done.8.refs_2_), channel_id=1, source_target_pairs={{0,64},{64,0},{128,192},{192,128},{1,65},{65,1},{129,193},{193,129... | collective-permute-start | bytes 811016 | tf_op jit(solution)/shard_map/ppermute | solution.py:295
  63.6 8.9 %collective-permute-start.5 = (bf16[1056,128]{1,0:T(8,128)(2,1)S(1)}, bf16[1056,128]{1,0:T(8,128)(2,1)S(1)}, u32[]{:S(2)}, u32[]{:S(2)}) collective-permute-start(bf16[1056,128]{1,0:T(8,128)(2,1)S(1)} %collective-permute-done.4.refs_0_), channel_id=1, source_target_pairs={{0,64},{64,0},{128,192},{192,128},{1,65},{65,1},{129,193},{193,129... | collective-permute-start | bytes 811016 | tf_op jit(solution)/shard_map/ppermute | solution.py:295
  65.7 6.7 %collective-permute-start.13 = (bf16[528,128]{1,0:T(8,128)(2,1)S(1)}, bf16[528,128]{1,0:T(8,128)(2,1)S(1)}, u32[]{:S(2)}, u32[]{:S(2)}) collective-permute-start(bf16[528,128]{1,0:T(8,128)(2,1)S(1)} %collective-permute-done.12.refs_6_), channel_id=1, source_target_pairs={{0,64},{64,0},{128,192},{192,128},{1,65},{65,1},{129,193},{193,129... | collective-permute-start | bytes 405512 | tf_op jit(solution)/shard_map/ppermute | solution.py:295
  67.1 5.4 %collective-permute-start.11 = (bf16[528,128]{1,0:T(8,128)(2,1)S(1)}, bf16[528,128]{1,0:T(8,128)(2,1)S(1)}, u32[]{:S(2)}, u32[]{:S(2)}) collective-permute-start(bf16[528,128]{1,0:T(8,128)(2,1)S(1)} %collective-permute-done.10.refs_4_), channel_id=1, source_target_pairs={{0,64},{64,0},{128,192},{192,128},{1,65},{65,1},{129,193},{193,129... | collective-permute-start | bytes 405512 | tf_op jit(solution)/shard_map/ppermute | solution.py:295
  75.6 7.9 %collective-permute-start.24 = (f16[1024,128]{1,0:T(8,128)(2,1)S(1)}, f16[1024,128]{1,0:T(8,128)(2,1)S(1)}, u32[]{:S(2)}, u32[]{:S(2)}) collective-permute-start(f16[1024,128]{1,0:T(8,128)(2,1)S(1)} %get-tuple-element.15), channel_id=1, source_target_pairs={{0,3},{1,0},{2,1},{3,2},{4,7},{5,4},{6,5},{7,6},{8,11},{9,8},{10,9... | collective-permute-start | bytes 786440 | tf_op jit(solution)/shard_map/ppermute | solution.py:317
  75.7 9.1 %collective-permute-start.23 = (f16[1024,128]{1,0:T(8,128)(2,1)S(1)}, f16[1024,128]{1,0:T(8,128)(2,1)S(1)}, u32[]{:S(2)}, u32[]{:S(2)}) collective-permute-start(f16[1024,128]{1,0:T(8,128)(2,1)S(1)} %get-tuple-element.16), channel_id=1, source_target_pairs={{0,1},{1,2},{2,3},{3,0},{4,5},{5,6},{6,7},{7,4},{8,9},{9,10},{10,1... | collective-permute-start | bytes 786440 | tf_op jit(solution)/shard_map/ppermute | solution.py:316
  77.1 12.0 %collective-permute-start.26 = (f16[1024,128]{1,0:T(8,128)(2,1)S(1)}, f16[1024,128]{1,0:T(8,128)(2,1)S(1)}, u32[]{:S(2)}, u32[]{:S(2)}) collective-permute-start(f16[1024,128]{1,0:T(8,128)(2,1)S(1)} %get-tuple-element.13), channel_id=1, source_target_pairs={{0,3},{1,0},{2,1},{3,2},{4,7},{5,4},{6,5},{7,6},{8,11},{9,8},{10,9... | collective-permute-start | bytes 786440 | tf_op jit(solution)/shard_map/ppermute | solution.py:319
  78.4 12.0 %collective-permute-start.27 = (f16[1024,128]{1,0:T(8,128)(2,1)S(1)}, f16[1024,128]{1,0:T(8,128)(2,1)S(1)}, u32[]{:S(2)}, u32[]{:S(2)}) collective-permute-start(f16[1024,128]{1,0:T(8,128)(2,1)S(1)} %get-tuple-element.14), channel_id=1, source_target_pairs={{0,1},{1,2},{2,3},{3,0},{4,5},{5,6},{6,7},{7,4},{8,9},{9,10},{10,1... | collective-permute-start | bytes 786440 | tf_op jit(solution)/shard_map/ppermute | solution.py:318
  85.0 11.1 %collective-permute-start.25 = (f16[1024,128]{1,0:T(8,128)(2,1)S(1)}, f16[1024,128]{1,0:T(8,128)(2,1)S(1)}, u32[]{:S(2)}, u32[]{:S(2)}) collective-permute-start(f16[1024,128]{1,0:T(8,128)(2,1)S(1)} %get-tuple-element.7), channel_id=1, source_target_pairs={{0,1},{1,2},{2,3},{3,0},{4,5},{5,6},{6,7},{7,4},{8,9},{9,10},{10,1... | collective-permute-start | bytes 786440 | tf_op jit(solution)/shard_map/ppermute | solution.py:323
  85.1 11.0 %collective-permute-start.28 = (f16[1024,128]{1,0:T(8,128)(2,1)S(1)}, f16[1024,128]{1,0:T(8,128)(2,1)S(1)}, u32[]{:S(2)}, u32[]{:S(2)}) collective-permute-start(f16[1024,128]{1,0:T(8,128)(2,1)S(1)} %get-tuple-element.8), channel_id=1, source_target_pairs={{0,3},{1,0},{2,1},{3,2},{4,7},{5,4},{6,5},{7,6},{8,11},{9,8},{10,9... | collective-permute-start | bytes 786440 | tf_op jit(solution)/shard_map/ppermute | solution.py:324
  96.4 12.0 %collective-permute-start.29 = (f16[2048,128]{1,0:T(8,128)(2,1)S(1)}, f16[2048,128]{1,0:T(8,128)(2,1)S(1)}, u32[]{:S(2)}, u32[]{:S(2)}) collective-permute-start(f16[2048,128]{1,0:T(8,128)(2,1)S(1)} %pad_maximum_fusion), channel_id=1, source_target_pairs={{0,4},{4,64},{8,12},{12,72},{16,20},{20,80},{24,28},{28,88},{32,36... | collective-permute-start | bytes 1572872 | tf_op jit(solution)/shard_map/ppermute | solution.py:335
  99.5 9.2 %collective-permute-start.32 = (f32[128]{0:T(128)S(1)}, f32[128]{0:T(128)S(1)}, u32[]{:S(2)}, u32[]{:S(2)}) collective-permute-start(f32[128]{0:T(128)S(1)} %multiply_reduce_fusion), channel_id=1, source_target_pairs={{0,196},{4,128},{8,204},{12,136},{16,212},{20,144},{24,220},{28,15... | collective-permute-start | bytes 1544 | tf_op jit(solution)/shard_map/ppermute | solution.py:342
  101.5 7.3 %collective-permute-start.31 = (f32[128]{0:T(128)S(1)}, f32[128]{0:T(128)S(1)}, u32[]{:S(2)}, u32[]{:S(2)}) collective-permute-start(f32[128]{0:T(128)S(1)} %multiply_reduce_fusion), channel_id=1, source_target_pairs={{0,132},{4,192},{8,140},{12,200},{16,148},{20,208},{24,156},{28,21... | collective-permute-start | bytes 1544 | tf_op jit(solution)/shard_map/ppermute | solution.py:342
  101.5 7.3 %collective-permute-start.30 = (f32[128]{0:T(128)S(1)}, f32[128]{0:T(128)S(1)}, u32[]{:S(2)}, u32[]{:S(2)}) collective-permute-start(f32[128]{0:T(128)S(1)} %multiply_reduce_fusion), channel_id=1, source_target_pairs={{0,68},{4,0},{8,76},{12,8},{16,84},{20,16},{24,92},{28,24},{32,100... | collective-permute-start | bytes 1544 | tf_op jit(solution)/shard_map/ppermute | solution.py:342

commit v4 on v3

--- a/solution.py
+++ b/solution.py
@@ -176,9 +176,14 @@
 
 def product_kernel(n_parts, counts, per, again, *refs):
     part_refs = refs[:n_parts]
-    right_ref = refs[n_parts]
-    out_ref = refs[1 + n_parts + again]
-    spots, table, sem = refs[2 + n_parts + again:]
+    if again:
+        right_ref, _, out_ref = refs[n_parts:n_parts + 3]
+    else:
+        quarter_refs, (right_ref, out_ref) = refs[n_parts:-5], refs[-5:-3]
+        for m, ref in enumerate(quarter_refs):
+            height = ref.shape[0]
+            right_ref[m * height:(m + 1) * height, :] = ref[...]
+    spots, table, sem = refs[-3:]
     layer = lax.axis_index("layer")
     n_layer, rows, _ = out_ref.shape
     kt = right_ref.shape[0] // T
@@ -217,16 +222,19 @@
             q += 1
 
 
-def product(parts, counts, per, right, rows, n_layer, total=None):
+def product(parts, counts, per, rights, rows, n_layer, total=None):
     n_parts = len(parts)
-    width = right.shape[1]
     again = total is not None
+    width = rights[0].shape[1]
+    depth = sum(r.shape[0] for r in rights)
     tiles = sum(counts) * per
+    result = pltpu.VMEM((n_layer, rows + T, width // n_layer), jnp.float32)
+    right = pltpu.VMEM((depth, width), jnp.bfloat16)
     return pl.pallas_call(
         functools.partial(product_kernel, n_parts, counts, per, again),
-        out_shape=pltpu.VMEM((n_layer, rows + T, width // n_layer), jnp.float32),
-        in_specs=[VMEM] * (n_parts + 1 + again),
-        out_specs=VMEM,
+        out_shape=result if again else (right, result),
+        in_specs=[VMEM] * (n_parts + len(rights) + again),
+        out_specs=VMEM if again else (VMEM, VMEM),
         scratch_shapes=[
             pltpu.VMEM((8, T), jnp.int32),
             pltpu.SMEM((8, T), jnp.int32),
@@ -236,7 +244,7 @@
         cost_estimate=pl.CostEstimate(flops=2 * tiles * T * T * width, bytes_accessed=2**20, transcendentals=0),
         compiler_params=pltpu.CompilerParams(vmem_limit_bytes=GRANT),
         name="add_product" if again else "product",
-    )(*parts, right, *((total,) if again else ()))
+    )(*parts, *rights, *((total,) if again else ()))
 
 
 def coords(sizes):
@@ -303,11 +311,10 @@
             to = (lo_to * 2 + (hi ^ hi_to ^ lo_to ^ 1), zz * 2 + hi_to, y)
             perm.append((flat(r, c, y, sizes), flat(*to, sizes)))
         rights.append(lax.ppermute(quarter, axes, perm))
-    right = jnp.concatenate(rights)
     early = [p for pair in parts[:2 * last - 3] for p in pair]
     late = [p for pair in parts[2 * last - 3:] for p in pair]
-    out = product(early, [p.shape[0] // half for p in early], per, right, height, n_layer)
-    out = product(late, [p.shape[0] // half for p in late], per, right, height, n_layer, out)
+    right, out = product(early, [p.shape[0] // half for p in early], per, rights, height, n_layer)
+    out = product(late, [p.shape[0] // half for p in late], per, [right], height, n_layer, out)
 
     up = [(y, (y + 1) % n_layer) for y in range(n_layer)]
     down = [(y, (y - 1) % n_layer) for y in range(n_layer)]

time: 110 us -> 114 us (1.036)
  starting transfers between devices: 51 us -> 59.8 us
  waiting for transfers between devices: 36.9 us -> 33.4 us
  blocking collectives: 8.58 us -> 6.48 us
    ppermute x4, waiting for transfers between devices: 12.4 us -> 2 us  [shards(): down = lax.ppermute(down, 'col', ring(-1))]
    ppermute x4, waiting for transfers between devices: 2.9 us -> 9.24 us  [shards(): up = lax.ppermute(up, 'col', ring(1))]
    ppermute x1, waiting for transfers between devices: 4.93 us -> 0.01 us  [shards(): far_b = lax.ppermute(send[1, mid:], 'layer', down)]
    ppermute x1, starting transfers between devices: 0.08 us -> 3.87 us  [shards(): far_b = lax.ppermute(send[1, mid:], 'layer', down)]
    ppermute x1, waiting for transfers between devices: 6.3 us -> 2.74 us  [shards(): lax.ppermute(total, ('row', 'col'), [(r * n_col + c, o[0] * n_col + o[1])...]
    ppermute x1, waiting for transfers between devices: 0.74 us -> 4.09 us  [shards(): mass = lax.ppermute(lax.psum(column_sums(mask, values), 'row'), axes, table)]
    ppermute x3, starting transfers between devices: 2.64 us -> 5.99 us  [shards(): weights.append(lax.ppermute(summand, ('row', 'col'), perm))]
    ppermute x1, waiting for transfers between devices: 1.3 us -> 4.63 us  [shards(): far_a = lax.ppermute(send[1, :mid], 'layer', up)]
  transfers between devices with their start and end apart: 33 -> 33, of which waited for: 14 -> 12; matrix products, arithmetic and copies ran while one was open for 1% -> 1% of each run, Pallas kernels for 5% -> 5%
where the time goes in v4:
time: 114 us
  starting transfers between devices  59.8 us (52%)
  waiting for transfers between devices  33.4 us (29%)
  Pallas kernels  10.5 us (9%)
  blocking collectives  6.48 us (6%)
  other arithmetic  2.42 us (2%)
    ppermute x4, starting transfers between devices, shards(): down = lax.ppermute(down, 'col', ring(-1))  13.5 us
    ppermute x9, starting transfers between devices, shards(): parts = [(p, lax.ppermute(p, 'row', swap)) for p in mine]  9.68 us
    ppermute x4, waiting for transfers between devices, shards(): up = lax.ppermute(up, 'col', ring(1))  9.24 us
    ppermute x4, starting transfers between devices, shards(): rights.append(lax.ppermute(quarter, axes, perm))  9.13 us
    pallas_call x2, Pallas kernels, product(): pl.pallas_call(functools.partial(product_kernel, n_parts, counts, per, ag...  6.9 us
    psum x1, blocking collectives, shards(): mass = lax.ppermute(lax.psum(column_sums(mask, values), 'row'), axes, table)  6.48 us
    ppermute x3, starting transfers between devices, shards(): weights.append(lax.ppermute(summand, ('row', 'col'), perm))  5.99 us
    ppermute x1, waiting for transfers between devices, shards(): up_a = lax.ppermute(up_a, 'layer', up)  5.62 us
  transfers between devices with their start and end apart: 33, of which 12 were waited for; matrix products, arithmetic and copies ran while one was open for 1% of the time, Pallas kernels for 5%

profile of v4, /device:TPU:1, one launch (start us, length us, event | category | flops | bytes accessed | tf_op | source)
XLA Modules:
  0.0 113.8 jit_solution(1853362755018704226)
XLA Ops:
  0.0 2.0 %share.1 = bf16[1056,128]{1,0:T(8,128)(2,1)S(1)} custom-call(s32[4,16]{1,0:T(4,128)} %bitcast.33, bf16[2048,512]{1,0:T(8,128)(2,1)} %values_ref.3), custom_call_target="tpu_custom_call" | custom-call | flops 1048576 | bytes 2097152 | tf_op jit(solution)/shard_map/share/pallas_call | solution.py:74
  2.0 5.6 %collective-permute-start = (bf16[1056,128]{1,0:T(8,128)(2,1)S(1)}, bf16[1056,128]{1,0:T(8,128)(2,1)S(1)}, u32[]{:S(2)}, u32[]{:S(2)}) collective-permute-start(bf16[1056,128]{1,0:T(8,128)(2,1)S(1)} %share.1), channel_id=1, source_target_pairs={{0,8},{1,120},{2,0},{3,64},{4,2},{5,66},{6,10},{7,122},{8,73},{9,1... | collective-permute-start | bytes 811016 | tf_op jit(solution)/shard_map/ppermute | solution.py:285
  7.5 0.7 copy-done.1
  8.2 0.7 masked_quarter.1
  8.9 3.7 %collective-permute-start.19 = (bf16[512,512]{1,0:T(8,128)(2,1)S(1)}, bf16[512,512]{1,0:T(8,128)(2,1)S(1)}, u32[]{:S(2)}, u32[]{:S(2)}) collective-permute-start(bf16[512,512]{1,0:T(8,128)(2,1)S(1)} %masked_quarter.1), channel_id=1, source_target_pairs={{0,64},{1,65},{2,66},{3,67},{4,0},{5,1},{6,2},{7,3},{8,72},{9,73},... | collective-permute-start | bytes 1572872 | tf_op jit(solution)/shard_map/ppermute | solution.py:313
  12.6 0.9 column_sums.1
  13.5 6.5 %psum.7 = f32[4,128]{1,0:T(4,128)S(1)} all-reduce(f32[4,128]{1,0:T(4,128)S(1)} %column_sums.1), channel_id=1, replica_groups=mesh['row'=4,'col'=16,'layer'=4] {'row'}, use_global_device_ids=true, to_apply=%region_0.0 | all-reduce | flops 512 | bytes 4096 | tf_op jit(solution)/shard_map/psum | solution.py:286
  20.0 2.9 %collective-permute-start.1 = (f32[4,128]{1,0:T(4,128)S(1)}, f32[4,128]{1,0:T(4,128)S(1)}, u32[]{:S(2)}, u32[]{:S(2)}) collective-permute-start(f32[4,128]{1,0:T(4,128)S(1)} %psum.7), channel_id=1, source_target_pairs={{0,8},{1,120},{2,0},{3,64},{4,2},{5,66},{6,10},{7,122},{8,73},{9,1... | collective-permute-start | bytes 6152 | tf_op jit(solution)/shard_map/ppermute | solution.py:286
  22.9 4.1 %collective-permute-done.1.mass_ref = f32[4,128]{1,0:T(4,128)S(1)} collective-permute-done((f32[4,128]{1,0:T(4,128)S(1)}, f32[4,128]{1,0:T(4,128)S(1)}, u32[]{:S(2)}, u32[]{:S(2)}) %collective-permute-start.1) | collective-permute-done | bytes 2080 | tf_op jit(solution)/shard_map/ppermute | solution.py:286
  27.2 4.6 %collective-permute-start.6 = (bf16[1056,128]{1,0:T(8,128)(2,1)S(1)}, bf16[1056,128]{1,0:T(8,128)(2,1)S(1)}, u32[]{:S(2)}, u32[]{:S(2)}) collective-permute-start(bf16[1056,128]{1,0:T(8,128)(2,1)S(1)} %scale.1.refs_0_), channel_id=1, source_target_pairs={{0,56},{4,60},{8,0},{12,4},{16,8},{20,12},{24,16},{28,20},{32,24},... | collective-permute-start | bytes 811016 | tf_op jit(solution)/shard_map/ppermute | solution.py:301
  31.8 5.4 %collective-permute-done.2.refs_2_ = bf16[1056,128]{1,0:T(8,128)(2,1)S(1)} collective-permute-done((bf16[1056,128]{1,0:T(8,128)(2,1)S(1)}, bf16[1056,128]{1,0:T(8,128)(2,1)S(1)}, u32[]{:S(2)}, u32[]{:S(2)}) %collective-permute-start.2) | collective-permute-done | bytes 270368 | tf_op jit(solution)/shard_map/ppermute | solution.py:300
  37.2 0.7 collective-permute-start.20
  37.9 4.8 %collective-permute-start.21 = (bf16[512,512]{1,0:T(8,128)(2,1)S(1)}, bf16[512,512]{1,0:T(8,128)(2,1)S(1)}, u32[]{:S(2)}, u32[]{:S(2)}) collective-permute-start(bf16[512,512]{1,0:T(8,128)(2,1)S(1)} %masked_quarter.1), channel_id=1, source_target_pairs={{0,128},{1,129},{2,130},{3,131},{4,192},{5,193},{6,194},{7,195},{8... | collective-permute-start | bytes 1572872 | tf_op jit(solution)/shard_map/ppermute | solution.py:313
  42.6 2.7 %collective-permute-start.7 = (bf16[1056,128]{1,0:T(8,128)(2,1)S(1)}, bf16[1056,128]{1,0:T(8,128)(2,1)S(1)}, u32[]{:S(2)}, u32[]{:S(2)}) collective-permute-start(bf16[1056,128]{1,0:T(8,128)(2,1)S(1)} %collective-permute-done.6.refs_4_), channel_id=1, source_target_pairs={{0,56},{4,60},{8,0},{12,4},{16,8},{20,12},{24,16},{28,20},{32,24},... | collective-permute-start | bytes 811016 | tf_op jit(solution)/shard_map/ppermute | solution.py:301
  45.4 1.4 %collective-permute-done.3.refs_6_ = bf16[1056,128]{1,0:T(8,128)(2,1)S(1)} collective-permute-done((bf16[1056,128]{1,0:T(8,128)(2,1)S(1)}, bf16[1056,128]{1,0:T(8,128)(2,1)S(1)}, u32[]{:S(2)}, u32[]{:S(2)}) %collective-permute-start.3) | collective-permute-done | bytes 270368 | tf_op jit(solution)/shard_map/ppermute | solution.py:300
  46.8 2.0 %collective-permute-done.7.refs_8_ = bf16[1056,128]{1,0:T(8,128)(2,1)S(1)} collective-permute-done((bf16[1056,128]{1,0:T(8,128)(2,1)S(1)}, bf16[1056,128]{1,0:T(8,128)(2,1)S(1)}, u32[]{:S(2)}, u32[]{:S(2)}) %collective-permute-start.7) | collective-permute-done | bytes 270368 | tf_op jit(solution)/shard_map/ppermute | solution.py:301
  48.8 3.5 %collective-permute-start.8 = (bf16[1056,128]{1,0:T(8,128)(2,1)S(1)}, bf16[1056,128]{1,0:T(8,128)(2,1)S(1)}, u32[]{:S(2)}, u32[]{:S(2)}) collective-permute-start(bf16[1056,128]{1,0:T(8,128)(2,1)S(1)} %collective-permute-done.7.refs_8_), channel_id=1, source_target_pairs={{0,56},{4,60},{8,0},{12,4},{16,8},{20,12},{24,16},{28,20},{32,24},... | collective-permute-start | bytes 811016 | tf_op jit(solution)/shard_map/ppermute | solution.py:301
  52.3 3.5 %collective-permute-start.14 = (bf16[1056,128]{1,0:T(8,128)(2,1)S(1)}, bf16[1056,128]{1,0:T(8,128)(2,1)S(1)}, u32[]{:S(2)}, u32[]{:S(2)}) collective-permute-start(bf16[1056,128]{1,0:T(8,128)(2,1)S(1)} %scale.1.refs_0_), channel_id=1, source_target_pairs={{0,64},{64,0},{128,192},{192,128},{1,65},{65,1},{129,193},{193,129... | collective-permute-start | bytes 811016 | tf_op jit(solution)/shard_map/ppermute | solution.py:303
  55.8 2.3 %collective-permute-done.21.refs_12_ = bf16[512,512]{1,0:T(8,128)(2,1)S(1)} collective-permute-done((bf16[512,512]{1,0:T(8,128)(2,1)S(1)}, bf16[512,512]{1,0:T(8,128)(2,1)S(1)}, u32[]{:S(2)}, u32[]{:S(2)}) %collective-permute-start.21) | collective-permute-done | bytes 524320 | tf_op jit(solution)/shard_map/ppermute | solution.py:313
  58.0 3.6 %collective-permute-start.15 = (bf16[1056,128]{1,0:T(8,128)(2,1)S(1)}, bf16[1056,128]{1,0:T(8,128)(2,1)S(1)}, u32[]{:S(2)}, u32[]{:S(2)}) collective-permute-start(bf16[1056,128]{1,0:T(8,128)(2,1)S(1)} %collective-permute-done.2.refs_2_), channel_id=1, source_target_pairs={{0,64},{64,0},{128,192},{192,128},{1,65},{65,1},{129,193},{193,129... | collective-permute-start | bytes 811016 | tf_op jit(solution)/shard_map/ppermute | solution.py:303
  61.6 0.5 collective-permute-start.17
  62.1 0.3 collective-permute-start.18
  62.5 0.3 collective-permute-start.10
  62.8 2.7 %collective-permute-start.12 = (bf16[528,128]{1,0:T(8,128)(2,1)S(1)}, bf16[528,128]{1,0:T(8,128)(2,1)S(1)}, u32[]{:S(2)}, u32[]{:S(2)}) collective-permute-start(bf16[528,128]{1,0:T(8,128)(2,1)S(1)} %slice.46), channel_id=1, source_target_pairs={{0,56},{4,60},{8,0},{12,4},{16,8},{20,12},{24,16},{28,20},{32,24},... | collective-permute-start | bytes 405512 | tf_op jit(solution)/shard_map/ppermute | solution.py:301
  65.5 0.7 collective-permute-start.5
  66.2 2.4 %collective-permute-done.10.refs_4_ = bf16[528,128]{1,0:T(8,128)(2,1)S(1)} collective-permute-done((bf16[528,128]{1,0:T(8,128)(2,1)S(1)}, bf16[528,128]{1,0:T(8,128)(2,1)S(1)}, u32[]{:S(2)}, u32[]{:S(2)}) %collective-permute-start.10) | collective-permute-done | bytes 135200 | tf_op jit(solution)/shard_map/ppermute | solution.py:300
  68.6 1.1 collective-permute-start.11
  69.8 4.3 %product.1 = (bf16[2048,512]{1,0:T(8,128)(2,1)S(1)}, f32[4,2176,128]{2,1,0:T(8,128)S(1)}) custom-call(bf16[1056,128]{1,0:T(8,128)(2,1)S(1)} %scale.1.refs_0_, bf16[1056,128]{1,0:T(8,128)(2,1)S(1)} %collective-permute-done.14.refs_1_, bf16[1056,128]{1,0:T(8,128)(2,1)S(1)} %collective-permute-done.2.refs_2_, ...), custom_call_target="tpu_custom_call" | custom-call | flops 1342177280 | bytes 1048576 | tf_op jit(solution)/shard_map/product/pallas_call | solution.py:233
  74.1 2.6 %add_product.1 = f32[4,2176,128]{2,1,0:T(8,128)S(1)} custom-call(bf16[1056,128]{1,0:T(8,128)(2,1)S(1)} %collective-permute-done.4.refs_0_, bf16[1056,128]{1,0:T(8,128)(2,1)S(1)} %collective-permute-done.5.refs_1_, bf16[1056,128]{1,0:T(8,128)(2,1)S(1)} %collective-permute-done.8.refs_2_, ...), custom_call_target="tpu_custom_call", output_to_operand_aliasing={{}: (9, {})} | custom-call | flops 805306368 | bytes 1048576 | tf_op jit(solution)/shard_map/add_product/pallas_call | solution.py:233
  76.9 0.2 slice_bitcast_fusion.5
  77.1 1.6 %collective-permute-start.23 = (f16[1024,128]{1,0:T(8,128)(2,1)S(1)}, f16[1024,128]{1,0:T(8,128)(2,1)S(1)}, u32[]{:S(2)}, u32[]{:S(2)}) collective-permute-start(f16[1024,128]{1,0:T(8,128)(2,1)S(1)} %get-tuple-element.20), channel_id=1, source_target_pairs={{0,1},{1,2},{2,3},{3,0},{4,5},{5,6},{6,7},{7,4},{8,9},{9,10},{10,1... | collective-permute-start | bytes 786440 | tf_op jit(solution)/shard_map/ppermute | solution.py:323
  78.7 3.9 %collective-permute-start.24 = (f16[1024,128]{1,0:T(8,128)(2,1)S(1)}, f16[1024,128]{1,0:T(8,128)(2,1)S(1)}, u32[]{:S(2)}, u32[]{:S(2)}) collective-permute-start(f16[1024,128]{1,0:T(8,128)(2,1)S(1)} %get-tuple-element.19), channel_id=1, source_target_pairs={{0,3},{1,0},{2,1},{3,2},{4,7},{5,4},{6,5},{7,6},{8,11},{9,8},{10,9... | collective-permute-start | bytes 786440 | tf_op jit(solution)/shard_map/ppermute | solution.py:324
  82.6 1.4 %collective-permute-start.26 = (f16[1024,128]{1,0:T(8,128)(2,1)S(1)}, f16[1024,128]{1,0:T(8,128)(2,1)S(1)}, u32[]{:S(2)}, u32[]{:S(2)}) collective-permute-start(f16[1024,128]{1,0:T(8,128)(2,1)S(1)} %get-tuple-element.17), channel_id=1, source_target_pairs={{0,3},{1,0},{2,1},{3,2},{4,7},{5,4},{6,5},{7,6},{8,11},{9,8},{10,9... | collective-permute-start | bytes 786440 | tf_op jit(solution)/shard_map/ppermute | solution.py:326
  84.1 4.6 %collective-permute-done.23 = f16[1024,128]{1,0:T(8,128)(2,1)S(1)} collective-permute-done((f16[1024,128]{1,0:T(8,128)(2,1)S(1)}, f16[1024,128]{1,0:T(8,128)(2,1)S(1)}, u32[]{:S(2)}, u32[]{:S(2)}) %collective-permute-start.23) | collective-permute-done | bytes 262176 | tf_op jit(solution)/shard_map/ppermute | solution.py:323
  88.9 0.7 collective-permute-start.25
  89.6 2.1 %collective-permute-start.28 = (f16[1024,128]{1,0:T(8,128)(2,1)S(1)}, f16[1024,128]{1,0:T(8,128)(2,1)S(1)}, u32[]{:S(2)}, u32[]{:S(2)}) collective-permute-start(f16[1024,128]{1,0:T(8,128)(2,1)S(1)} %get-tuple-element.12), channel_id=1, source_target_pairs={{0,3},{1,0},{2,1},{3,2},{4,7},{5,4},{6,5},{7,6},{8,11},{9,8},{10,9... | collective-permute-start | bytes 786440 | tf_op jit(solution)/shard_map/ppermute | solution.py:331
  91.7 1.8 %collective-permute-done.26 = f16[1024,128]{1,0:T(8,128)(2,1)S(1)} collective-permute-done((f16[1024,128]{1,0:T(8,128)(2,1)S(1)}, f16[1024,128]{1,0:T(8,128)(2,1)S(1)}, u32[]{:S(2)}, u32[]{:S(2)}) %collective-permute-start.26) | collective-permute-done | bytes 262176 | tf_op jit(solution)/shard_map/ppermute | solution.py:326
  93.4 0.9 collective-permute-done.27
  94.3 5.6 %collective-permute-done.25 = f16[1024,128]{1,0:T(8,128)(2,1)S(1)} collective-permute-done((f16[1024,128]{1,0:T(8,128)(2,1)S(1)}, f16[1024,128]{1,0:T(8,128)(2,1)S(1)}, u32[]{:S(2)}, u32[]{:S(2)}) %collective-permute-start.25) | collective-permute-done | bytes 262176 | tf_op jit(solution)/shard_map/ppermute | solution.py:330
  100.0 0.2 fusion.8
  100.3 3.0 %collective-permute-start.29 = (f16[2048,128]{1,0:T(8,128)(2,1)S(1)}, f16[2048,128]{1,0:T(8,128)(2,1)S(1)}, u32[]{:S(2)}, u32[]{:S(2)}) collective-permute-start(f16[2048,128]{1,0:T(8,128)(2,1)S(1)} %pad_maximum_fusion), channel_id=1, source_target_pairs={{0,4},{4,64},{8,12},{12,72},{16,20},{20,80},{24,28},{28,88},{32,36... | collective-permute-start | bytes 1572872 | tf_op jit(solution)/shard_map/ppermute | solution.py:342
  103.3 0.3 multiply_reduce_fusion
  103.6 0.7 collective-permute-start.30
  104.3 4.0 %collective-permute-start.31 = (f32[128]{0:T(128)S(1)}, f32[128]{0:T(128)S(1)}, u32[]{:S(2)}, u32[]{:S(2)}) collective-permute-start(f32[128]{0:T(128)S(1)} %multiply_reduce_fusion), channel_id=1, source_target_pairs={{0,132},{4,192},{8,140},{12,200},{16,148},{20,208},{24,156},{28,21... | collective-permute-start | bytes 1544 | tf_op jit(solution)/shard_map/ppermute | solution.py:349
  108.3 1.3 %collective-permute-start.32 = (f32[128]{0:T(128)S(1)}, f32[128]{0:T(128)S(1)}, u32[]{:S(2)}, u32[]{:S(2)}) collective-permute-start(f32[128]{0:T(128)S(1)} %multiply_reduce_fusion), channel_id=1, source_target_pairs={{0,196},{4,128},{8,204},{12,136},{16,212},{20,144},{24,220},{28,15... | collective-permute-start | bytes 1544 | tf_op jit(solution)/shard_map/ppermute | solution.py:349
  109.6 2.7 %collective-permute-done.29 = f16[2048,128]{1,0:T(8,128)(2,1)S(1)} collective-permute-done((f16[2048,128]{1,0:T(8,128)(2,1)S(1)}, f16[2048,128]{1,0:T(8,128)(2,1)S(1)}, u32[]{:S(2)}, u32[]{:S(2)}) %collective-permute-start.29) | collective-permute-done | bytes 524320 | tf_op jit(solution)/shard_map/ppermute | solution.py:342
  112.3 0.3 fusion
  112.7 1.1 multiply_divide_fusion
  (40 shorter events, 1.0 us)
Async XLA Ops:
  0.0 7.5 %copy-start = (bf16[2048,512]{1,0:T(8,128)(2,1)S(1)}, bf16[2048,512]{1,0:T(8,128)(2,1)}, u32[]{:S(2)}) copy-start(bf16[2048,512]{1,0:T(8,128)(2,1)} %values_ref.3) | copy-start | bytes 6291460
  2.0 25.0 %collective-permute-start = (bf16[1056,128]{1,0:T(8,128)(2,1)S(1)}, bf16[1056,128]{1,0:T(8,128)(2,1)S(1)}, u32[]{:S(2)}, u32[]{:S(2)}) collective-permute-start(bf16[1056,128]{1,0:T(8,128)(2,1)S(1)} %share.1), channel_id=1, source_target_pairs={{0,8},{1,120},{2,0},{3,64},{4,2},{5,66},{6,10},{7,122},{8,73},{9,1... | collective-permute-start | bytes 811016 | tf_op jit(solution)/shard_map/ppermute | solution.py:285
  7.5 0.7 copy-start.1
  8.9 33.7 %collective-permute-start.19 = (bf16[512,512]{1,0:T(8,128)(2,1)S(1)}, bf16[512,512]{1,0:T(8,128)(2,1)S(1)}, u32[]{:S(2)}, u32[]{:S(2)}) collective-permute-start(bf16[512,512]{1,0:T(8,128)(2,1)S(1)} %masked_quarter.1), channel_id=1, source_target_pairs={{0,64},{1,65},{2,66},{3,67},{4,0},{5,1},{6,2},{7,3},{8,72},{9,73},... | collective-permute-start | bytes 1572872 | tf_op jit(solution)/shard_map/ppermute | solution.py:313
  20.0 7.0 %collective-permute-start.1 = (f32[4,128]{1,0:T(4,128)S(1)}, f32[4,128]{1,0:T(4,128)S(1)}, u32[]{:S(2)}, u32[]{:S(2)}) collective-permute-start(f32[4,128]{1,0:T(4,128)S(1)} %psum.7), channel_id=1, source_target_pairs={{0,8},{1,120},{2,0},{3,64},{4,2},{5,66},{6,10},{7,122},{8,73},{9,1... | collective-permute-start | bytes 6152 | tf_op jit(solution)/shard_map/ppermute | solution.py:286
  27.1 10.1 %collective-permute-start.2 = (bf16[1056,128]{1,0:T(8,128)(2,1)S(1)}, bf16[1056,128]{1,0:T(8,128)(2,1)S(1)}, u32[]{:S(2)}, u32[]{:S(2)}) collective-permute-start(bf16[1056,128]{1,0:T(8,128)(2,1)S(1)} %scale.1.refs_0_), channel_id=1, source_target_pairs={{0,8},{4,12},{8,16},{12,20},{16,24},{20,28},{24,32},{28,36},{32,40... | collective-permute-start | bytes 811016 | tf_op jit(solution)/shard_map/ppermute | solution.py:300
  27.2 15.5 %collective-permute-start.6 = (bf16[1056,128]{1,0:T(8,128)(2,1)S(1)}, bf16[1056,128]{1,0:T(8,128)(2,1)S(1)}, u32[]{:S(2)}, u32[]{:S(2)}) collective-permute-start(bf16[1056,128]{1,0:T(8,128)(2,1)S(1)} %scale.1.refs_0_), channel_id=1, source_target_pairs={{0,56},{4,60},{8,0},{12,4},{16,8},{20,12},{24,16},{28,20},{32,24},... | collective-permute-start | bytes 811016 | tf_op jit(solution)/shard_map/ppermute | solution.py:301
  37.2 9.6 %collective-permute-start.3 = (bf16[1056,128]{1,0:T(8,128)(2,1)S(1)}, bf16[1056,128]{1,0:T(8,128)(2,1)S(1)}, u32[]{:S(2)}, u32[]{:S(2)}) collective-permute-start(bf16[1056,128]{1,0:T(8,128)(2,1)S(1)} %collective-permute-done.2.refs_2_), channel_id=1, source_target_pairs={{0,8},{4,12},{8,16},{12,20},{16,24},{20,28},{24,32},{28,36},{32,40... | collective-permute-start | bytes 811016 | tf_op jit(solution)/shard_map/ppermute | solution.py:300
  37.2 15.1 %collective-permute-start.20 = (bf16[512,512]{1,0:T(8,128)(2,1)S(1)}, bf16[512,512]{1,0:T(8,128)(2,1)S(1)}, u32[]{:S(2)}, u32[]{:S(2)}) collective-permute-start(bf16[512,512]{1,0:T(8,128)(2,1)S(1)} %masked_quarter.1), channel_id=1, source_target_pairs={{0,4},{1,5},{2,6},{3,7},{4,68},{5,69},{6,70},{7,71},{8,12},{9,13},... | collective-permute-start | bytes 1572872 | tf_op jit(solution)/shard_map/ppermute | solution.py:313
  37.9 20.2 %collective-permute-start.21 = (bf16[512,512]{1,0:T(8,128)(2,1)S(1)}, bf16[512,512]{1,0:T(8,128)(2,1)S(1)}, u32[]{:S(2)}, u32[]{:S(2)}) collective-permute-start(bf16[512,512]{1,0:T(8,128)(2,1)S(1)} %masked_quarter.1), channel_id=1, source_target_pairs={{0,128},{1,129},{2,130},{3,131},{4,192},{5,193},{6,194},{7,195},{8... | collective-permute-start | bytes 1572872 | tf_op jit(solution)/shard_map/ppermute | solution.py:313
  42.6 19.0 %collective-permute-start.22 = (bf16[512,512]{1,0:T(8,128)(2,1)S(1)}, bf16[512,512]{1,0:T(8,128)(2,1)S(1)}, u32[]{:S(2)}, u32[]{:S(2)}) collective-permute-start(bf16[512,512]{1,0:T(8,128)(2,1)S(1)} %masked_quarter.1), channel_id=1, source_target_pairs={{0,196},{1,197},{2,198},{3,199},{4,132},{5,133},{6,134},{7,135},{8... | collective-permute-start | bytes 1572872 | tf_op jit(solution)/shard_map/ppermute | solution.py:313
  42.6 6.2 %collective-permute-start.7 = (bf16[1056,128]{1,0:T(8,128)(2,1)S(1)}, bf16[1056,128]{1,0:T(8,128)(2,1)S(1)}, u32[]{:S(2)}, u32[]{:S(2)}) collective-permute-start(bf16[1056,128]{1,0:T(8,128)(2,1)S(1)} %collective-permute-done.6.refs_4_), channel_id=1, source_target_pairs={{0,56},{4,60},{8,0},{12,4},{16,8},{20,12},{24,16},{28,20},{32,24},... | collective-permute-start | bytes 811016 | tf_op jit(solution)/shard_map/ppermute | solution.py:301
  46.8 14.8 %collective-permute-start.4 = (bf16[1056,128]{1,0:T(8,128)(2,1)S(1)}, bf16[1056,128]{1,0:T(8,128)(2,1)S(1)}, u32[]{:S(2)}, u32[]{:S(2)}) collective-permute-start(bf16[1056,128]{1,0:T(8,128)(2,1)S(1)} %collective-permute-done.3.refs_6_), channel_id=1, source_target_pairs={{0,8},{4,12},{8,16},{12,20},{16,24},{20,28},{24,32},{28,36},{32,40... | collective-permute-start | bytes 811016 | tf_op jit(solution)/shard_map/ppermute | solution.py:300
  48.8 13.4 %collective-permute-start.8 = (bf16[1056,128]{1,0:T(8,128)(2,1)S(1)}, bf16[1056,128]{1,0:T(8,128)(2,1)S(1)}, u32[]{:S(2)}, u32[]{:S(2)}) collective-permute-start(bf16[1056,128]{1,0:T(8,128)(2,1)S(1)} %collective-permute-done.7.refs_8_), channel_id=1, source_target_pairs={{0,56},{4,60},{8,0},{12,4},{16,8},{20,12},{24,16},{28,20},{32,24},... | collective-permute-start | bytes 811016 | tf_op jit(solution)/shard_map/ppermute | solution.py:301
  52.3 10.1 %collective-permute-start.14 = (bf16[1056,128]{1,0:T(8,128)(2,1)S(1)}, bf16[1056,128]{1,0:T(8,128)(2,1)S(1)}, u32[]{:S(2)}, u32[]{:S(2)}) collective-permute-start(bf16[1056,128]{1,0:T(8,128)(2,1)S(1)} %scale.1.refs_0_), channel_id=1, source_target_pairs={{0,64},{64,0},{128,192},{192,128},{1,65},{65,1},{129,193},{193,129... | collective-permute-start | bytes 811016 | tf_op jit(solution)/shard_map/ppermute | solution.py:303
  58.0 4.7 %collective-permute-start.15 = (bf16[1056,128]{1,0:T(8,128)(2,1)S(1)}, bf16[1056,128]{1,0:T(8,128)(2,1)S(1)}, u32[]{:S(2)}, u32[]{:S(2)}) collective-permute-start(bf16[1056,128]{1,0:T(8,128)(2,1)S(1)} %collective-permute-done.2.refs_2_), channel_id=1, source_target_pairs={{0,64},{64,0},{128,192},{192,128},{1,65},{65,1},{129,193},{193,129... | collective-permute-start | bytes 811016 | tf_op jit(solution)/shard_map/ppermute | solution.py:303
  61.6 3.8 %collective-permute-start.16 = (bf16[1056,128]{1,0:T(8,128)(2,1)S(1)}, bf16[1056,128]{1,0:T(8,128)(2,1)S(1)}, u32[]{:S(2)}, u32[]{:S(2)}) collective-permute-start(bf16[1056,128]{1,0:T(8,128)(2,1)S(1)} %collective-permute-done.6.refs_4_), channel_id=1, source_target_pairs={{0,64},{64,0},{128,192},{192,128},{1,65},{65,1},{129,193},{193,129... | collective-permute-start | bytes 811016 | tf_op jit(solution)/shard_map/ppermute | solution.py:303
  61.6 4.5 %collective-permute-start.17 = (bf16[1056,128]{1,0:T(8,128)(2,1)S(1)}, bf16[1056,128]{1,0:T(8,128)(2,1)S(1)}, u32[]{:S(2)}, u32[]{:S(2)}) collective-permute-start(bf16[1056,128]{1,0:T(8,128)(2,1)S(1)} %collective-permute-done.3.refs_6_), channel_id=1, source_target_pairs={{0,64},{64,0},{128,192},{192,128},{1,65},{65,1},{129,193},{193,129... | collective-permute-start | bytes 811016 | tf_op jit(solution)/shard_map/ppermute | solution.py:303
  62.1 7.6 %collective-permute-start.18 = (bf16[1056,128]{1,0:T(8,128)(2,1)S(1)}, bf16[1056,128]{1,0:T(8,128)(2,1)S(1)}, u32[]{:S(2)}, u32[]{:S(2)}) collective-permute-start(bf16[1056,128]{1,0:T(8,128)(2,1)S(1)} %collective-permute-done.7.refs_8_), channel_id=1, source_target_pairs={{0,64},{64,0},{128,192},{192,128},{1,65},{65,1},{129,193},{193,129... | collective-permute-start | bytes 811016 | tf_op jit(solution)/shard_map/ppermute | solution.py:303
  62.5 6.2 %collective-permute-start.10 = (bf16[528,128]{1,0:T(8,128)(2,1)S(1)}, bf16[528,128]{1,0:T(8,128)(2,1)S(1)}, u32[]{:S(2)}, u32[]{:S(2)}) collective-permute-start(bf16[528,128]{1,0:T(8,128)(2,1)S(1)} %slice.45), channel_id=1, source_target_pairs={{0,8},{4,12},{8,16},{12,20},{16,24},{20,28},{24,32},{28,36},{32,40... | collective-permute-start | bytes 405512 | tf_op jit(solution)/shard_map/ppermute | solution.py:300
  62.8 7.0 %collective-permute-start.12 = (bf16[528,128]{1,0:T(8,128)(2,1)S(1)}, bf16[528,128]{1,0:T(8,128)(2,1)S(1)}, u32[]{:S(2)}, u32[]{:S(2)}) collective-permute-start(bf16[528,128]{1,0:T(8,128)(2,1)S(1)} %slice.46), channel_id=1, source_target_pairs={{0,56},{4,60},{8,0},{12,4},{16,8},{20,12},{24,16},{28,20},{32,24},... | collective-permute-start | bytes 405512 | tf_op jit(solution)/shard_map/ppermute | solution.py:301
  65.5 8.6 %collective-permute-start.5 = (bf16[1056,128]{1,0:T(8,128)(2,1)S(1)}, bf16[1056,128]{1,0:T(8,128)(2,1)S(1)}, u32[]{:S(2)}, u32[]{:S(2)}) collective-permute-start(bf16[1056,128]{1,0:T(8,128)(2,1)S(1)} %collective-permute-done.4.refs_0_), channel_id=1, source_target_pairs={{0,64},{64,0},{128,192},{192,128},{1,65},{65,1},{129,193},{193,129... | collective-permute-start | bytes 811016 | tf_op jit(solution)/shard_map/ppermute | solution.py:303
  66.1 8.0 %collective-permute-start.9 = (bf16[1056,128]{1,0:T(8,128)(2,1)S(1)}, bf16[1056,128]{1,0:T(8,128)(2,1)S(1)}, u32[]{:S(2)}, u32[]{:S(2)}) collective-permute-start(bf16[1056,128]{1,0:T(8,128)(2,1)S(1)} %collective-permute-done.8.refs_2_), channel_id=1, source_target_pairs={{0,64},{64,0},{128,192},{192,128},{1,65},{65,1},{129,193},{193,129... | collective-permute-start | bytes 811016 | tf_op jit(solution)/shard_map/ppermute | solution.py:303
  68.6 5.4 %collective-permute-start.11 = (bf16[528,128]{1,0:T(8,128)(2,1)S(1)}, bf16[528,128]{1,0:T(8,128)(2,1)S(1)}, u32[]{:S(2)}, u32[]{:S(2)}) collective-permute-start(bf16[528,128]{1,0:T(8,128)(2,1)S(1)} %collective-permute-done.10.refs_4_), channel_id=1, source_target_pairs={{0,64},{64,0},{128,192},{192,128},{1,65},{65,1},{129,193},{193,129... | collective-permute-start | bytes 405512 | tf_op jit(solution)/shard_map/ppermute | solution.py:303
  69.7 4.3 %collective-permute-start.13 = (bf16[528,128]{1,0:T(8,128)(2,1)S(1)}, bf16[528,128]{1,0:T(8,128)(2,1)S(1)}, u32[]{:S(2)}, u32[]{:S(2)}) collective-permute-start(bf16[528,128]{1,0:T(8,128)(2,1)S(1)} %collective-permute-done.12.refs_6_), channel_id=1, source_target_pairs={{0,64},{64,0},{128,192},{192,128},{1,65},{65,1},{129,193},{193,129... | collective-permute-start | bytes 405512 | tf_op jit(solution)/shard_map/ppermute | solution.py:303
  77.1 11.6 %collective-permute-start.23 = (f16[1024,128]{1,0:T(8,128)(2,1)S(1)}, f16[1024,128]{1,0:T(8,128)(2,1)S(1)}, u32[]{:S(2)}, u32[]{:S(2)}) collective-permute-start(f16[1024,128]{1,0:T(8,128)(2,1)S(1)} %get-tuple-element.20), channel_id=1, source_target_pairs={{0,1},{1,2},{2,3},{3,0},{4,5},{5,6},{6,7},{7,4},{8,9},{9,10},{10,1... | collective-permute-start | bytes 786440 | tf_op jit(solution)/shard_map/ppermute | solution.py:323
  78.7 10.0 %collective-permute-start.24 = (f16[1024,128]{1,0:T(8,128)(2,1)S(1)}, f16[1024,128]{1,0:T(8,128)(2,1)S(1)}, u32[]{:S(2)}, u32[]{:S(2)}) collective-permute-start(f16[1024,128]{1,0:T(8,128)(2,1)S(1)} %get-tuple-element.19), channel_id=1, source_target_pairs={{0,3},{1,0},{2,1},{3,2},{4,7},{5,4},{6,5},{7,6},{8,11},{9,8},{10,9... | collective-permute-start | bytes 786440 | tf_op jit(solution)/shard_map/ppermute | solution.py:324
  82.6 10.8 %collective-permute-start.26 = (f16[1024,128]{1,0:T(8,128)(2,1)S(1)}, f16[1024,128]{1,0:T(8,128)(2,1)S(1)}, u32[]{:S(2)}, u32[]{:S(2)}) collective-permute-start(f16[1024,128]{1,0:T(8,128)(2,1)S(1)} %get-tuple-element.17), channel_id=1, source_target_pairs={{0,3},{1,0},{2,1},{3,2},{4,7},{5,4},{6,5},{7,6},{8,11},{9,8},{10,9... | collective-permute-start | bytes 786440 | tf_op jit(solution)/shard_map/ppermute | solution.py:326
  84.0 10.3 %collective-permute-start.27 = (f16[1024,128]{1,0:T(8,128)(2,1)S(1)}, f16[1024,128]{1,0:T(8,128)(2,1)S(1)}, u32[]{:S(2)}, u32[]{:S(2)}) collective-permute-start(f16[1024,128]{1,0:T(8,128)(2,1)S(1)} %get-tuple-element.18), channel_id=1, source_target_pairs={{0,1},{1,2},{2,3},{3,0},{4,5},{5,6},{6,7},{7,4},{8,9},{9,10},{10,1... | collective-permute-start | bytes 786440 | tf_op jit(solution)/shard_map/ppermute | solution.py:325
  88.9 11.1 %collective-permute-start.25 = (f16[1024,128]{1,0:T(8,128)(2,1)S(1)}, f16[1024,128]{1,0:T(8,128)(2,1)S(1)}, u32[]{:S(2)}, u32[]{:S(2)}) collective-permute-start(f16[1024,128]{1,0:T(8,128)(2,1)S(1)} %get-tuple-element.11), channel_id=1, source_target_pairs={{0,1},{1,2},{2,3},{3,0},{4,5},{5,6},{6,7},{7,4},{8,9},{9,10},{10,1... | collective-permute-start | bytes 786440 | tf_op jit(solution)/shard_map/ppermute | solution.py:330
  89.6 10.4 %collective-permute-start.28 = (f16[1024,128]{1,0:T(8,128)(2,1)S(1)}, f16[1024,128]{1,0:T(8,128)(2,1)S(1)}, u32[]{:S(2)}, u32[]{:S(2)}) collective-permute-start(f16[1024,128]{1,0:T(8,128)(2,1)S(1)} %get-tuple-element.12), channel_id=1, source_target_pairs={{0,3},{1,0},{2,1},{3,2},{4,7},{5,4},{6,5},{7,6},{8,11},{9,8},{10,9... | collective-permute-start | bytes 786440 | tf_op jit(solution)/shard_map/ppermute | solution.py:331
  100.3 12.0 %collective-permute-start.29 = (f16[2048,128]{1,0:T(8,128)(2,1)S(1)}, f16[2048,128]{1,0:T(8,128)(2,1)S(1)}, u32[]{:S(2)}, u32[]{:S(2)}) collective-permute-start(f16[2048,128]{1,0:T(8,128)(2,1)S(1)} %pad_maximum_fusion), channel_id=1, source_target_pairs={{0,4},{4,64},{8,12},{12,72},{16,20},{20,80},{24,28},{28,88},{32,36... | collective-permute-start | bytes 1572872 | tf_op jit(solution)/shard_map/ppermute | solution.py:342
  103.6 9.0 %collective-permute-start.30 = (f32[128]{0:T(128)S(1)}, f32[128]{0:T(128)S(1)}, u32[]{:S(2)}, u32[]{:S(2)}) collective-permute-start(f32[128]{0:T(128)S(1)} %multiply_reduce_fusion), channel_id=1, source_target_pairs={{0,68},{4,0},{8,76},{12,8},{16,84},{20,16},{24,92},{28,24},{32,100... | collective-permute-start | bytes 1544 | tf_op jit(solution)/shard_map/ppermute | solution.py:349
  104.3 8.4 %collective-permute-start.31 = (f32[128]{0:T(128)S(1)}, f32[128]{0:T(128)S(1)}, u32[]{:S(2)}, u32[]{:S(2)}) collective-permute-start(f32[128]{0:T(128)S(1)} %multiply_reduce_fusion), channel_id=1, source_target_pairs={{0,132},{4,192},{8,140},{12,200},{16,148},{20,208},{24,156},{28,21... | collective-permute-start | bytes 1544 | tf_op jit(solution)/shard_map/ppermute | solution.py:349
  108.3 4.4 %collective-permute-start.32 = (f32[128]{0:T(128)S(1)}, f32[128]{0:T(128)S(1)}, u32[]{:S(2)}, u32[]{:S(2)}) collective-permute-start(f32[128]{0:T(128)S(1)} %multiply_reduce_fusion), channel_id=1, source_target_pairs={{0,196},{4,128},{8,204},{12,136},{16,212},{20,144},{24,220},{28,15... | collective-permute-start | bytes 1544 | tf_op jit(solution)/shard_map/ppermute | solution.py:349

commit v5 on v4

--- a/solution.py
+++ b/solution.py
@@ -259,6 +259,10 @@
     return (r * sizes[1] + c) * sizes[2] + y
 
 
+def named(array, axes, perm):
+    return lax.ppermute(array, axes, perm)
+
+
 def shards(sizes, values, tile_mask):
     n_row, n_col, n_layer = sizes
     axes = ("row", "col", "layer")
@@ -282,8 +286,10 @@
         move, core = {0: (1, 0), 1: (-1, 1), 2: (0, 0), 3: (0, 1)}[(y - y_to) % n_layer]
         spread[r, c, y] = flat(r // 2 * 2 + core, (zz + move) % n_z * 2 + r % 2, y_to, sizes)
     table = [(flat(*at, sizes), to) for at, to in spread.items()]
-    raw = lax.ppermute(raw, axes, table)
-    mass = lax.ppermute(lax.psum(column_sums(mask, values), "row"), axes, table)
+    raw = named(raw, axes, table)
+    sums = column_sums(mask, values)
+    others = [named(sums, "row", [(r, r ^ k) for r in range(n_row)]) for k in range(1, n_row)]
+    mass = named((sums + others[0]) + (others[1] + others[2]), axes, table)
     quarter = masked_quarter(mask, values, n_layer)
     part = scale(raw, mass, per, halves)
 
@@ -297,10 +303,10 @@
     for step in range(1, last + 1):
         if step == last:
             up, down = up[:half], down[half:]
-        up = lax.ppermute(up, "col", ring(1))
-        down = lax.ppermute(down, "col", ring(-1))
+        up = named(up, "col", ring(1))
+        down = named(down, "col", ring(-1))
         mine += [up, down]
-    parts = [(p, lax.ppermute(p, "row", swap)) for p in mine]
+    parts = [(p, named(p, "row", swap)) for p in mine]
 
     rights = []
     for m in range(n_row):
@@ -310,7 +316,7 @@
             lo_to, hi_to = lo ^ m // 2, core ^ m % 2
             to = (lo_to * 2 + (hi ^ hi_to ^ lo_to ^ 1), zz * 2 + hi_to, y)
             perm.append((flat(r, c, y, sizes), flat(*to, sizes)))
-        rights.append(lax.ppermute(quarter, axes, perm))
+        rights.append(named(quarter, axes, perm))
     early = [p for pair in parts[:2 * last - 3] for p in pair]
     late = [p for pair in parts[2 * last - 3:] for p in pair]
     right, out = product(early, [p.shape[0] // half for p in early], per, rights, height, n_layer)
@@ -320,15 +326,15 @@
     down = [(y, (y - 1) % n_layer) for y in range(n_layer)]
     mid = height // 2
     send = lax.optimization_barrier(out[1:, :height].astype(f16))
-    far_a = lax.ppermute(send[1, :mid], "layer", up)
-    far_b = lax.ppermute(send[1, mid:], "layer", down)
-    up_b = lax.ppermute(send[0, mid:], "layer", up)
-    down_a = lax.ppermute(send[2, :mid], "layer", down)
+    far_a = named(send[1, :mid], "layer", up)
+    far_b = named(send[1, mid:], "layer", down)
+    up_b = named(send[0, mid:], "layer", up)
+    down_a = named(send[2, :mid], "layer", down)
     up_a = (out[1, :mid] + far_a.astype(f32)).astype(f16)
     down_b = (out[3, mid:height] + far_b.astype(f32)).astype(f16)
     up_a, down_b = lax.optimization_barrier((up_a, down_b))
-    up_a = lax.ppermute(up_a, "layer", up)
-    down_b = lax.ppermute(down_b, "layer", down)
+    up_a = named(up_a, "layer", up)
+    down_b = named(down_b, "layer", down)
     total = jnp.concatenate([
         out[0, :mid] + (up_a.astype(f32) + down_a.astype(f32)),
         out[0, mid:height] + (up_b.astype(f32) + down_b.astype(f32)),
@@ -339,14 +345,14 @@
         for c in range(n_col):
             lo, core, hi = r // 2, r % 2, c % 2
             owner[r, c] = (lo * 2 + hi, c // 2 * 2 + (core ^ hi ^ lo ^ 1))
-    expanded = lax.ppermute(
+    expanded = named(
         total, ("row", "col"), [(r * n_col + c, o[0] * n_col + o[1]) for (r, c), o in owner.items()])
     summand = total.astype(f32)
     summand = jnp.sum(summand * summand, axis=0)
     weights = []
     for k in range(1, n_row):
         perm = [(r * n_col + c, (o[0] ^ k) * n_col + o[1]) for (r, c), o in owner.items()]
-        weights.append(lax.ppermute(summand, ("row", "col"), perm))
+        weights.append(named(summand, ("row", "col"), perm))
     expanded = expanded.astype(f32)
     inflated = expanded * expanded
     weight = jnp.sum(inflated, axis=0) + (weights[0] + (weights[1] + weights[2]))

time: 114 us -> 113 us (level)
  blocking collectives: 6.48 us -> 0 us
  waiting for transfers between devices: 33.4 us -> 37.5 us
    psum x1 -> x0, blocking collectives: 6.48 us -> none  [shards(): mass = lax.ppermute(lax.psum(column_sums(mask, values), 'row'), axes, table)]
    ppermute x33 -> x36, waiting for transfers between devices: 33.4 us -> 37.5 us  [named(): return lax.ppermute(array, axes, perm)]
    ppermute x33 -> x36, starting transfers between devices: 59.8 us -> 60.9 us  [named(): return lax.ppermute(array, axes, perm)]
  transfers between devices with their start and end apart: 33 -> 36, of which waited for: 12 -> 13; matrix products, arithmetic and copies ran while one was open for 1% -> 1% of each run, Pallas kernels for 5% -> 5%
where the time goes in v5:
time: 113 us
  starting transfers between devices  60.9 us (54%)
  waiting for transfers between devices  37.5 us (33%)
  Pallas kernels  10.5 us (9%)
  other arithmetic  2.42 us (2%)
    ppermute x36, starting transfers between devices, named(): return lax.ppermute(array, axes, perm)  60.9 us
    ppermute x36, waiting for transfers between devices, named(): return lax.ppermute(array, axes, perm)  37.5 us
    pallas_call x2, Pallas kernels, product(): pl.pallas_call(functools.partial(product_kernel, n_parts, counts, per, ag...  6.91 us
  transfers between devices with their start and end apart: 36, of which 13 were waited for; matrix products, arithmetic and copies ran while one was open for 1% of the time, Pallas kernels for 5%

profile of v5, /device:TPU:1, one launch (start us, length us, event | category | flops | bytes accessed | tf_op | source)
XLA Modules:
  0.0 112.5 jit_solution(6760385782945271182)
XLA Ops:
  0.0 2.0 %share.1 = bf16[1056,128]{1,0:T(8,128)(2,1)S(1)} custom-call(s32[4,16]{1,0:T(4,128)} %bitcast.33, bf16[2048,512]{1,0:T(8,128)(2,1)} %values_ref.3), custom_call_target="tpu_custom_call" | custom-call | flops 1048576 | bytes 2097152 | tf_op jit(solution)/shard_map/share/pallas_call | solution.py:74
  2.0 5.6 %collective-permute-start = (bf16[1056,128]{1,0:T(8,128)(2,1)S(1)}, bf16[1056,128]{1,0:T(8,128)(2,1)S(1)}, u32[]{:S(2)}, u32[]{:S(2)}) collective-permute-start(bf16[1056,128]{1,0:T(8,128)(2,1)S(1)} %share.1), channel_id=1, source_target_pairs={{0,8},{1,120},{2,0},{3,64},{4,2},{5,66},{6,10},{7,122},{8,73},{9,1... | collective-permute-start | bytes 811016 | tf_op jit(solution)/shard_map/ppermute | solution.py:263
  7.5 0.7 copy-done.1
  8.2 0.7 masked_quarter.1
  8.9 3.7 %collective-permute-start.22 = (bf16[512,512]{1,0:T(8,128)(2,1)S(1)}, bf16[512,512]{1,0:T(8,128)(2,1)S(1)}, u32[]{:S(2)}, u32[]{:S(2)}) collective-permute-start(bf16[512,512]{1,0:T(8,128)(2,1)S(1)} %masked_quarter.1), channel_id=1, source_target_pairs={{0,64},{1,65},{2,66},{3,67},{4,0},{5,1},{6,2},{7,3},{8,72},{9,73},... | collective-permute-start | bytes 1572872 | tf_op jit(solution)/shard_map/ppermute | solution.py:263
  12.6 0.9 column_sums.1
  13.7 2.0 %collective-permute-start.3 = (f32[4,128]{1,0:T(4,128)S(1)}, f32[4,128]{1,0:T(4,128)S(1)}, u32[]{:S(2)}, u32[]{:S(2)}) collective-permute-start(f32[4,128]{1,0:T(4,128)S(1)} %column_sums.1), channel_id=1, source_target_pairs={{0,192},{64,128},{128,64},{192,0},{1,193},{65,129},{129,65},{193,1... | collective-permute-start | bytes 6152 | tf_op jit(solution)/shard_map/ppermute | solution.py:263
  15.8 3.1 %collective-permute-done.2 = f32[4,128]{1,0:T(4,128)S(1)} collective-permute-done((f32[4,128]{1,0:T(4,128)S(1)}, f32[4,128]{1,0:T(4,128)S(1)}, u32[]{:S(2)}, u32[]{:S(2)}) %collective-permute-start.2) | collective-permute-done | bytes 2080 | tf_op jit(solution)/shard_map/ppermute | solution.py:263
  18.9 4.1 %collective-permute-start.4 = (f32[4,128]{1,0:T(4,128)S(1)}, f32[4,128]{1,0:T(4,128)S(1)}, u32[]{:S(2)}, u32[]{:S(2)}) collective-permute-start(f32[4,128]{1,0:T(4,128)S(1)} %add_add_fusion), channel_id=1, source_target_pairs={{0,8},{1,120},{2,0},{3,64},{4,2},{5,66},{6,10},{7,122},{8,73},{9,1... | collective-permute-start | bytes 6152 | tf_op jit(solution)/shard_map/ppermute | solution.py:263
  23.0 3.1 %collective-permute-done.4.mass_ref = f32[4,128]{1,0:T(4,128)S(1)} collective-permute-done((f32[4,128]{1,0:T(4,128)S(1)}, f32[4,128]{1,0:T(4,128)S(1)}, u32[]{:S(2)}, u32[]{:S(2)}) %collective-permute-start.4) | collective-permute-done | bytes 2080 | tf_op jit(solution)/shard_map/ppermute | solution.py:263
  26.3 4.1 %collective-permute-start.9 = (bf16[1056,128]{1,0:T(8,128)(2,1)S(1)}, bf16[1056,128]{1,0:T(8,128)(2,1)S(1)}, u32[]{:S(2)}, u32[]{:S(2)}) collective-permute-start(bf16[1056,128]{1,0:T(8,128)(2,1)S(1)} %scale.1.refs_0_), channel_id=1, source_target_pairs={{0,56},{4,60},{8,0},{12,4},{16,8},{20,12},{24,16},{28,20},{32,24},... | collective-permute-start | bytes 811016 | tf_op jit(solution)/shard_map/ppermute | solution.py:263
  30.4 5.9 %collective-permute-done.5.refs_2_ = bf16[1056,128]{1,0:T(8,128)(2,1)S(1)} collective-permute-done((bf16[1056,128]{1,0:T(8,128)(2,1)S(1)}, bf16[1056,128]{1,0:T(8,128)(2,1)S(1)}, u32[]{:S(2)}, u32[]{:S(2)}) %collective-permute-start.5) | collective-permute-done | bytes 270368 | tf_op jit(solution)/shard_map/ppermute | solution.py:263
  36.3 0.7 collective-permute-start.23
  37.0 4.8 %collective-permute-start.24 = (bf16[512,512]{1,0:T(8,128)(2,1)S(1)}, bf16[512,512]{1,0:T(8,128)(2,1)S(1)}, u32[]{:S(2)}, u32[]{:S(2)}) collective-permute-start(bf16[512,512]{1,0:T(8,128)(2,1)S(1)} %masked_quarter.1), channel_id=1, source_target_pairs={{0,128},{1,129},{2,130},{3,131},{4,192},{5,193},{6,194},{7,195},{8... | collective-permute-start | bytes 1572872 | tf_op jit(solution)/shard_map/ppermute | solution.py:263
  41.8 2.7 %collective-permute-start.10 = (bf16[1056,128]{1,0:T(8,128)(2,1)S(1)}, bf16[1056,128]{1,0:T(8,128)(2,1)S(1)}, u32[]{:S(2)}, u32[]{:S(2)}) collective-permute-start(bf16[1056,128]{1,0:T(8,128)(2,1)S(1)} %collective-permute-done.9.refs_4_), channel_id=1, source_target_pairs={{0,56},{4,60},{8,0},{12,4},{16,8},{20,12},{24,16},{28,20},{32,24},... | collective-permute-start | bytes 811016 | tf_op jit(solution)/shard_map/ppermute | solution.py:263
  44.5 1.1 collective-permute-done.6.refs_6_
  45.6 2.3 %collective-permute-done.10.refs_8_ = bf16[1056,128]{1,0:T(8,128)(2,1)S(1)} collective-permute-done((bf16[1056,128]{1,0:T(8,128)(2,1)S(1)}, bf16[1056,128]{1,0:T(8,128)(2,1)S(1)}, u32[]{:S(2)}, u32[]{:S(2)}) %collective-permute-start.10) | collective-permute-done | bytes 270368 | tf_op jit(solution)/shard_map/ppermute | solution.py:263
  47.9 3.5 %collective-permute-start.11 = (bf16[1056,128]{1,0:T(8,128)(2,1)S(1)}, bf16[1056,128]{1,0:T(8,128)(2,1)S(1)}, u32[]{:S(2)}, u32[]{:S(2)}) collective-permute-start(bf16[1056,128]{1,0:T(8,128)(2,1)S(1)} %collective-permute-done.10.refs_8_), channel_id=1, source_target_pairs={{0,56},{4,60},{8,0},{12,4},{16,8},{20,12},{24,16},{28,20},{32,24},... | collective-permute-start | bytes 811016 | tf_op jit(solution)/shard_map/ppermute | solution.py:263
  51.4 3.5 %collective-permute-start.17 = (bf16[1056,128]{1,0:T(8,128)(2,1)S(1)}, bf16[1056,128]{1,0:T(8,128)(2,1)S(1)}, u32[]{:S(2)}, u32[]{:S(2)}) collective-permute-start(bf16[1056,128]{1,0:T(8,128)(2,1)S(1)} %scale.1.refs_0_), channel_id=1, source_target_pairs={{0,64},{64,0},{128,192},{192,128},{1,65},{65,1},{129,193},{193,129... | collective-permute-start | bytes 811016 | tf_op jit(solution)/shard_map/ppermute | solution.py:263
  54.9 3.5 %collective-permute-done.24.refs_12_ = bf16[512,512]{1,0:T(8,128)(2,1)S(1)} collective-permute-done((bf16[512,512]{1,0:T(8,128)(2,1)S(1)}, bf16[512,512]{1,0:T(8,128)(2,1)S(1)}, u32[]{:S(2)}, u32[]{:S(2)}) %collective-permute-start.24) | collective-permute-done | bytes 524320 | tf_op jit(solution)/shard_map/ppermute | solution.py:263
  58.5 2.3 %collective-permute-start.18 = (bf16[1056,128]{1,0:T(8,128)(2,1)S(1)}, bf16[1056,128]{1,0:T(8,128)(2,1)S(1)}, u32[]{:S(2)}, u32[]{:S(2)}) collective-permute-start(bf16[1056,128]{1,0:T(8,128)(2,1)S(1)} %collective-permute-done.5.refs_2_), channel_id=1, source_target_pairs={{0,64},{64,0},{128,192},{192,128},{1,65},{65,1},{129,193},{193,129... | collective-permute-start | bytes 811016 | tf_op jit(solution)/shard_map/ppermute | solution.py:263
  60.8 0.5 collective-permute-start.20
  61.5 0.4 collective-permute-done.18.refs_3_
  61.9 2.7 %collective-permute-start.15 = (bf16[528,128]{1,0:T(8,128)(2,1)S(1)}, bf16[528,128]{1,0:T(8,128)(2,1)S(1)}, u32[]{:S(2)}, u32[]{:S(2)}) collective-permute-start(bf16[528,128]{1,0:T(8,128)(2,1)S(1)} %slice.46), channel_id=1, source_target_pairs={{0,56},{4,60},{8,0},{12,4},{16,8},{20,12},{24,16},{28,20},{32,24},... | collective-permute-start | bytes 405512 | tf_op jit(solution)/shard_map/ppermute | solution.py:263
  64.6 0.7 collective-permute-start.12
  65.4 2.1 %collective-permute-done.13.refs_4_ = bf16[528,128]{1,0:T(8,128)(2,1)S(1)} collective-permute-done((bf16[528,128]{1,0:T(8,128)(2,1)S(1)}, bf16[528,128]{1,0:T(8,128)(2,1)S(1)}, u32[]{:S(2)}, u32[]{:S(2)}) %collective-permute-start.13) | collective-permute-done | bytes 135200 | tf_op jit(solution)/shard_map/ppermute | solution.py:263
  67.4 1.3 %collective-permute-start.14 = (bf16[528,128]{1,0:T(8,128)(2,1)S(1)}, bf16[528,128]{1,0:T(8,128)(2,1)S(1)}, u32[]{:S(2)}, u32[]{:S(2)}) collective-permute-start(bf16[528,128]{1,0:T(8,128)(2,1)S(1)} %collective-permute-done.13.refs_4_), channel_id=1, source_target_pairs={{0,64},{64,0},{128,192},{192,128},{1,65},{65,1},{129,193},{193,129... | collective-permute-start | bytes 405512 | tf_op jit(solution)/shard_map/ppermute | solution.py:263
  68.7 4.3 %product.1 = (bf16[2048,512]{1,0:T(8,128)(2,1)S(1)}, f32[4,2176,128]{2,1,0:T(8,128)S(1)}) custom-call(bf16[1056,128]{1,0:T(8,128)(2,1)S(1)} %scale.1.refs_0_, bf16[1056,128]{1,0:T(8,128)(2,1)S(1)} %collective-permute-done.17.refs_1_, bf16[1056,128]{1,0:T(8,128)(2,1)S(1)} %collective-permute-done.5.refs_2_, ...), custom_call_target="tpu_custom_call" | custom-call | flops 1342177280 | bytes 1048576 | tf_op jit(solution)/shard_map/product/pallas_call | solution.py:233
  73.1 2.6 %add_product.1 = f32[4,2176,128]{2,1,0:T(8,128)S(1)} custom-call(bf16[1056,128]{1,0:T(8,128)(2,1)S(1)} %collective-permute-done.7.refs_0_, bf16[1056,128]{1,0:T(8,128)(2,1)S(1)} %collective-permute-done.8.refs_1_, bf16[1056,128]{1,0:T(8,128)(2,1)S(1)} %collective-permute-done.11.refs_2_, ...), custom_call_target="tpu_custom_call", output_to_operand_aliasing={{}: (9, {})} | custom-call | flops 805306368 | bytes 1048576 | tf_op jit(solution)/shard_map/add_product/pallas_call | solution.py:233
  75.9 0.2 slice_bitcast_fusion.5
  76.1 1.6 %collective-permute-start.26 = (f16[1024,128]{1,0:T(8,128)(2,1)S(1)}, f16[1024,128]{1,0:T(8,128)(2,1)S(1)}, u32[]{:S(2)}, u32[]{:S(2)}) collective-permute-start(f16[1024,128]{1,0:T(8,128)(2,1)S(1)} %get-tuple-element.20), channel_id=1, source_target_pairs={{0,1},{1,2},{2,3},{3,0},{4,5},{5,6},{6,7},{7,4},{8,9},{9,10},{10,1... | collective-permute-start | bytes 786440 | tf_op jit(solution)/shard_map/ppermute | solution.py:263
  77.8 3.9 %collective-permute-start.27 = (f16[1024,128]{1,0:T(8,128)(2,1)S(1)}, f16[1024,128]{1,0:T(8,128)(2,1)S(1)}, u32[]{:S(2)}, u32[]{:S(2)}) collective-permute-start(f16[1024,128]{1,0:T(8,128)(2,1)S(1)} %get-tuple-element.19), channel_id=1, source_target_pairs={{0,3},{1,0},{2,1},{3,2},{4,7},{5,4},{6,5},{7,6},{8,11},{9,8},{10,9... | collective-permute-start | bytes 786440 | tf_op jit(solution)/shard_map/ppermute | solution.py:263
  81.6 1.2 %collective-permute-start.29 = (f16[1024,128]{1,0:T(8,128)(2,1)S(1)}, f16[1024,128]{1,0:T(8,128)(2,1)S(1)}, u32[]{:S(2)}, u32[]{:S(2)}) collective-permute-start(f16[1024,128]{1,0:T(8,128)(2,1)S(1)} %get-tuple-element.17), channel_id=1, source_target_pairs={{0,3},{1,0},{2,1},{3,2},{4,7},{5,4},{6,5},{7,6},{8,11},{9,8},{10,9... | collective-permute-start | bytes 786440 | tf_op jit(solution)/shard_map/ppermute | solution.py:263
  82.8 0.3 collective-permute-start.30
  83.1 4.4 %collective-permute-done.26 = f16[1024,128]{1,0:T(8,128)(2,1)S(1)} collective-permute-done((f16[1024,128]{1,0:T(8,128)(2,1)S(1)}, f16[1024,128]{1,0:T(8,128)(2,1)S(1)}, u32[]{:S(2)}, u32[]{:S(2)}) %collective-permute-start.26) | collective-permute-done | bytes 262176 | tf_op jit(solution)/shard_map/ppermute | solution.py:263
  87.7 0.7 collective-permute-start.28
  88.3 2.2 %collective-permute-start.31 = (f16[1024,128]{1,0:T(8,128)(2,1)S(1)}, f16[1024,128]{1,0:T(8,128)(2,1)S(1)}, u32[]{:S(2)}, u32[]{:S(2)}) collective-permute-start(f16[1024,128]{1,0:T(8,128)(2,1)S(1)} %get-tuple-element.12), channel_id=1, source_target_pairs={{0,3},{1,0},{2,1},{3,2},{4,7},{5,4},{6,5},{7,6},{8,11},{9,8},{10,9... | collective-permute-start | bytes 786440 | tf_op jit(solution)/shard_map/ppermute | solution.py:263
  90.5 1.9 %collective-permute-done.29 = f16[1024,128]{1,0:T(8,128)(2,1)S(1)} collective-permute-done((f16[1024,128]{1,0:T(8,128)(2,1)S(1)}, f16[1024,128]{1,0:T(8,128)(2,1)S(1)}, u32[]{:S(2)}, u32[]{:S(2)}) %collective-permute-start.29) | collective-permute-done | bytes 262176 | tf_op jit(solution)/shard_map/ppermute | solution.py:263
  92.4 0.7 collective-permute-done.30
  93.1 5.6 %collective-permute-done.28 = f16[1024,128]{1,0:T(8,128)(2,1)S(1)} collective-permute-done((f16[1024,128]{1,0:T(8,128)(2,1)S(1)}, f16[1024,128]{1,0:T(8,128)(2,1)S(1)}, u32[]{:S(2)}, u32[]{:S(2)}) %collective-permute-start.28) | collective-permute-done | bytes 262176 | tf_op jit(solution)/shard_map/ppermute | solution.py:263
  98.7 0.2 fusion.8
  99.1 3.0 %collective-permute-start.32 = (f16[2048,128]{1,0:T(8,128)(2,1)S(1)}, f16[2048,128]{1,0:T(8,128)(2,1)S(1)}, u32[]{:S(2)}, u32[]{:S(2)}) collective-permute-start(f16[2048,128]{1,0:T(8,128)(2,1)S(1)} %pad_maximum_fusion), channel_id=1, source_target_pairs={{0,4},{4,64},{8,12},{12,72},{16,20},{20,80},{24,28},{28,88},{32,36... | collective-permute-start | bytes 1572872 | tf_op jit(solution)/shard_map/ppermute | solution.py:263
  102.1 0.3 multiply_reduce_fusion
  102.4 0.7 collective-permute-start.33
  103.0 4.7 %collective-permute-start.34 = (f32[128]{0:T(128)S(1)}, f32[128]{0:T(128)S(1)}, u32[]{:S(2)}, u32[]{:S(2)}) collective-permute-start(f32[128]{0:T(128)S(1)} %multiply_reduce_fusion), channel_id=1, source_target_pairs={{0,132},{4,192},{8,140},{12,200},{16,148},{20,208},{24,156},{28,21... | collective-permute-start | bytes 1544 | tf_op jit(solution)/shard_map/ppermute | solution.py:263
  107.9 3.3 %collective-permute-done.32 = f16[2048,128]{1,0:T(8,128)(2,1)S(1)} collective-permute-done((f16[2048,128]{1,0:T(8,128)(2,1)S(1)}, f16[2048,128]{1,0:T(8,128)(2,1)S(1)}, u32[]{:S(2)}, u32[]{:S(2)}) %collective-permute-start.32) | collective-permute-done | bytes 524320 | tf_op jit(solution)/shard_map/ppermute | solution.py:263
  111.1 0.3 fusion
  111.4 1.1 multiply_divide_fusion
  (46 shorter events, 1.3 us)
Async XLA Ops:
  0.0 7.5 %copy-start = (bf16[2048,512]{1,0:T(8,128)(2,1)S(1)}, bf16[2048,512]{1,0:T(8,128)(2,1)}, u32[]{:S(2)}) copy-start(bf16[2048,512]{1,0:T(8,128)(2,1)} %values_ref.3) | copy-start | bytes 6291460
  2.0 24.2 %collective-permute-start = (bf16[1056,128]{1,0:T(8,128)(2,1)S(1)}, bf16[1056,128]{1,0:T(8,128)(2,1)S(1)}, u32[]{:S(2)}, u32[]{:S(2)}) collective-permute-start(bf16[1056,128]{1,0:T(8,128)(2,1)S(1)} %share.1), channel_id=1, source_target_pairs={{0,8},{1,120},{2,0},{3,64},{4,2},{5,66},{6,10},{7,122},{8,73},{9,1... | collective-permute-start | bytes 811016 | tf_op jit(solution)/shard_map/ppermute | solution.py:263
  7.5 0.7 copy-start.1
  8.9 32.8 %collective-permute-start.22 = (bf16[512,512]{1,0:T(8,128)(2,1)S(1)}, bf16[512,512]{1,0:T(8,128)(2,1)S(1)}, u32[]{:S(2)}, u32[]{:S(2)}) collective-permute-start(bf16[512,512]{1,0:T(8,128)(2,1)S(1)} %masked_quarter.1), channel_id=1, source_target_pairs={{0,64},{1,65},{2,66},{3,67},{4,0},{5,1},{6,2},{7,3},{8,72},{9,73},... | collective-permute-start | bytes 1572872 | tf_op jit(solution)/shard_map/ppermute | solution.py:263
  13.5 2.2 %collective-permute-start.1 = (f32[4,128]{1,0:T(4,128)S(1)}, f32[4,128]{1,0:T(4,128)S(1)}, u32[]{:S(2)}, u32[]{:S(2)}) collective-permute-start(f32[4,128]{1,0:T(4,128)S(1)} %column_sums.1), channel_id=1, source_target_pairs={{0,64},{64,0},{128,192},{192,128},{1,65},{65,1},{129,193},{193,129... | collective-permute-start | bytes 6152 | tf_op jit(solution)/shard_map/ppermute | solution.py:263
  13.6 5.3 %collective-permute-start.2 = (f32[4,128]{1,0:T(4,128)S(1)}, f32[4,128]{1,0:T(4,128)S(1)}, u32[]{:S(2)}, u32[]{:S(2)}) collective-permute-start(f32[4,128]{1,0:T(4,128)S(1)} %column_sums.1), channel_id=1, source_target_pairs={{0,128},{64,192},{128,0},{192,64},{1,129},{65,193},{129,1},{193,65... | collective-permute-start | bytes 6152 | tf_op jit(solution)/shard_map/ppermute | solution.py:263
  13.7 5.2 %collective-permute-start.3 = (f32[4,128]{1,0:T(4,128)S(1)}, f32[4,128]{1,0:T(4,128)S(1)}, u32[]{:S(2)}, u32[]{:S(2)}) collective-permute-start(f32[4,128]{1,0:T(4,128)S(1)} %column_sums.1), channel_id=1, source_target_pairs={{0,192},{64,128},{128,64},{192,0},{1,193},{65,129},{129,65},{193,1... | collective-permute-start | bytes 6152 | tf_op jit(solution)/shard_map/ppermute | solution.py:263
  18.9 7.2 %collective-permute-start.4 = (f32[4,128]{1,0:T(4,128)S(1)}, f32[4,128]{1,0:T(4,128)S(1)}, u32[]{:S(2)}, u32[]{:S(2)}) collective-permute-start(f32[4,128]{1,0:T(4,128)S(1)} %add_add_fusion), channel_id=1, source_target_pairs={{0,8},{1,120},{2,0},{3,64},{4,2},{5,66},{6,10},{7,122},{8,73},{9,1... | collective-permute-start | bytes 6152 | tf_op jit(solution)/shard_map/ppermute | solution.py:263
  26.2 10.1 %collective-permute-start.5 = (bf16[1056,128]{1,0:T(8,128)(2,1)S(1)}, bf16[1056,128]{1,0:T(8,128)(2,1)S(1)}, u32[]{:S(2)}, u32[]{:S(2)}) collective-permute-start(bf16[1056,128]{1,0:T(8,128)(2,1)S(1)} %scale.1.refs_0_), channel_id=1, source_target_pairs={{0,8},{4,12},{8,16},{12,20},{16,24},{20,28},{24,32},{28,36},{32,40... | collective-permute-start | bytes 811016 | tf_op jit(solution)/shard_map/ppermute | solution.py:263
  26.3 15.5 %collective-permute-start.9 = (bf16[1056,128]{1,0:T(8,128)(2,1)S(1)}, bf16[1056,128]{1,0:T(8,128)(2,1)S(1)}, u32[]{:S(2)}, u32[]{:S(2)}) collective-permute-start(bf16[1056,128]{1,0:T(8,128)(2,1)S(1)} %scale.1.refs_0_), channel_id=1, source_target_pairs={{0,56},{4,60},{8,0},{12,4},{16,8},{20,12},{24,16},{28,20},{32,24},... | collective-permute-start | bytes 811016 | tf_op jit(solution)/shard_map/ppermute | solution.py:263
  36.3 9.3 %collective-permute-start.6 = (bf16[1056,128]{1,0:T(8,128)(2,1)S(1)}, bf16[1056,128]{1,0:T(8,128)(2,1)S(1)}, u32[]{:S(2)}, u32[]{:S(2)}) collective-permute-start(bf16[1056,128]{1,0:T(8,128)(2,1)S(1)} %collective-permute-done.5.refs_2_), channel_id=1, source_target_pairs={{0,8},{4,12},{8,16},{12,20},{16,24},{20,28},{24,32},{28,36},{32,40... | collective-permute-start | bytes 811016 | tf_op jit(solution)/shard_map/ppermute | solution.py:263
  36.3 15.1 %collective-permute-start.23 = (bf16[512,512]{1,0:T(8,128)(2,1)S(1)}, bf16[512,512]{1,0:T(8,128)(2,1)S(1)}, u32[]{:S(2)}, u32[]{:S(2)}) collective-permute-start(bf16[512,512]{1,0:T(8,128)(2,1)S(1)} %masked_quarter.1), channel_id=1, source_target_pairs={{0,4},{1,5},{2,6},{3,7},{4,68},{5,69},{6,70},{7,71},{8,12},{9,13},... | collective-permute-start | bytes 1572872 | tf_op jit(solution)/shard_map/ppermute | solution.py:263
  37.0 21.4 %collective-permute-start.24 = (bf16[512,512]{1,0:T(8,128)(2,1)S(1)}, bf16[512,512]{1,0:T(8,128)(2,1)S(1)}, u32[]{:S(2)}, u32[]{:S(2)}) collective-permute-start(bf16[512,512]{1,0:T(8,128)(2,1)S(1)} %masked_quarter.1), channel_id=1, source_target_pairs={{0,128},{1,129},{2,130},{3,131},{4,192},{5,193},{6,194},{7,195},{8... | collective-permute-start | bytes 1572872 | tf_op jit(solution)/shard_map/ppermute | solution.py:263
  41.8 19.0 %collective-permute-start.25 = (bf16[512,512]{1,0:T(8,128)(2,1)S(1)}, bf16[512,512]{1,0:T(8,128)(2,1)S(1)}, u32[]{:S(2)}, u32[]{:S(2)}) collective-permute-start(bf16[512,512]{1,0:T(8,128)(2,1)S(1)} %masked_quarter.1), channel_id=1, source_target_pairs={{0,196},{1,197},{2,198},{3,199},{4,132},{5,133},{6,134},{7,135},{8... | collective-permute-start | bytes 1572872 | tf_op jit(solution)/shard_map/ppermute | solution.py:263
  41.8 6.2 %collective-permute-start.10 = (bf16[1056,128]{1,0:T(8,128)(2,1)S(1)}, bf16[1056,128]{1,0:T(8,128)(2,1)S(1)}, u32[]{:S(2)}, u32[]{:S(2)}) collective-permute-start(bf16[1056,128]{1,0:T(8,128)(2,1)S(1)} %collective-permute-done.9.refs_4_), channel_id=1, source_target_pairs={{0,56},{4,60},{8,0},{12,4},{16,8},{20,12},{24,16},{28,20},{32,24},... | collective-permute-start | bytes 811016 | tf_op jit(solution)/shard_map/ppermute | solution.py:263
  45.6 15.1 %collective-permute-start.7 = (bf16[1056,128]{1,0:T(8,128)(2,1)S(1)}, bf16[1056,128]{1,0:T(8,128)(2,1)S(1)}, u32[]{:S(2)}, u32[]{:S(2)}) collective-permute-start(bf16[1056,128]{1,0:T(8,128)(2,1)S(1)} %collective-permute-done.6.refs_6_), channel_id=1, source_target_pairs={{0,8},{4,12},{8,16},{12,20},{16,24},{20,28},{24,32},{28,36},{32,40... | collective-permute-start | bytes 811016 | tf_op jit(solution)/shard_map/ppermute | solution.py:263
  47.9 13.3 %collective-permute-start.11 = (bf16[1056,128]{1,0:T(8,128)(2,1)S(1)}, bf16[1056,128]{1,0:T(8,128)(2,1)S(1)}, u32[]{:S(2)}, u32[]{:S(2)}) collective-permute-start(bf16[1056,128]{1,0:T(8,128)(2,1)S(1)} %collective-permute-done.10.refs_8_), channel_id=1, source_target_pairs={{0,56},{4,60},{8,0},{12,4},{16,8},{20,12},{24,16},{28,20},{32,24},... | collective-permute-start | bytes 811016 | tf_op jit(solution)/shard_map/ppermute | solution.py:263
  51.4 10.0 %collective-permute-start.17 = (bf16[1056,128]{1,0:T(8,128)(2,1)S(1)}, bf16[1056,128]{1,0:T(8,128)(2,1)S(1)}, u32[]{:S(2)}, u32[]{:S(2)}) collective-permute-start(bf16[1056,128]{1,0:T(8,128)(2,1)S(1)} %scale.1.refs_0_), channel_id=1, source_target_pairs={{0,64},{64,0},{128,192},{192,128},{1,65},{65,1},{129,193},{193,129... | collective-permute-start | bytes 811016 | tf_op jit(solution)/shard_map/ppermute | solution.py:263
  58.5 3.5 %collective-permute-start.18 = (bf16[1056,128]{1,0:T(8,128)(2,1)S(1)}, bf16[1056,128]{1,0:T(8,128)(2,1)S(1)}, u32[]{:S(2)}, u32[]{:S(2)}) collective-permute-start(bf16[1056,128]{1,0:T(8,128)(2,1)S(1)} %collective-permute-done.5.refs_2_), channel_id=1, source_target_pairs={{0,64},{64,0},{128,192},{192,128},{1,65},{65,1},{129,193},{193,129... | collective-permute-start | bytes 811016 | tf_op jit(solution)/shard_map/ppermute | solution.py:263
  60.8 3.8 %collective-permute-start.19 = (bf16[1056,128]{1,0:T(8,128)(2,1)S(1)}, bf16[1056,128]{1,0:T(8,128)(2,1)S(1)}, u32[]{:S(2)}, u32[]{:S(2)}) collective-permute-start(bf16[1056,128]{1,0:T(8,128)(2,1)S(1)} %collective-permute-done.9.refs_4_), channel_id=1, source_target_pairs={{0,64},{64,0},{128,192},{192,128},{1,65},{65,1},{129,193},{193,129... | collective-permute-start | bytes 811016 | tf_op jit(solution)/shard_map/ppermute | solution.py:263
  60.8 4.5 %collective-permute-start.20 = (bf16[1056,128]{1,0:T(8,128)(2,1)S(1)}, bf16[1056,128]{1,0:T(8,128)(2,1)S(1)}, u32[]{:S(2)}, u32[]{:S(2)}) collective-permute-start(bf16[1056,128]{1,0:T(8,128)(2,1)S(1)} %collective-permute-done.6.refs_6_), channel_id=1, source_target_pairs={{0,64},{64,0},{128,192},{192,128},{1,65},{65,1},{129,193},{193,129... | collective-permute-start | bytes 811016 | tf_op jit(solution)/shard_map/ppermute | solution.py:263
  61.3 7.4 %collective-permute-start.21 = (bf16[1056,128]{1,0:T(8,128)(2,1)S(1)}, bf16[1056,128]{1,0:T(8,128)(2,1)S(1)}, u32[]{:S(2)}, u32[]{:S(2)}) collective-permute-start(bf16[1056,128]{1,0:T(8,128)(2,1)S(1)} %collective-permute-done.10.refs_8_), channel_id=1, source_target_pairs={{0,64},{64,0},{128,192},{192,128},{1,65},{65,1},{129,193},{193,129... | collective-permute-start | bytes 811016 | tf_op jit(solution)/shard_map/ppermute | solution.py:263
  61.4 6.0 %collective-permute-start.13 = (bf16[528,128]{1,0:T(8,128)(2,1)S(1)}, bf16[528,128]{1,0:T(8,128)(2,1)S(1)}, u32[]{:S(2)}, u32[]{:S(2)}) collective-permute-start(bf16[528,128]{1,0:T(8,128)(2,1)S(1)} %slice.45), channel_id=1, source_target_pairs={{0,8},{4,12},{8,16},{12,20},{16,24},{20,28},{24,32},{28,36},{32,40... | collective-permute-start | bytes 405512 | tf_op jit(solution)/shard_map/ppermute | solution.py:263
  61.9 6.8 %collective-permute-start.15 = (bf16[528,128]{1,0:T(8,128)(2,1)S(1)}, bf16[528,128]{1,0:T(8,128)(2,1)S(1)}, u32[]{:S(2)}, u32[]{:S(2)}) collective-permute-start(bf16[528,128]{1,0:T(8,128)(2,1)S(1)} %slice.46), channel_id=1, source_target_pairs={{0,56},{4,60},{8,0},{12,4},{16,8},{20,12},{24,16},{28,20},{32,24},... | collective-permute-start | bytes 405512 | tf_op jit(solution)/shard_map/ppermute | solution.py:263
  64.6 8.4 %collective-permute-start.12 = (bf16[1056,128]{1,0:T(8,128)(2,1)S(1)}, bf16[1056,128]{1,0:T(8,128)(2,1)S(1)}, u32[]{:S(2)}, u32[]{:S(2)}) collective-permute-start(bf16[1056,128]{1,0:T(8,128)(2,1)S(1)} %collective-permute-done.11.refs_2_), channel_id=1, source_target_pairs={{0,64},{64,0},{128,192},{192,128},{1,65},{65,1},{129,193},{193,129... | collective-permute-start | bytes 811016 | tf_op jit(solution)/shard_map/ppermute | solution.py:263
  65.3 7.8 %collective-permute-start.8 = (bf16[1056,128]{1,0:T(8,128)(2,1)S(1)}, bf16[1056,128]{1,0:T(8,128)(2,1)S(1)}, u32[]{:S(2)}, u32[]{:S(2)}) collective-permute-start(bf16[1056,128]{1,0:T(8,128)(2,1)S(1)} %collective-permute-done.7.refs_0_), channel_id=1, source_target_pairs={{0,64},{64,0},{128,192},{192,128},{1,65},{65,1},{129,193},{193,129... | collective-permute-start | bytes 811016 | tf_op jit(solution)/shard_map/ppermute | solution.py:263
  67.4 5.6 %collective-permute-start.14 = (bf16[528,128]{1,0:T(8,128)(2,1)S(1)}, bf16[528,128]{1,0:T(8,128)(2,1)S(1)}, u32[]{:S(2)}, u32[]{:S(2)}) collective-permute-start(bf16[528,128]{1,0:T(8,128)(2,1)S(1)} %collective-permute-done.13.refs_4_), channel_id=1, source_target_pairs={{0,64},{64,0},{128,192},{192,128},{1,65},{65,1},{129,193},{193,129... | collective-permute-start | bytes 405512 | tf_op jit(solution)/shard_map/ppermute | solution.py:263
  68.7 4.3 %collective-permute-start.16 = (bf16[528,128]{1,0:T(8,128)(2,1)S(1)}, bf16[528,128]{1,0:T(8,128)(2,1)S(1)}, u32[]{:S(2)}, u32[]{:S(2)}) collective-permute-start(bf16[528,128]{1,0:T(8,128)(2,1)S(1)} %collective-permute-done.15.refs_6_), channel_id=1, source_target_pairs={{0,64},{64,0},{128,192},{192,128},{1,65},{65,1},{129,193},{193,129... | collective-permute-start | bytes 405512 | tf_op jit(solution)/shard_map/ppermute | solution.py:263
  76.1 11.4 %collective-permute-start.26 = (f16[1024,128]{1,0:T(8,128)(2,1)S(1)}, f16[1024,128]{1,0:T(8,128)(2,1)S(1)}, u32[]{:S(2)}, u32[]{:S(2)}) collective-permute-start(f16[1024,128]{1,0:T(8,128)(2,1)S(1)} %get-tuple-element.20), channel_id=1, source_target_pairs={{0,1},{1,2},{2,3},{3,0},{4,5},{5,6},{6,7},{7,4},{8,9},{9,10},{10,1... | collective-permute-start | bytes 786440 | tf_op jit(solution)/shard_map/ppermute | solution.py:263
  77.8 9.7 %collective-permute-start.27 = (f16[1024,128]{1,0:T(8,128)(2,1)S(1)}, f16[1024,128]{1,0:T(8,128)(2,1)S(1)}, u32[]{:S(2)}, u32[]{:S(2)}) collective-permute-start(f16[1024,128]{1,0:T(8,128)(2,1)S(1)} %get-tuple-element.19), channel_id=1, source_target_pairs={{0,3},{1,0},{2,1},{3,2},{4,7},{5,4},{6,5},{7,6},{8,11},{9,8},{10,9... | collective-permute-start | bytes 786440 | tf_op jit(solution)/shard_map/ppermute | solution.py:263
  81.6 10.8 %collective-permute-start.29 = (f16[1024,128]{1,0:T(8,128)(2,1)S(1)}, f16[1024,128]{1,0:T(8,128)(2,1)S(1)}, u32[]{:S(2)}, u32[]{:S(2)}) collective-permute-start(f16[1024,128]{1,0:T(8,128)(2,1)S(1)} %get-tuple-element.17), channel_id=1, source_target_pairs={{0,3},{1,0},{2,1},{3,2},{4,7},{5,4},{6,5},{7,6},{8,11},{9,8},{10,9... | collective-permute-start | bytes 786440 | tf_op jit(solution)/shard_map/ppermute | solution.py:263
  82.8 10.3 %collective-permute-start.30 = (f16[1024,128]{1,0:T(8,128)(2,1)S(1)}, f16[1024,128]{1,0:T(8,128)(2,1)S(1)}, u32[]{:S(2)}, u32[]{:S(2)}) collective-permute-start(f16[1024,128]{1,0:T(8,128)(2,1)S(1)} %get-tuple-element.18), channel_id=1, source_target_pairs={{0,1},{1,2},{2,3},{3,0},{4,5},{5,6},{6,7},{7,4},{8,9},{9,10},{10,1... | collective-permute-start | bytes 786440 | tf_op jit(solution)/shard_map/ppermute | solution.py:263
  87.7 11.1 %collective-permute-start.28 = (f16[1024,128]{1,0:T(8,128)(2,1)S(1)}, f16[1024,128]{1,0:T(8,128)(2,1)S(1)}, u32[]{:S(2)}, u32[]{:S(2)}) collective-permute-start(f16[1024,128]{1,0:T(8,128)(2,1)S(1)} %get-tuple-element.11), channel_id=1, source_target_pairs={{0,1},{1,2},{2,3},{3,0},{4,5},{5,6},{6,7},{7,4},{8,9},{9,10},{10,1... | collective-permute-start | bytes 786440 | tf_op jit(solution)/shard_map/ppermute | solution.py:263
  88.3 10.4 %collective-permute-start.31 = (f16[1024,128]{1,0:T(8,128)(2,1)S(1)}, f16[1024,128]{1,0:T(8,128)(2,1)S(1)}, u32[]{:S(2)}, u32[]{:S(2)}) collective-permute-start(f16[1024,128]{1,0:T(8,128)(2,1)S(1)} %get-tuple-element.12), channel_id=1, source_target_pairs={{0,3},{1,0},{2,1},{3,2},{4,7},{5,4},{6,5},{7,6},{8,11},{9,8},{10,9... | collective-permute-start | bytes 786440 | tf_op jit(solution)/shard_map/ppermute | solution.py:263
  99.1 12.0 %collective-permute-start.32 = (f16[2048,128]{1,0:T(8,128)(2,1)S(1)}, f16[2048,128]{1,0:T(8,128)(2,1)S(1)}, u32[]{:S(2)}, u32[]{:S(2)}) collective-permute-start(f16[2048,128]{1,0:T(8,128)(2,1)S(1)} %pad_maximum_fusion), channel_id=1, source_target_pairs={{0,4},{4,64},{8,12},{12,72},{16,20},{20,80},{24,28},{28,88},{32,36... | collective-permute-start | bytes 1572872 | tf_op jit(solution)/shard_map/ppermute | solution.py:263
  102.4 9.0 %collective-permute-start.33 = (f32[128]{0:T(128)S(1)}, f32[128]{0:T(128)S(1)}, u32[]{:S(2)}, u32[]{:S(2)}) collective-permute-start(f32[128]{0:T(128)S(1)} %multiply_reduce_fusion), channel_id=1, source_target_pairs={{0,68},{4,0},{8,76},{12,8},{16,84},{20,16},{24,92},{28,24},{32,100... | collective-permute-start | bytes 1544 | tf_op jit(solution)/shard_map/ppermute | solution.py:263
  103.0 8.4 %collective-permute-start.34 = (f32[128]{0:T(128)S(1)}, f32[128]{0:T(128)S(1)}, u32[]{:S(2)}, u32[]{:S(2)}) collective-permute-start(f32[128]{0:T(128)S(1)} %multiply_reduce_fusion), channel_id=1, source_target_pairs={{0,132},{4,192},{8,140},{12,200},{16,148},{20,208},{24,156},{28,21... | collective-permute-start | bytes 1544 | tf_op jit(solution)/shard_map/ppermute | solution.py:263
  107.8 3.7 %collective-permute-start.35 = (f32[128]{0:T(128)S(1)}, f32[128]{0:T(128)S(1)}, u32[]{:S(2)}, u32[]{:S(2)}) collective-permute-start(f32[128]{0:T(128)S(1)} %multiply_reduce_fusion), channel_id=1, source_target_pairs={{0,196},{4,128},{8,204},{12,136},{16,212},{20,144},{24,220},{28,15... | collective-permute-start | bytes 1544 | tf_op jit(solution)/shard_map/ppermute | solution.py:263
